TPU v7x, 32 devices: a whole 2x2x4 slice. The times are simulated.
32 devices in a mesh: grp: 2 (over x), row: 16 (over z, y, core).
Axes of the slice: x: 2, y: 2, z: 4, core: 2. Of those that a mesh axis runs over, the one named last changes fastest.
Arguments:
- positions: float32 [3, 12288], P(None, ('grp', 'row')), parts along dimension 1, may hold values from -6 to 6
- noise: float32 [3, 12288], P(None, ('grp', 'row')), parts along dimension 1, may hold values from -6 to 6
- atom_single: bfloat16 [12288, 128], P(('grp', 'row')), parts along dimension 0, may hold values from -6 to 6
- atom_token: int32 [12288], P(('grp', 'row')), parts along dimension 0, may hold values from 0 to 511, as said below
- atom_counts: int32 [32], P(('grp', 'row')), parts along dimension 0, may hold values from 192 to 384, as said below
- window_offsets: int32 [384], P(('grp', 'row')), parts along dimension 0, may hold values from -64 to -32
- atom_bias: float32 [4, 12288, 128], P(None, ('grp', 'row')), parts along dimension 1, may hold values from -4 to 302
- token_single: bfloat16 [1024, 768], P(('grp', 'row')), parts along dimension 0, may hold values from -6 to 6
- token_bias: float32 [16, 1024, 512], P(None, ('grp', 'row')), parts along dimension 1, may hold values from -9 to 302
- pair_mask: int32 [1024, 512], P(('grp', 'row')), parts along dimension 0, may hold values from 0 to 1, as said below
- w_coord: float32 [3, 128], replicated, may hold values from -3.5 to 3.5
- w_atom_qkv: bfloat16 [128, 384], replicated, may hold values from -0.5 to 0.5
- w_atom_out: bfloat16 [128, 128], replicated, may hold values from -0.5 to 0.5
- w_agg: bfloat16 [128, 768], replicated, may hold values from -0.5 to 0.5
- w_tok_qkv: bfloat16 [768, 2304], replicated, may hold values from -0.21875 to 0.21875
- w_tok_gate: bfloat16 [768, 768], replicated, may hold values from -0.21875 to 0.21875
- w_tok_out: bfloat16 [768, 768], replicated, may hold values from -0.21875 to 0.21875
- w_back: bfloat16 [768, 128], replicated, may hold values from -0.21875 to 0.21875
- w_pos: bfloat16 [3, 128], replicated, may hold values from -0.5 to 0.5
Outputs:
- denoised: float32 [3, 12288], P(None, ('grp', 'row')), parts along dimension 1
- token_out: bfloat16 [1024, 768], P(('grp', 'row')), parts along dimension 0
There are 2 independent parts, one for each index of `grp`. A program takes and returns all parts, laid end to end along the dimension named above; an argument that names none is the same for every part. Nothing has to cross between parts.
Inputs may be any that keep to these rules, and one draw needn't show every extreme that they name: `atom_token`: slots i * 384 to (i + 1) * 384 - 1 name tokens from i * 32 - 32 // 4 to (i + 1) * 32 + 32 // 4; ids never fall along the slots. `atom_counts`: entry i is the number of live slots at the front of slots i * 384 onward; some entry equals 384. `pair_mask`: each token's own column, and the column of its index xor 1, are 1.
All inputs are finite; a program needn't handle non-finite values.
Results may differ from a plain program's by a relative error of at most 0.0075.
Values may be sent and summed in bfloat16 or wider, within the bound.
No kernel may reach another device: no remote copies, remote signals or barrier semaphores. Data moves between devices by JAX's collectives and lax.ppermute only.
A program may use at most 64 MiB of HBM per device.

v0:
```python
import jax
import jax.numpy as jnp
from jax import lax
from jax.sharding import PartitionSpec as P

AH = 4
TH = 16
QWIN = 32
KWIN = 128


noise_level = 2.0
input_scale = 1.0 / 5.0**0.5
skip_scale = 1.0 / 5.0
output_scale = 2.0 / 5.0**0.5
masked_score = -1e30


def from_behind(value, axis, steps):
    count = lax.axis_size(axis)
    first, last = (max(0, -steps), min(count, count - steps))
    return lax.ppermute(value, axis, [(source, source + steps) for source in range(first, last)])


def extended_2(array, sides, width):
    for axis, dim in sides:
        count, length = (lax.axis_size(axis), array.shape[dim])
        up = [(i, (i + 1) % count) for i in range(count - 1)]
        down = [(j, i) for i, j in up]
        last = lax.slice_in_dim(array, length - width, length, axis=dim)
        first = lax.slice_in_dim(array, 0, width, axis=dim)
        before = lax.ppermute(last, axis, up)
        after = lax.ppermute(first, axis, down)
        array = jnp.concatenate([before, array, after], axis=dim)
    return array


def normalize(values):
    values = values.astype(jnp.float32)
    center = values - jnp.mean(values, axis=-1, keepdims=True)
    spread = jnp.mean(center * center, axis=-1, keepdims=True)
    return center * lax.rsqrt(spread + 1e-05)


def on_device(
    positions,
    noise,
    atom_single,
    atom_token,
    atom_counts,
    window_offsets,
    atom_bias,
    token_single,
    token_bias,
    pair_mask,
    w_coord,
    w_atom_qkv,
    w_atom_out,
    w_agg,
    w_tok_qkv,
    w_tok_gate,
    w_tok_out,
    w_back,
    w_pos,
):
    position = lax.axis_index("row")
    last_device = lax.axis_size("row") - 1
    capacity = atom_single.shape[0]
    atom_width = atom_single.shape[1]
    block_rows = token_single.shape[0]
    model_width = token_single.shape[1]
    live_count = atom_counts[0]
    slot_ids = jnp.arange(capacity, dtype=jnp.int32)
    living = slot_ids < live_count
    noisy_coords = positions + noise_level * noise
    atom_start = atom_single.astype(jnp.float32) + lax.dot_general(
        input_scale * noisy_coords,
        w_coord,
        (((0,), (0,)), ((), ())),
        precision=lax.Precision.HIGHEST,
        preferred_element_type=jnp.float32,
    )
    normed = normalize(atom_start).astype(jnp.bfloat16)
    projected = jnp.dot(normed, w_atom_qkv, preferred_element_type=jnp.float32).astype(jnp.bfloat16)
    queries = projected[:, :atom_width]
    key_vals = projected[:, atom_width:]
    behind = KWIN // 2
    ahead_rows = KWIN - QWIN
    tail_rows = lax.dynamic_slice_in_dim(key_vals, live_count - behind, behind, 0)
    lower_rim = from_behind(tail_rows, "row", 1)
    upper_rim = from_behind(key_vals[:ahead_rows], "row", -1)
    extended = jnp.concatenate(
        [lower_rim, key_vals, jnp.zeros((ahead_rows, 2 * atom_width), jnp.bfloat16)], axis=0
    )
    extended = lax.dynamic_update_slice_in_dim(extended, upper_rim, behind + live_count, 0)
    key_slots = jnp.arange(behind + capacity + ahead_rows, dtype=jnp.int32)
    usable = (
        (key_slots < behind) & (position > 0)
        | (key_slots >= behind) & (key_slots < behind + live_count)
        | (key_slots >= behind + live_count)
        & (key_slots < behind + live_count + ahead_rows)
        & (position < last_device)
    )
    per_window = capacity // QWIN
    window_base = behind + QWIN * jnp.arange(per_window, dtype=jnp.int32) + window_offsets
    window_slots = window_base[:, None] + jnp.arange(KWIN, dtype=jnp.int32)[None, :]
    window_kv = jnp.take(extended, window_slots, axis=0)
    key_usable = usable[window_slots]
    head_width = atom_width // AH
    query_heads = queries.reshape(per_window, QWIN, AH, head_width)
    key_heads = window_kv[..., :atom_width].reshape(per_window, KWIN, AH, head_width)
    value_heads = window_kv[..., atom_width:].reshape(per_window, KWIN, AH, head_width)
    scores = jnp.einsum(
        "wqhd,wkhd->hwqk", query_heads, key_heads, preferred_element_type=jnp.float32
    ) / head_width**0.5 + atom_bias.reshape(AH, per_window, QWIN, KWIN)
    scores = jnp.where(key_usable[None, :, None, :], scores, masked_score)
    weights = jax.nn.softmax(scores, axis=-1).astype(jnp.bfloat16)
    attended = jnp.einsum(
        "hwqk,wkhd->wqhd", weights, value_heads, preferred_element_type=jnp.float32
    ).reshape(capacity, atom_width)
    atom_mid = atom_start + jnp.dot(
        attended.astype(jnp.bfloat16), w_atom_out, preferred_element_type=jnp.float32
    )
    spread_rows = jnp.maximum(
        jnp.dot(atom_mid.astype(jnp.bfloat16), w_agg, preferred_element_type=jnp.float32), 0.0
    ).astype(jnp.bfloat16)
    live_rows = jnp.where(living[:, None], spread_rows, jnp.zeros_like(spread_rows))
    live_ones = living.astype(jnp.bfloat16)
    relative = atom_token - (position - 1) * block_rows
    local_hot = (relative[None, :] == jnp.arange(3 * block_rows, dtype=jnp.int32)[:, None]).astype(
        jnp.bfloat16
    )
    partial_value = jnp.dot(local_hot, live_rows, preferred_element_type=jnp.float32)
    counted = jnp.dot(local_hot, live_ones, preferred_element_type=jnp.float32)
    from_upper = (
        from_behind(partial_value[:block_rows].astype(jnp.bfloat16), "row", -1).astype(jnp.float32),
        from_behind(counted[:block_rows].astype(jnp.bfloat16), "row", -1).astype(jnp.float32),
    )
    from_lower = (
        from_behind(partial_value[2 * block_rows :].astype(jnp.bfloat16), "row", 1).astype(
            jnp.float32
        ),
        from_behind(counted[2 * block_rows :].astype(jnp.bfloat16), "row", 1).astype(jnp.float32),
    )
    token_sum = partial_value[block_rows : 2 * block_rows] + from_upper[0] + from_lower[0]
    token_count = counted[block_rows : 2 * block_rows] + from_upper[1] + from_lower[1]
    token_in = token_single.astype(jnp.float32) + token_sum / jnp.maximum(token_count, 1.0)[:, None]
    token_norm = normalize(token_in).astype(jnp.bfloat16)
    token_query = jnp.dot(
        token_norm, w_tok_qkv[:, :model_width], preferred_element_type=jnp.float32
    ).astype(jnp.bfloat16)
    kv_weight = w_tok_qkv[:, model_width:]
    all_kv = jnp.dot(
        lax.all_gather(token_norm, "row", axis=0, tiled=True),
        kv_weight,
        preferred_element_type=jnp.float32,
    ).astype(jnp.bfloat16)
    key_count = all_kv.shape[0]
    token_head = model_width // TH
    head_query = token_query.reshape(block_rows, TH, token_head)
    head_key = all_kv[:, :model_width].reshape(key_count, TH, token_head)
    head_value = all_kv[:, model_width:].reshape(key_count, TH, token_head)
    token_scores = (
        jnp.einsum("qhd,khd->hqk", head_query, head_key, preferred_element_type=jnp.float32)
        / token_head**0.5
        + token_bias
    )
    token_scores = jnp.where(pair_mask[None] == 1, token_scores, masked_score)
    token_weights = jax.nn.softmax(token_scores, axis=-1).astype(jnp.bfloat16)
    token_att = jnp.einsum(
        "hqk,khd->qhd", token_weights, head_value, preferred_element_type=jnp.float32
    ).reshape(block_rows, model_width)
    gating = jax.nn.sigmoid(jnp.dot(token_norm, w_tok_gate, preferred_element_type=jnp.float32))
    gated = (gating * token_att).astype(jnp.bfloat16)
    token_out = (token_in + jnp.dot(gated, w_tok_out, preferred_element_type=jnp.float32)).astype(
        jnp.bfloat16
    )
    back_rows = jnp.dot(token_out, w_back, preferred_element_type=jnp.float32).astype(jnp.bfloat16)
    near_rows = extended_2(back_rows, (("row", 0),), block_rows)
    atom_last = atom_mid + lax.dot_general(
        local_hot, near_rows, (((0,), (0,)), ((), ())), preferred_element_type=jnp.float32
    )
    final_norm = normalize(atom_last).astype(jnp.bfloat16)
    update = lax.dot_general(
        w_pos, final_norm, (((1,), (1,)), ((), ())), preferred_element_type=jnp.float32
    )
    denoised = jnp.where(living[None, :], skip_scale * noisy_coords + output_scale * update, 0.0)
    return (denoised, token_out)


def solution(mesh):
    placed = (
        P(None, ("grp", "row")),
        P(None, ("grp", "row")),
        P(("grp", "row"), None),
        P(("grp", "row")),
        P(("grp", "row")),
        P(("grp", "row")),
        P(None, ("grp", "row"), None),
        P(("grp", "row"), None),
        P(None, ("grp", "row"), None),
        P(("grp", "row"), None),
        P(),
        P(),
        P(),
        P(),
        P(),
        P(),
        P(),
        P(),
        P(),
    )
    return jax.shard_map(
        on_device,
        mesh=mesh,
        in_specs=placed,
        out_specs=(P(None, ("grp", "row")), P(("grp", "row"), None)),
        check_vma=False,
    )
```

profile of v0, /device:TPU:1, one launch (start us, length us, event | category | flops | bytes accessed | tf_op | source)
XLA Modules:
  0.0 93.2 jit_solution(17594367340603574368)
XLA Ops:
  2.4 1.1 %fusion.80 = (f32[384]{0:T(512)S(1)}, f32[384,128]{0,1:T(8,128)S(1)}) fusion(f32[3,128]{1,0:T(4,128)} %param.29, f32[3,384]{1,0:T(4,128)} %param.19, f32[3,384]{1,0:T(4,128)} %param.20, bf16[384,128]{0,1:T(8,128)(2,1)S(1)} %copy.28), kind=kOutput, calls=%fused_computation.126 | convolution fusion | flops 1920000 | bytes 307200 | tf_op jit(solution)/shard_map/dot_general | solution.py:76
  3.6 1.2 %convolution_convert_fusion.2 = bf16[384,384]{1,0:T(8,128)(2,1)S(1)} fusion(bf16[128,384]{1,0:T(8,128)(2,1)} %param.30, f32[384,128]{0,1:T(8,128)S(1)} %get-tuple-element.13, f32[384]{0:T(512)S(1)} %add_rsqrt_fusion.1, f32[384]{0:T(512)S(1)} %broadcast_multiply_fusion.1), kind=kOutput, calls=%fused_computation.21 | convolution fusion | flops 38043648 | bytes 592896 | tf_op jit(solution)/shard_map/dot_general | solution.py:84
  4.8 4.5 %collective-permute-start = (bf16[64,256]{1,0:T(8,128)(2,1)S(1)}, bf16[64,256]{1,0:T(8,128)(2,1)S(1)}, u32[]{:S(2)}, u32[]{:S(2)}) collective-permute-start(bf16[64,256]{1,0:T(8,128)(2,1)S(1)} %constant_dynamic-slice_fusion), channel_id=1, source_target_pairs={{0,1},{1,2},{2,3},{3,4},{4,5},{5,6},{6,7},{7,8},{8,9},{9,10},{10,1... | collective-permute-start | bytes 98312 | tf_op jit(solution)/shard_map/ppermute | solution.py:22
  9.4 1.9 %collective-permute-start.1 = (bf16[96,256]{1,0:T(8,128)(2,1)S(1)}, bf16[96,256]{1,0:T(8,128)(2,1)S(1)}, u32[]{:S(2)}, u32[]{:S(2)}) collective-permute-start(bf16[96,256]{1,0:T(8,128)(2,1)S(1)} %slice.70), channel_id=1, source_target_pairs={{1,0},{2,1},{3,2},{4,3},{5,4},{6,5},{7,6},{8,7},{9,8},{10,9},{11,1... | collective-permute-start | bytes 147464 | tf_op jit(solution)/shard_map/ppermute | solution.py:22
  11.6 1.9 %collective-permute-start.4 = (bf16[32]{0:T(256)(128)(2,1)S(1)}, bf16[32]{0:T(256)(128)(2,1)S(1)}, u32[]{:S(2)}, u32[]{:S(2)}) collective-permute-start(bf16[32]{0:T(256)(128)(2,1)S(1)} %get-tuple-element.10), channel_id=1, source_target_pairs={{1,0},{2,1},{3,2},{4,3},{5,4},{6,5},{7,6},{8,7},{9,8},{10,9},{11,1... | collective-permute-start | bytes 200 | tf_op jit(solution)/shard_map/ppermute | solution.py:22
  13.5 3.6 %collective-permute-start.5 = (bf16[32]{0:T(256)(128)(2,1)S(1)}, bf16[32]{0:T(256)(128)(2,1)S(1)}, u32[]{:S(2)}, u32[]{:S(2)}) collective-permute-start(bf16[32]{0:T(256)(128)(2,1)S(1)} %get-tuple-element.11), channel_id=1, source_target_pairs={{0,1},{1,2},{2,3},{3,4},{4,5},{5,6},{6,7},{7,8},{8,9},{9,10},{10,1... | collective-permute-start | bytes 200 | tf_op jit(solution)/shard_map/ppermute | solution.py:22
  17.7 9.4 %gather_fusion.1 = pred[1536]{0:T(1024)(128)(4,1)S(1)} fusion(pred[544]{0:T(1024)(128)(4,1)S(1)} %fusion.62, s32[2048]{0:T(1024)S(1)} %pad_clamp_fusion), kind=kCustom, calls=%fused_computation.1 | custom fusion | bytes 9216 | tf_op jit(solution)/shard_map/gather | solution.py:108
  27.7 4.8 %gather_fusion = bf16[1536,256]{1,0:T(8,128)(2,1)S(1)} fusion(bf16[544,256]{1,0:T(8,128)(2,1)S(1)} %dynamic_update_slice.3, s32[2048]{0:T(1024)S(1)} %pad_clamp_fusion), kind=kCustom, calls=%fused_computation | custom fusion | bytes 1579008 | tf_op jit(solution)/shard_map/jit(_take)/gather | solution.py:107
  34.2 1.3 %fusion.81 = (f32[4,12,32]{2,1,0:T(8,128)S(1)}, f32[4,12,32,128]{3,2,1,0:T(8,128)}) fusion(f32[4,12,32,128]{3,2,1,0:T(8,128)S(1)} %bitcast.51, bf16[12,128,4,32]{1,3,2,0:T(8,128)(2,1)S(1)} %bitcast.49, bf16[12,32,4,32]{3,2,1,0:T(4,128)(2,1)S(1)} %reshape.140, pred[12,128]{1,0:T(8,128)(4,1)S(1)} %bitcast.53), kind=kOutput, calls=%fused_computation.127 | convolution fusion | flops 13566079 | bytes 2072064 | tf_op jit(solution)/shard_map/sub | solution.py:117
  35.5 1.7 %fusion.14 = bf16[12,32,4,32]{1,3,2,0:T(8,128)(2,1)S(1)} fusion(bf16[12,128,4,32]{1,3,2,0:T(8,128)(2,1)} %bitcast.52, f32[4,12,32,128]{3,2,1,0:T(8,128)} %get-tuple-element.15, f32[4,12,32]{2,1,0:T(8,128)S(1)} %get-tuple-element.14), kind=kOutput, calls=%fused_computation.22 | convolution fusion | flops 13025280 | bytes 1284096 | tf_op jit(solution)/shard_map/hwqk,wkhd->wqhd/dot_general | solution.py:118
  38.7 1.9 %collective-permute-start.2 = (bf16[32,768]{1,0:T(8,128)(2,1)S(1)}, bf16[32,768]{1,0:T(8,128)(2,1)S(1)}, u32[]{:S(2)}, u32[]{:S(2)}) collective-permute-start(bf16[32,768]{1,0:T(8,128)(2,1)S(1)} %get-tuple-element.8), channel_id=1, source_target_pairs={{1,0},{2,1},{3,2},{4,3},{5,4},{6,5},{7,6},{8,7},{9,8},{10,9},{11,1... | collective-permute-start | bytes 147464 | tf_op jit(solution)/shard_map/ppermute | solution.py:22
  40.7 3.6 %collective-permute-start.3 = (bf16[32,768]{1,0:T(8,128)(2,1)S(1)}, bf16[32,768]{1,0:T(8,128)(2,1)S(1)}, u32[]{:S(2)}, u32[]{:S(2)}) collective-permute-start(bf16[32,768]{1,0:T(8,128)(2,1)S(1)} %get-tuple-element.9), channel_id=1, source_target_pairs={{0,1},{1,2},{2,3},{3,4},{4,5},{5,6},{6,7},{7,8},{8,9},{9,10},{10,1... | collective-permute-start | bytes 147464 | tf_op jit(solution)/shard_map/ppermute | solution.py:22
  44.4 1.4 %collective-permute-done.3 = bf16[32,768]{1,0:T(8,128)(2,1)S(1)} collective-permute-done((bf16[32,768]{1,0:T(8,128)(2,1)S(1)}, bf16[32,768]{1,0:T(8,128)(2,1)S(1)}, u32[]{:S(2)}, u32[]{:S(2)}) %collective-permute-start.3) | collective-permute-done | bytes 49184 | tf_op jit(solution)/shard_map/ppermute | solution.py:22
  46.4 24.6 %all_gather.3 = bf16[512,768]{1,0:T(8,128)(2,1)S(1)} all-gather(bf16[32,768]{1,0:T(8,128)(2,1)S(1)} %multiply_convert_fusion.4), channel_id=1, replica_groups=mesh['grp'=2,'row'=16] {'row'}, dimensions={0}, use_global_device_ids=true | all-gather | bytes 835584 | tf_op jit(solution)/shard_map/all_gather | solution.py:154
  71.0 1.6 %fusion.23 = bf16[32,768]{1,0:T(8,128)(2,1)S(1)} fusion(bf16[32,768]{1,0:T(8,128)(2,1)S(1)} %multiply_convert_fusion.4, bf16[768,2304]{1,0:T(8,128)(2,1)} %param.33), kind=kOutput, calls=%fused_computation.37 | convolution fusion | flops 37773312 | bytes 1277952 | tf_op jit(solution)/shard_map/dot_general | solution.py:149
  72.6 3.1 %convolution_convert_fusion = bf16[512,1536]{1,0:T(8,128)(2,1)S(1)} fusion(bf16[512,768]{1,0:T(8,128)(2,1)S(1)} %all_gather.3, bf16[768,2304]{1,0:T(8,128)(2,1)} %param.33), kind=kOutput, calls=%fused_computation.4 | convolution fusion | flops 1208745984 | bytes 4718592 | tf_op jit(solution)/shard_map/dot_general | solution.py:153
  75.7 1.2 %copy.35 = bf16[512,768]{0,1:T(8,128)(2,1)} copy(bf16[512,768]{1,0:T(8,128)(2,1)S(1)} %get-tuple-element.4) | data formatting | bytes 1572864 | tf_op jit(solution)/shard_map/slice | solution.py:161
  77.1 1.8 %fusion.7 = f32[16,32,512]{2,1,0:T(8,128)S(1)} fusion(f32[16,32,512]{2,1,0:T(8,128)} %param.27, bf16[512,16,48]{0,2,1:T(8,128)(2,1)} %bitcast.47, pred[32,512]{1,0:T(8,128)(4,1)S(1)} %broadcast_compare_fusion, bf16[32,16,48]{2,1,0:T(8,128)(2,1)S(1)} %reshape.144), kind=kOutput, calls=%fused_computation.12 | convolution fusion | flops 25952256 | bytes 2949120 | tf_op jit(solution)/shard_map/qhd,khd->hqk/dot_general | solution.py:164
  79.1 1.2 %copy.34 = bf16[512,768]{0,1:T(8,128)(2,1)} copy(bf16[512,768]{1,0:T(8,128)(2,1)S(1)} %get-tuple-element.5) | data formatting | bytes 1572864 | tf_op jit(solution)/shard_map/slice | solution.py:162
  80.3 2.1 %convolution_bitcast_fusion = f32[32,16,48]{2,0,1:T(8,128)S(1)} fusion(bf16[512,16,48]{0,2,1:T(8,128)(2,1)} %bitcast.50, f32[16,32]{1,0:T(8,128)S(1)} %fusion.86, f32[16,32,512]{2,1,0:T(8,128)S(1)} %fusion.7), kind=kOutput, calls=%fused_computation.25 | convolution fusion | flops 25953280 | bytes 1935360 | tf_op jit(solution)/shard_map/hqk,khd->qhd/dot_general | solution.py:170
  82.8 2.0 %fusion.21 = bf16[32,768]{1,0:T(8,128)(2,1)S(1)} fusion(f32[32,768]{1,0:T(8,128)S(1)} %get-tuple-element.3, bf16[768,768]{1,0:T(8,128)(2,1)S(1)} %copy-done, f32[32,768]{1,0:T(8,128)S(1)} %reshape.146, bf16[32,768]{1,0:T(8,128)(2,1)S(1)} %multiply_convert_fusion.4, bf16[768,768]{1,0:T(8,128)(2,1)} %param.34), kind=kOutput, calls=%fused_computation.35 | convolution fusion | flops 75669504 | bytes 2654208 | tf_op jit(solution)/shard_map/dot_general | solution.py:175
  84.9 2.3 %collective-permute-start.6 = (bf16[32,128]{1,0:T(8,128)(2,1)S(1)}, bf16[32,128]{1,0:T(8,128)(2,1)S(1)}, u32[]{:S(2)}, u32[]{:S(2)}) collective-permute-start(bf16[32,128]{1,0:T(8,128)(2,1)S(1)} %convolution_convert_fusion.3), channel_id=1, source_target_pairs={{0,1},{1,2},{2,3},{3,4},{4,5},{5,6},{6,7},{7,8},{8,9},{9,10},{10,1... | collective-permute-start | bytes 24584 | tf_op jit(solution)/shard_map/ppermute | solution.py:32
  87.2 2.0 %collective-permute-start.7 = (bf16[32,128]{1,0:T(8,128)(2,1)S(1)}, bf16[32,128]{1,0:T(8,128)(2,1)S(1)}, u32[]{:S(2)}, u32[]{:S(2)}) collective-permute-start(bf16[32,128]{1,0:T(8,128)(2,1)S(1)} %convolution_convert_fusion.3), channel_id=1, source_target_pairs={{1,0},{2,1},{3,2},{4,3},{5,4},{6,5},{7,6},{8,7},{9,8},{10,9},{11,1... | collective-permute-start | bytes 24584 | tf_op jit(solution)/shard_map/ppermute | solution.py:33
  89.2 2.9 %collective-permute-done.7 = bf16[32,128]{1,0:T(8,128)(2,1)S(1)} collective-permute-done((bf16[32,128]{1,0:T(8,128)(2,1)S(1)}, bf16[32,128]{1,0:T(8,128)(2,1)S(1)}, u32[]{:S(2)}, u32[]{:S(2)}) %collective-permute-start.7) | collective-permute-done | bytes 8224 | tf_op jit(solution)/shard_map/ppermute | solution.py:33
  (81 shorter events, 8.2 us)
Async XLA Ops:
  0.6 82.1 %copy-start = (bf16[768,768]{1,0:T(8,128)(2,1)S(1)}, bf16[768,768]{1,0:T(8,128)(2,1)}, u32[]{:S(2)}) copy-start(bf16[768,768]{1,0:T(8,128)(2,1)} %param.35) | copy-start | bytes 3538948
  0.6 10.7 %copy-start.9 = (s32[384]{0:T(512)S(1)}, s32[384]{0:T(512)}, u32[]{:S(2)}) copy-start(s32[384]{0:T(512)} %param.22) | copy-start | bytes 4612
  0.7 16.5 %copy-start.12 = (s32[12]{0:T(128)S(1)}, s32[12]{0:T(128)}, u32[]{:S(2)}) copy-start(s32[12]{0:T(128)} %param.24) | copy-start | bytes 148
  0.7 16.7 %copy-start.4 = (s32[32,512]{1,0:T(8,128)S(1)}, s32[32,512]{1,0:T(8,128)}, u32[]{:S(2)}) copy-start(s32[32,512]{1,0:T(8,128)} %param.28) | copy-start | bytes 196612
  4.8 22.3 %collective-permute-start = (bf16[64,256]{1,0:T(8,128)(2,1)S(1)}, bf16[64,256]{1,0:T(8,128)(2,1)S(1)}, u32[]{:S(2)}, u32[]{:S(2)}) collective-permute-start(bf16[64,256]{1,0:T(8,128)(2,1)S(1)} %constant_dynamic-slice_fusion), channel_id=1, source_target_pairs={{0,1},{1,2},{2,3},{3,4},{4,5},{5,6},{6,7},{7,8},{8,9},{9,10},{10,1... | collective-permute-start | bytes 98312 | tf_op jit(solution)/shard_map/ppermute | solution.py:22
  9.4 17.9 %collective-permute-start.1 = (bf16[96,256]{1,0:T(8,128)(2,1)S(1)}, bf16[96,256]{1,0:T(8,128)(2,1)S(1)}, u32[]{:S(2)}, u32[]{:S(2)}) collective-permute-start(bf16[96,256]{1,0:T(8,128)(2,1)S(1)} %slice.70), channel_id=1, source_target_pairs={{1,0},{2,1},{3,2},{4,3},{5,4},{6,5},{7,6},{8,7},{9,8},{10,9},{11,1... | collective-permute-start | bytes 147464 | tf_op jit(solution)/shard_map/ppermute | solution.py:22
  11.6 32.7 %collective-permute-start.4 = (bf16[32]{0:T(256)(128)(2,1)S(1)}, bf16[32]{0:T(256)(128)(2,1)S(1)}, u32[]{:S(2)}, u32[]{:S(2)}) collective-permute-start(bf16[32]{0:T(256)(128)(2,1)S(1)} %get-tuple-element.10), channel_id=1, source_target_pairs={{1,0},{2,1},{3,2},{4,3},{5,4},{6,5},{7,6},{8,7},{9,8},{10,9},{11,1... | collective-permute-start | bytes 200 | tf_op jit(solution)/shard_map/ppermute | solution.py:22
  13.5 30.8 %collective-permute-start.5 = (bf16[32]{0:T(256)(128)(2,1)S(1)}, bf16[32]{0:T(256)(128)(2,1)S(1)}, u32[]{:S(2)}, u32[]{:S(2)}) collective-permute-start(bf16[32]{0:T(256)(128)(2,1)S(1)} %get-tuple-element.11), channel_id=1, source_target_pairs={{0,1},{1,2},{2,3},{3,4},{4,5},{5,6},{6,7},{7,8},{8,9},{9,10},{10,1... | collective-permute-start | bytes 200 | tf_op jit(solution)/shard_map/ppermute | solution.py:22
  32.9 1.3 %copy-start.1 = (f32[4,384,128]{2,1,0:T(8,128)S(1)}, f32[4,384,128]{2,1,0:T(8,128)}, u32[]{:S(2)}) copy-start(f32[4,384,128]{2,1,0:T(8,128)} %param.25) | copy-start | bytes 2359300
  37.2 0.8 copy-start.6
  37.2 1.0 %copy-start.11 = (bf16[128,768]{1,0:T(8,128)(2,1)S(1)}, bf16[128,768]{1,0:T(8,128)(2,1)}, u32[]{:S(2)}) copy-start(bf16[128,768]{1,0:T(8,128)(2,1)} %param.32) | copy-start | bytes 589828
  37.5 8.4 %copy-start.5 = (bf16[32,768]{1,0:T(8,128)(2,1)S(1)}, bf16[32,768]{1,0:T(8,128)(2,1)}, u32[]{:S(2)}) copy-start(bf16[32,768]{1,0:T(8,128)(2,1)} %param.26) | copy-start | bytes 147460
  38.7 5.7 %collective-permute-start.2 = (bf16[32,768]{1,0:T(8,128)(2,1)S(1)}, bf16[32,768]{1,0:T(8,128)(2,1)S(1)}, u32[]{:S(2)}, u32[]{:S(2)}) collective-permute-start(bf16[32,768]{1,0:T(8,128)(2,1)S(1)} %get-tuple-element.8), channel_id=1, source_target_pairs={{1,0},{2,1},{3,2},{4,3},{5,4},{6,5},{7,6},{8,7},{9,8},{10,9},{11,1... | collective-permute-start | bytes 147464 | tf_op jit(solution)/shard_map/ppermute | solution.py:22
  40.7 5.2 %collective-permute-start.3 = (bf16[32,768]{1,0:T(8,128)(2,1)S(1)}, bf16[32,768]{1,0:T(8,128)(2,1)S(1)}, u32[]{:S(2)}, u32[]{:S(2)}) collective-permute-start(bf16[32,768]{1,0:T(8,128)(2,1)S(1)} %get-tuple-element.9), channel_id=1, source_target_pairs={{0,1},{1,2},{2,3},{3,4},{4,5},{5,6},{6,7},{7,8},{8,9},{9,10},{10,1... | collective-permute-start | bytes 147464 | tf_op jit(solution)/shard_map/ppermute | solution.py:22
  82.7 2.0 %copy-start.2 = (bf16[768,128]{1,0:T(8,128)(2,1)S(1)}, bf16[768,128]{1,0:T(8,128)(2,1)}, u32[]{:S(2)}) copy-start(bf16[768,128]{1,0:T(8,128)(2,1)} %param.36) | copy-start | bytes 589828
  82.7 9.7 %copy-start.7 = (f32[3,384]{1,0:T(4,128)S(1)}, f32[3,384]{1,0:T(4,128)}, u32[]{:S(2)}) copy-start(f32[3,384]{1,0:T(4,128)} %param.19) | copy-start | bytes 13828
  82.7 9.7 %copy-start.8 = (f32[3,384]{1,0:T(4,128)S(1)}, f32[3,384]{1,0:T(4,128)}, u32[]{:S(2)}) copy-start(f32[3,384]{1,0:T(4,128)} %param.20) | copy-start | bytes 13828
  82.7 9.7 %copy-start.10 = (bf16[3,128]{1,0:T(4,128)(2,1)S(1)}, bf16[3,128]{1,0:T(4,128)(2,1)}, u32[]{:S(2)}) copy-start(bf16[3,128]{1,0:T(4,128)(2,1)} %param.37) | copy-start | bytes 2308
  84.7 8.5 %copy-start.3 = (bf16[32,768]{1,0:T(8,128)(2,1)}, bf16[32,768]{1,0:T(8,128)(2,1)S(1)}, u32[]{:S(2)}) copy-start(bf16[32,768]{1,0:T(8,128)(2,1)S(1)} %fusion.21) | copy-start | bytes 147460
  84.9 4.3 %collective-permute-start.6 = (bf16[32,128]{1,0:T(8,128)(2,1)S(1)}, bf16[32,128]{1,0:T(8,128)(2,1)S(1)}, u32[]{:S(2)}, u32[]{:S(2)}) collective-permute-start(bf16[32,128]{1,0:T(8,128)(2,1)S(1)} %convolution_convert_fusion.3), channel_id=1, source_target_pairs={{0,1},{1,2},{2,3},{3,4},{4,5},{5,6},{6,7},{7,8},{8,9},{9,10},{10,1... | collective-permute-start | bytes 24584 | tf_op jit(solution)/shard_map/ppermute | solution.py:32
  87.2 5.0 %collective-permute-start.7 = (bf16[32,128]{1,0:T(8,128)(2,1)S(1)}, bf16[32,128]{1,0:T(8,128)(2,1)S(1)}, u32[]{:S(2)}, u32[]{:S(2)}) collective-permute-start(bf16[32,128]{1,0:T(8,128)(2,1)S(1)} %convolution_convert_fusion.3), channel_id=1, source_target_pairs={{1,0},{2,1},{3,2},{4,3},{5,4},{6,5},{7,6},{8,7},{9,8},{10,9},{11,1... | collective-permute-start | bytes 24584 | tf_op jit(solution)/shard_map/ppermute | solution.py:33
where the time goes:
time: 93.8 us; the launch traced here: 93.2 us
  blocking collectives  24.6 us (26%)
  starting transfers between devices  21.9 us (23%)
  local copies, waits for them, and re-layouts  21.3 us (23%)
  matrix products  17.7 us (19%)
  waiting for transfers between devices  4.37 us (5%)
  between operations  1.97 us (2%)
  other arithmetic  1.38 us (1%)
    all_gather x1, blocking collectives, on_device(): lax.all_gather(token_norm, 'row', axis=0, tiled=True)  24.6 us
    ppermute x6, starting transfers between devices, from_behind(): lax.ppermute(value, axis, [(source, source + steps) for source in range(f...  17.6 us
    gather x1, local copies, waits for them, and re-layouts, on_device(): key_usable = usable[window_slots]  9.45 us
    gather x2, local copies, waits for them, and re-layouts, on_device(): window_kv = jnp.take(extended, window_slots, axis=0)  5.13 us
    dot_general x1, matrix products, on_device(): jnp.dot(lax.all_gather(token_norm, 'row', axis=0, tiled=True), kv_weight,...  3.06 us
    ppermute x1, waiting for transfers between devices, extended_2(): after = lax.ppermute(first, axis, down)  2.91 us
    ppermute x1, starting transfers between devices, extended_2(): before = lax.ppermute(last, axis, up)  2.29 us
    dot_general x1, matrix products, on_device(): jnp.einsum('hqk,khd->qhd', token_weights, head_value, preferred_element_t...  2.09 us
  transfers between devices with their start and end apart: 8, of which 2 were waited for; matrix products, arithmetic and copies ran while one was open for 22% of the time, Pallas kernels for 0%

commit v1 on v0

v1 whole, which is shorter than its diff:
```python
import functools

import jax
import jax.numpy as jnp
from jax import lax
from jax.experimental import pallas as pl
from jax.experimental.pallas import tpu as pltpu
from jax.sharding import PartitionSpec as P

AH = 4
TH = 16
QWIN = 32
KWIN = 128
BEHIND = KWIN // 2
AHEAD = KWIN - QWIN

noise_level = 2.0
input_scale = 1.0 / 5.0**0.5
skip_scale = 1.0 / 5.0
output_scale = 2.0 / 5.0**0.5
masked_score = -1e30

F32 = jnp.float32
BF16 = jnp.bfloat16
NT = (((1,), (1,)), ((), ()))


def dot(a, b):
    return jnp.dot(a, b, preferred_element_type=F32)


def dot_nt(a, b):
    return lax.dot_general(a, b, NT, preferred_element_type=F32)


def normalize(values):
    center = values - jnp.mean(values, axis=-1, keepdims=True)
    spread = jnp.mean(center * center, axis=-1, keepdims=True)
    return center * lax.rsqrt(spread + 1e-05)


def iota(shape, dim):
    return lax.broadcasted_iota(jnp.int32, shape, dim)


VMEM = pl.BlockSpec(memory_space=pltpu.VMEM)
SMEM = pl.BlockSpec(memory_space=pltpu.SMEM)


def call(body, outs, name, specs, scratch=(), flops=10**7, limit=None):
    moved = sum(o.size * o.dtype.itemsize for o in outs)
    return pl.pallas_call(
        body,
        out_shape=tuple(outs),
        in_specs=specs,
        out_specs=tuple([VMEM] * len(outs)),
        scratch_shapes=list(scratch),
        name=name,
        cost_estimate=pl.CostEstimate(flops=flops, bytes_accessed=moved, transcendentals=0),
        compiler_params=pltpu.CompilerParams(vmem_limit_bytes=limit),
    )


def shape(dims, dtype):
    return jax.ShapeDtypeStruct(dims, dtype)


def embed_body(info, pos_ref, noise_ref, single_ref, wc_ref, wqkv_ref, start_ref, q_ref, k_ref, v_ref, pair_ref, odd_ref):
    rows, width = single_ref.shape
    scaled = input_scale * (pos_ref[...] + noise_level * noise_ref[...])
    padded = jnp.concatenate([scaled, jnp.zeros((5, rows), F32)], axis=0)
    across = jnp.transpose(padded)
    start = single_ref[...].astype(F32)
    for c in range(3):
        start = start + across[:, c : c + 1] * wc_ref[c : c + 1, :]
    start_ref[...] = start
    qkv = dot(normalize(start).astype(BF16), wqkv_ref[...]).astype(BF16)
    q_ref[...] = qkv[:, :width]
    tail = info[0] - BEHIND
    even = info[1] % 2 == 0
    for n, ref in enumerate((k_ref, v_ref)):
        at = slice(n * width, (n + 1) * width)
        ref[:rows, :] = qkv[:, (n + 1) * width : (n + 2) * width].astype(F32)
        ref[rows:, :] = jnp.zeros((AHEAD, width), F32)
        pair_ref[:, at] = ref[pl.ds(jnp.where(even, tail, 0), AHEAD), :].astype(BF16)
        odd_ref[:, at] = ref[pl.ds(jnp.where(even, 0, tail), AHEAD), :].astype(BF16)


def onehot(info, token_ref, half, block_rows):
    rows = token_ref.shape[1]
    relative = token_ref[...] - (info[1] * block_rows - half)
    living = iota((1, rows), 1) < info[0]
    hot = (iota((block_rows + 2 * half, rows), 0) == relative) & living
    return hot.astype(F32)


def atoms_body(
    half,
    info,
    offsets,
    token_ref,
    start_ref,
    q_ref,
    k_ref,
    v_ref,
    pair_ref,
    odd_ref,
    bias_ref,
    wout_ref,
    wagg_ref,
    mid_ref,
    own_ref,
    pair_out,
    odd_out,
    hot_ref,
    k_ext,
    v_ext,
    att,
):
    rows, width = start_ref.shape
    live, me, last = info[0], info[1], info[2]
    even = me % 2 == 0
    pair = pair_ref[...].astype(F32)
    odd = odd_ref[...].astype(F32)
    for n, (ref, ext) in enumerate(((k_ref, k_ext), (v_ref, v_ext))):
        at = slice(n * width, (n + 1) * width)
        ext[:BEHIND, :] = jnp.where(even, odd[:BEHIND, at], pair[:BEHIND, at])
        ext[BEHIND : BEHIND + rows + AHEAD, :] = ref[...]
        ext[pl.ds(BEHIND + live, AHEAD), :] = jnp.where(even, pair[:, at], odd[:, at])
    low = jnp.where(me > 0, 0, BEHIND)
    high = BEHIND + live + jnp.where(me < last, AHEAD, 0)
    scale = 1.0 / (width // AH) ** 0.5
    head_of_row = iota((AH * QWIN, width), 0) // QWIN
    head_of_lane = iota((AH * QWIN, width), 1) // (width // AH)
    own_head = head_of_row == head_of_lane
    lane_head = iota((QWIN, width), 1) // (width // AH)
    for m in range(rows // QWIN):
        base = BEHIND + QWIN * m + offsets[m]
        keys = k_ext[pl.ds(base, KWIN), :].astype(BF16)
        values = v_ext[pl.ds(base, KWIN), :].astype(BF16)
        window_q = q_ref[m * QWIN : (m + 1) * QWIN, :].astype(F32)
        stacked = jnp.where(own_head, jnp.concatenate([window_q] * AH, axis=0), 0.0).astype(BF16)
        bias = bias_ref[:, m * QWIN : (m + 1) * QWIN, :].reshape(AH * QWIN, KWIN)
        scores = dot_nt(stacked, keys) * scale + bias
        slots = base + iota((1, KWIN), 1)
        scores = jnp.where((slots >= low) & (slots < high), scores, masked_score)
        scores = jnp.exp(scores - jnp.max(scores, axis=-1, keepdims=True))
        weights = (scores / jnp.sum(scores, axis=-1, keepdims=True)).astype(BF16)
        mixed = dot(weights, values)
        out = mixed[:QWIN]
        for h in range(1, AH):
            out = jnp.where(lane_head == h, mixed[h * QWIN : (h + 1) * QWIN], out)
        att[m * QWIN : (m + 1) * QWIN, :] = out.astype(BF16)
    mid = start_ref[...] + dot(att[...], wout_ref[...])
    mid_ref[...] = mid
    spread = jnp.maximum(dot(mid.astype(BF16), wagg_ref[...]), 0.0).astype(BF16)
    block_rows = own_ref.shape[0]
    hot = onehot(info, token_ref, half, block_rows)
    hot_ref[...] = hot.astype(BF16)
    sums = dot(hot.astype(BF16), spread)
    counts = jnp.sum(hot, axis=1, keepdims=True)
    first = jnp.minimum(counts, 256.0)
    lane = iota((counts.shape[0], 128), 1)
    packed = jnp.where(lane == 0, first, jnp.where(lane == 1, counts - first, 0.0))
    model = wagg_ref.shape[1]
    own_ref[:, :model] = sums[half : half + block_rows]
    own_ref[:, model:] = packed[half : half + block_rows]
    lower = jnp.concatenate([sums[:half], packed[:half]], axis=1)
    upper = jnp.concatenate([sums[half + block_rows :], packed[half + block_rows :]], axis=1)
    pair_out[...] = jnp.where(even, upper, lower).astype(BF16)
    odd_out[...] = jnp.where(even, lower, upper).astype(BF16)


def token_body(info, own_ref, pair_ref, odd_ref, single_ref, in_ref, norm_ref):
    even = info[1] % 2 == 0
    model = single_ref.shape[1]
    pair = pair_ref[...].astype(F32)
    odd = odd_ref[...].astype(F32)
    both = own_ref[...] + jnp.concatenate([jnp.where(even, odd, pair), jnp.where(even, pair, odd)], axis=0)
    count = both[:, model : model + 1] + both[:, model + 1 : model + 2]
    token_in = single_ref[...].astype(F32) + both[:, :model] / jnp.maximum(count, 1.0)
    in_ref[...] = token_in
    norm_ref[...] = normalize(token_in).astype(BF16)


def query_body(norm_ref, wqkv_ref, wgate_ref, query_ref, gate_ref):
    rows, model = norm_ref.shape
    width = model // TH
    group = TH // 2
    span = group * width
    norm = norm_ref[...]
    tq = dot(norm, wqkv_ref[:, :model])
    own = iota((group * rows, span), 0) // rows == iota((group * rows, span), 1) // width
    for g in range(2):
        part = tq[:, g * span : (g + 1) * span]
        stacked = jnp.where(own, jnp.concatenate([part] * group, axis=0), 0.0).astype(BF16)
        wk = wqkv_ref[:, model + g * span : model + (g + 1) * span]
        query_ref[g * group * rows : (g + 1) * group * rows, :] = dot_nt(stacked, wk).astype(BF16)
    gate_ref[...] = jax.nn.sigmoid(dot(norm, wgate_ref[...]))


def attend_body(
    orders,
    half,
    info,
    in_ref,
    query_ref,
    gate_ref,
    all_ref,
    bias_ref,
    mask_ref,
    wqkv_ref,
    wout_ref,
    wback_ref,
    out_ref,
    back_ref,
    pair_out,
    odd_out,
    sorted_ref,
):
    rows, model = in_ref.shape
    keys = all_ref.shape[0]
    me = info[1]
    even = me % 2 == 0
    if orders is None:
        sorted_ref[...] = all_ref[...]
    else:
        for j in range(keys // rows):
            block = jnp.where(even, me ^ orders[0][j], me ^ orders[1][j])
            sorted_ref[pl.ds(pl.multiple_of(block * rows, rows), rows), :] = all_ref[j * rows : (j + 1) * rows, :]
    width = model // TH
    group = TH // 2
    span = group * width
    scale = 1.0 / width**0.5
    allowed = jnp.concatenate([mask_ref[...]] * group, axis=0) == 1
    values = sorted_ref[...]
    lane_head = iota((rows, span), 1) // width
    for g in range(2):
        at = slice(g * group * rows, (g + 1) * group * rows)
        bias = bias_ref[g * group : (g + 1) * group].reshape(group * rows, keys)
        scores = dot_nt(query_ref[at, :], values) * scale + bias
        scores = jnp.where(allowed, scores, masked_score)
        scores = jnp.exp(scores - jnp.max(scores, axis=-1, keepdims=True))
        weights = (scores / jnp.sum(scores, axis=-1, keepdims=True)).astype(BF16)
        mixed = dot(weights, values).astype(BF16)
        wide = dot(mixed, wqkv_ref[:, 2 * model + g * span : 2 * model + (g + 1) * span])
        part = wide[:rows]
        for h in range(1, group):
            part = jnp.where(lane_head == h, wide[h * rows : (h + 1) * rows], part)
        gated = (gate_ref[:, g * span : (g + 1) * span] * part).astype(BF16)
        added = dot(gated, wout_ref[g * span : (g + 1) * span, :])
        total = added if g == 0 else total + added
    token_out = (in_ref[...] + total).astype(BF16)
    out_ref[...] = token_out
    back = dot(token_out, wback_ref[...])
    back_ref[...] = back.astype(BF16)
    lower, upper = back[:half], back[rows - half :]
    pair_out[...] = jnp.where(even, upper, lower).astype(BF16)
    odd_out[...] = jnp.where(even, lower, upper).astype(BF16)


def final_body(info, hot_ref, mid_ref, back_ref, pair_ref, odd_ref, wpos_ref, pos_ref, noise_ref, out_ref):
    even = info[1] % 2 == 0
    pair = pair_ref[...].astype(F32)
    odd = odd_ref[...].astype(F32)
    near = jnp.concatenate(
        [jnp.where(even, odd, pair), back_ref[...].astype(F32), jnp.where(even, pair, odd)], axis=0
    ).astype(BF16)
    hot = jnp.transpose(hot_ref[...].astype(F32)).astype(BF16)
    last = mid_ref[...] + dot(hot, near)
    update = dot_nt(wpos_ref[...], normalize(last).astype(BF16))
    noisy = pos_ref[...] + noise_level * noise_ref[...]
    living = iota((1, noisy.shape[1]), 1) < info[0]
    out_ref[...] = jnp.where(living, skip_scale * noisy + output_scale * update, 0.0)


def exchange(pair, odd, count):
    pairs = [(i, i ^ 1) for i in range(count) if i ^ 1 < count]
    odds = [(i, i + 1) for i in range(1, count - 1, 2)]
    odds = odds + [(b, a) for a, b in odds]
    return lax.ppermute(pair, "row", pairs), lax.ppermute(odd, "row", odds)


def gather_plan(count):
    bits = [1 << b for b in range(count.bit_length() - 1)]
    if len(bits) < 2:
        return [[b, b] for b in bits[::-1]]
    even = bits[:0:-1]
    odd = even[:-2] + even[-2:][::-1] if len(even) > 1 else even
    return [[a, b] for a, b in zip(even, odd)] + [[1, 1]]


def gather(norm, count):
    if count & (count - 1) or count < 2:
        return lax.all_gather(norm, "row", axis=0, tiled=True), None
    orders = [[0], [0]]
    for step in gather_plan(count):
        perm = [(i, i ^ step[i % 2]) for i in range(count)]
        norm = jnp.concatenate([norm, lax.ppermute(norm, "row", perm)], axis=0)
        other = orders if step[0] != 1 else orders[::-1]
        orders = [orders[p] + [x ^ step[p] for x in other[p]] for p in range(2)]
    return norm, orders


def on_device(
    count,
    positions,
    noise,
    atom_single,
    atom_token,
    atom_counts,
    window_offsets,
    atom_bias,
    token_single,
    token_bias,
    pair_mask,
    w_coord,
    w_atom_qkv,
    w_atom_out,
    w_agg,
    w_tok_qkv,
    w_tok_gate,
    w_tok_out,
    w_back,
    w_pos,
):
    rows, width = atom_single.shape
    block_rows, model = token_single.shape
    half = block_rows // 2
    me = lax.axis_index("row").astype(jnp.int32)
    lane = jnp.arange(8, dtype=jnp.int32)
    info = jnp.where(lane == 0, atom_counts[0], jnp.where(lane == 1, me, count - 1))

    start, q, keys, values, pair, odd = call(
        embed_body,
        [
            shape((rows, width), F32),
            shape((rows, width), BF16),
            shape((rows + AHEAD, width), F32),
            shape((rows + AHEAD, width), F32),
            shape((AHEAD, 2 * width), BF16),
            shape((AHEAD, 2 * width), BF16),
        ],
        "embed",
        [SMEM] + [VMEM] * 5,
    )(info, positions, noise, atom_single, w_coord, w_atom_qkv)
    pair, odd = exchange(pair, odd, count)
    packed = model + 128
    mid, own, pair, odd, hot = call(
        functools.partial(atoms_body, half),
        [
            shape((rows, width), F32),
            shape((block_rows, packed), F32),
            shape((half, packed), BF16),
            shape((half, packed), BF16),
            shape((block_rows + 2 * half, rows), BF16),
        ],
        "atoms",
        [SMEM, SMEM] + [VMEM] * 10,
        [pltpu.VMEM((BEHIND + rows + AHEAD, width), F32)] * 2 + [pltpu.VMEM((rows, width), BF16)],
    )(info, window_offsets, atom_token[None], start, q, keys, values, pair, odd, atom_bias, w_atom_out, w_agg)
    pair, odd = exchange(pair, odd, count)
    token_in, norm = call(
        token_body,
        [shape((block_rows, model), F32), shape((block_rows, model), BF16)],
        "token",
        [SMEM] + [VMEM] * 4,
    )(info, own, pair, odd, token_single)
    everyone, orders = gather(norm, count)
    query, gate = call(
        query_body,
        [shape((TH * block_rows, model), BF16), shape((block_rows, model), F32)],
        "query",
        [VMEM] * 3,
    )(norm, w_tok_qkv, w_tok_gate)
    token_out, back, pair, odd = call(
        functools.partial(attend_body, orders, half),
        [
            shape((block_rows, model), BF16),
            shape((block_rows, width), BF16),
            shape((half, width), BF16),
            shape((half, width), BF16),
        ],
        "attend",
        [SMEM] + [VMEM] * 9,
        [pltpu.VMEM((count * block_rows, model), BF16)],
    )(info, token_in, query, gate, everyone, token_bias, pair_mask, w_tok_qkv, w_tok_out, w_back)
    pair, odd = exchange(pair, odd, count)
    (denoised,) = call(
        final_body,
        [shape(positions.shape, F32)],
        "final",
        [SMEM] + [VMEM] * 8,
    )(info, hot, mid, back, pair, odd, w_pos, positions, noise)
    return (denoised, token_out)


def solution(mesh):
    placed = (
        P(None, ("grp", "row")),
        P(None, ("grp", "row")),
        P(("grp", "row"), None),
        P(("grp", "row")),
        P(("grp", "row")),
        P(("grp", "row")),
        P(None, ("grp", "row"), None),
        P(("grp", "row"), None),
        P(None, ("grp", "row"), None),
        P(("grp", "row"), None),
    ) + (P(),) * 9
    return jax.shard_map(
        functools.partial(on_device, mesh.shape["row"]),
        mesh=mesh,
        in_specs=placed,
        out_specs=(P(None, ("grp", "row")), P(("grp", "row"), None)),
        check_vma=False,
    )
```

time: 93.8 us -> 67.2 us (0.72)
  the two profiles are of different devices: /device:TPU:1 before, /device:TPU:24 now
where the time goes in v1:
time: 67.2 us; the launch traced here: 66.8 us
  Pallas kernels  24.1 us (36%)
  waiting for transfers between devices  24 us (36%)
  starting transfers between devices  10.2 us (15%)
  local copies, waits for them, and re-layouts  4.03 us (6%)
  other arithmetic  3.03 us (5%)
  between operations  1.42 us (2%)
    ppermute x4, waiting for transfers between devices, gather(): norm = jnp.concatenate([norm, lax.ppermute(norm, 'row', perm)], axis=0)  15.5 us
    ppermute x6, starting transfers between devices, exchange(): return (lax.ppermute(pair, 'row', pairs), lax.ppermute(odd, 'row', odds))  9.61 us
    ppermute x6, waiting for transfers between devices, exchange(): return (lax.ppermute(pair, 'row', pairs), lax.ppermute(odd, 'row', odds))  8.57 us
    pallas_call x1, Pallas kernels, on_device(): call(functools.partial(atoms_body, half), [shape((rows, width), F32), sha...  6.76 us
    pallas_call x1, Pallas kernels, on_device(): call(functools.partial(attend_body, orders, half), [shape((block_rows, mo...  6.49 us
    pallas_call x1, Pallas kernels, on_device(): call(query_body, [shape((TH * block_rows, model), BF16), shape((block_row...  4.13 us
    unnamed x20, local copies, waits for them, and re-layouts  2.75 us
    pallas_call x1, Pallas kernels, on_device(): call(embed_body, [shape((rows, width), F32), shape((rows, width), BF16),...  2.74 us
  transfers between devices with their start and end apart: 10, of which 6 were waited for; matrix products, arithmetic and copies ran while one was open for 2% of the time, Pallas kernels for 6%

profile of v1, /device:TPU:24, one launch (start us, length us, event | category | flops | bytes accessed | tf_op | source)
XLA Modules:
  0.0 66.8 jit_solution(5600684408697375918)
XLA Ops:
  1.3 0.6 compare_select_fusion.1.info
  1.9 2.7 %embed.1 = (f32[384,128]{1,0:T(8,128)}, bf16[384,128]{1,0:T(8,128)(2,1)}, f32[480,128]{1,0:T(8,128)}, f32[480,128]{1,0:T(8,128)}, bf16[96,256]{1,0:T(8,128)(2,1)}, /*index=5*/bf16[96,256]{1,0:T(8,128)(2,1)}) custom-call(s32[8]{0:T(128)} %compare_select_fusion.1.info, f32[3,384]{1,0:T(4,128)} %pos_ref.3, f32[3,384]{1,0:T(4,128)} %noise_ref.3, ...), custom_call_target="tpu_custom_call" | custom-call | flops 10000000 | bytes 884736 | tf_op jit(solution)/shard_map/embed/pallas_call | solution.py:334
  4.6 3.4 %collective-permute-start.1 = (bf16[96,256]{1,0:T(8,128)(2,1)}, bf16[96,256]{1,0:T(8,128)(2,1)S(1)}, u32[]{:S(2)}, u32[]{:S(2)}) collective-permute-start(bf16[96,256]{1,0:T(8,128)(2,1)} %get-tuple-element.26), channel_id=1, source_target_pairs={{1,2},{3,4},{5,6},{7,8},{9,10},{11,12},{13,14},{2,1},{4,3},{6,5},{... | collective-permute-start | bytes 147464 | tf_op jit(solution)/shard_map/ppermute | solution.py:281
  8.0 1.2 %broadcast_in_dim.18.token_ref = s32[1,384]{1,0:T(1,128)} reshape(s32[384]{0:T(512)} %param.22) | data formatting | bytes 3072 | tf_op jit(solution)/shard_map/broadcast_in_dim | solution.py:361
  9.3 1.9 %collective-permute-done.1.odd_ref = bf16[96,256]{1,0:T(8,128)(2,1)S(1)} collective-permute-done((bf16[96,256]{1,0:T(8,128)(2,1)}, bf16[96,256]{1,0:T(8,128)(2,1)S(1)}, u32[]{:S(2)}, u32[]{:S(2)}) %collective-permute-start.1) | collective-permute-done | bytes 49184 | tf_op jit(solution)/shard_map/ppermute | solution.py:281
  11.2 0.6 copy-done.3
  11.8 6.8 %atoms.1 = (f32[384,128]{1,0:T(8,128)}, f32[32,896]{1,0:T(8,128)}, bf16[16,896]{1,0:T(8,128)(2,1)}, bf16[16,896]{1,0:T(8,128)(2,1)}, bf16[64,384]{1,0:T(8,128)(2,1)}) custom-call(s32[8]{0:T(128)} %compare_select_fusion.1.info, s32[12]{0:T(128)} %offsets.1, s32[1,384]{1,0:T(1,128)} %broadcast_in_dim.18.token_ref, f32[384,128]{1,0:T(8,128)} %get-tuple-element.21.start_ref, ...), custom_call_target="tpu_custom_call" | custom-call | flops 10000000 | bytes 417792 | tf_op jit(solution)/shard_map/atoms/pallas_call | solution.py:349
  18.6 3.3 %collective-permute-start.3 = (bf16[16,896]{1,0:T(8,128)(2,1)}, bf16[16,896]{1,0:T(8,128)(2,1)S(1)}, u32[]{:S(2)}, u32[]{:S(2)}) collective-permute-start(bf16[16,896]{1,0:T(8,128)(2,1)} %get-tuple-element.31), channel_id=1, source_target_pairs={{1,2},{3,4},{5,6},{7,8},{9,10},{11,12},{13,14},{2,1},{4,3},{6,5},{... | collective-permute-start | bytes 86024 | tf_op jit(solution)/shard_map/ppermute | solution.py:281
  21.9 3.0 %collective-permute-done.3.odd_ref = bf16[16,896]{1,0:T(8,128)(2,1)S(1)} collective-permute-done((bf16[16,896]{1,0:T(8,128)(2,1)}, bf16[16,896]{1,0:T(8,128)(2,1)S(1)}, u32[]{:S(2)}, u32[]{:S(2)}) %collective-permute-start.3) | collective-permute-done | bytes 28704 | tf_op jit(solution)/shard_map/ppermute | solution.py:281
  25.0 0.6 copy-done.5
  25.6 1.9 %token_.1 = (f32[32,768]{1,0:T(8,128)}, bf16[32,768]{1,0:T(8,128)(2,1)}) custom-call(s32[8]{0:T(128)} %compare_select_fusion.1.info, f32[32,896]{1,0:T(8,128)} %get-tuple-element.29.own_ref, bf16[16,896]{1,0:T(8,128)(2,1)} %copy-done.4, bf16[16,896]{1,0:T(8,128)(2,1)} %copy-done.5, bf16[32,768]{1,0:T(8,128)(2,1)} %single_ref.3), custom_call_target="tpu_custom_call" | custom-call | flops 10000000 | bytes 147456 | tf_op jit(solution)/shard_map/token/pallas_call | solution.py:363
  27.8 5.3 %collective-permute-done.4 = bf16[32,768]{1,0:T(8,128)(2,1)S(1)} collective-permute-done((bf16[32,768]{1,0:T(8,128)(2,1)}, bf16[32,768]{1,0:T(8,128)(2,1)S(1)}, u32[]{:S(2)}, u32[]{:S(2)}) %collective-permute-start.4) | collective-permute-done | bytes 49184 | tf_op jit(solution)/shard_map/ppermute | solution.py:299
  33.1 0.8 %pad_maximum_fusion.2 = bf16[64,768]{1,0:T(8,128)(2,1)S(1)} fusion(bf16[32,768]{1,0:T(8,128)(2,1)S(1)} %collective-permute-done.4, bf16[32,768]{1,0:T(8,128)(2,1)} %get-tuple-element.33.norm_ref), kind=kLoop, calls=%fused_computation.2 | loop fusion | flops 196608 | bytes 196608 | tf_op jit(solution)/shard_map/concatenate | solution.py:299
  34.0 4.5 %collective-permute-done.5 = bf16[64,768]{1,0:T(8,128)(2,1)S(1)} collective-permute-done((bf16[64,768]{1,0:T(8,128)(2,1)S(1)}, bf16[64,768]{1,0:T(8,128)(2,1)S(1)}, u32[]{:S(2)}, u32[]{:S(2)}) %collective-permute-start.5) | collective-permute-done | bytes 98336 | tf_op jit(solution)/shard_map/ppermute | solution.py:299
  38.5 0.8 %pad_maximum_fusion.1 = bf16[128,768]{1,0:T(8,128)(2,1)S(1)} fusion(bf16[64,768]{1,0:T(8,128)(2,1)S(1)} %collective-permute-done.5, bf16[32,768]{1,0:T(8,128)(2,1)S(1)} %collective-permute-done.4, bf16[32,768]{1,0:T(8,128)(2,1)} %get-tuple-element.33.norm_ref), kind=kLoop, calls=%fused_computation.1 | loop fusion | flops 589824 | bytes 393216 | tf_op jit(solution)/shard_map/concatenate | solution.py:299
  39.4 5.7 %collective-permute-done.6 = bf16[128,768]{1,0:T(8,128)(2,1)S(1)} collective-permute-done((bf16[128,768]{1,0:T(8,128)(2,1)S(1)}, bf16[128,768]{1,0:T(8,128)(2,1)S(1)}, u32[]{:S(2)}, u32[]{:S(2)}) %collective-permute-start.6) | collective-permute-done | bytes 196640 | tf_op jit(solution)/shard_map/ppermute | solution.py:299
  45.1 0.8 %pad_maximum_fusion = bf16[256,768]{1,0:T(8,128)(2,1)S(1)} fusion(bf16[128,768]{1,0:T(8,128)(2,1)S(1)} %collective-permute-done.6, bf16[64,768]{1,0:T(8,128)(2,1)S(1)} %collective-permute-done.5, bf16[32,768]{1,0:T(8,128)(2,1)S(1)} %collective-permute-done.4, bf16[32,768]{1,0:T(8,128)(2,1)} %get-tuple-element.33.norm_ref), kind=kLoop, calls=%fused_computation | loop fusion | flops 1572864 | bytes 786432 | tf_op jit(solution)/shard_map/concatenate | solution.py:299
  46.0 4.1 %query.1 = (bf16[512,768]{1,0:T(8,128)(2,1)}, f32[32,768]{1,0:T(8,128)}) custom-call(bf16[32,768]{1,0:T(8,128)(2,1)} %get-tuple-element.33.norm_ref, bf16[768,2304]{1,0:T(8,128)(2,1)} %wqkv_ref.5, bf16[768,768]{1,0:T(8,128)(2,1)} %wgate_ref.1), custom_call_target="tpu_custom_call" | custom-call | flops 10000000 | bytes 884736 | tf_op jit(solution)/shard_map/query/pallas_call | solution.py:370
  50.2 0.9 %copy-done.1 = bf16[512,768]{1,0:T(8,128)(2,1)} copy-done((bf16[512,768]{1,0:T(8,128)(2,1)}, bf16[512,768]{1,0:T(8,128)(2,1)S(1)}, u32[]{:S(2)}) %copy-start.1) | copy-done | bytes 786456
  51.1 6.5 %attend.1 = (bf16[32,768]{1,0:T(8,128)(2,1)}, bf16[32,128]{1,0:T(8,128)(2,1)}, bf16[16,128]{1,0:T(8,128)(2,1)}, bf16[16,128]{1,0:T(8,128)(2,1)}) custom-call(s32[8]{0:T(128)} %compare_select_fusion.1.info, f32[32,768]{1,0:T(8,128)} %get-tuple-element.32.in_ref, bf16[512,768]{1,0:T(8,128)(2,1)} %get-tuple-element.34.query_ref, ...), custom_call_target="tpu_custom_call" | custom-call | flops 10000000 | bytes 65536 | tf_op jit(solution)/shard_map/attend/pallas_call | solution.py:376
  58.1 2.4 %collective-permute-start.9 = (bf16[16,128]{1,0:T(8,128)(2,1)}, bf16[16,128]{1,0:T(8,128)(2,1)S(1)}, u32[]{:S(2)}, u32[]{:S(2)}) collective-permute-start(bf16[16,128]{1,0:T(8,128)(2,1)} %get-tuple-element.38), channel_id=1, source_target_pairs={{1,2},{3,4},{5,6},{7,8},{9,10},{11,12},{13,14},{2,1},{4,3},{6,5},{... | collective-permute-start | bytes 12296 | tf_op jit(solution)/shard_map/ppermute | solution.py:281
  60.5 3.6 %collective-permute-done.9.odd_ref = bf16[16,128]{1,0:T(8,128)(2,1)S(1)} collective-permute-done((bf16[16,128]{1,0:T(8,128)(2,1)}, bf16[16,128]{1,0:T(8,128)(2,1)S(1)}, u32[]{:S(2)}, u32[]{:S(2)}) %collective-permute-start.9) | collective-permute-done | bytes 4128 | tf_op jit(solution)/shard_map/ppermute | solution.py:281
  64.1 0.6 copy-done.7
  64.7 2.1 %final.1 = f32[3,384]{1,0:T(4,128)} custom-call(s32[8]{0:T(128)} %compare_select_fusion.1.info, bf16[64,384]{1,0:T(8,128)(2,1)} %get-tuple-element.27.hot_ref, f32[384,128]{1,0:T(8,128)} %get-tuple-element.28.mid_ref, bf16[32,128]{1,0:T(8,128)(2,1)} %get-tuple-element.36.back_ref, bf16[16,128]{1,0:T(8,128)(2,1)} %copy-done.6, bf16[16,128]{1,0:T(8,128)(2,1)} %copy-done.7, ...), custom_call_target="tpu_custom_call" | custom-call | flops 10000000 | bytes 4608 | tf_op jit(solution)/shard_map/final/pallas_call | solution.py:389
  (28 shorter events, 1.2 us)
Async XLA Ops:
  4.6 4.7 %collective-permute-start = (bf16[96,256]{1,0:T(8,128)(2,1)}, bf16[96,256]{1,0:T(8,128)(2,1)S(1)}, u32[]{:S(2)}, u32[]{:S(2)}) collective-permute-start(bf16[96,256]{1,0:T(8,128)(2,1)} %get-tuple-element.25), channel_id=1, source_target_pairs={{0,1},{1,0},{2,3},{3,2},{4,5},{5,4},{6,7},{7,6},{8,9},{9,8},{10,11... | collective-permute-start | bytes 147464 | tf_op jit(solution)/shard_map/ppermute | solution.py:281
  4.6 6.6 %collective-permute-start.1 = (bf16[96,256]{1,0:T(8,128)(2,1)}, bf16[96,256]{1,0:T(8,128)(2,1)S(1)}, u32[]{:S(2)}, u32[]{:S(2)}) collective-permute-start(bf16[96,256]{1,0:T(8,128)(2,1)} %get-tuple-element.26), channel_id=1, source_target_pairs={{1,2},{3,4},{5,6},{7,8},{9,10},{11,12},{13,14},{2,1},{4,3},{6,5},{... | collective-permute-start | bytes 147464 | tf_op jit(solution)/shard_map/ppermute | solution.py:281
  9.3 1.9 %copy-start.2 = (bf16[96,256]{1,0:T(8,128)(2,1)}, bf16[96,256]{1,0:T(8,128)(2,1)S(1)}, u32[]{:S(2)}) copy-start(bf16[96,256]{1,0:T(8,128)(2,1)S(1)} %collective-permute-done.pair_ref) | copy-start | bytes 147460
  11.2 0.6 copy-start.3
  18.6 3.3 %collective-permute-start.2 = (bf16[16,896]{1,0:T(8,128)(2,1)}, bf16[16,896]{1,0:T(8,128)(2,1)S(1)}, u32[]{:S(2)}, u32[]{:S(2)}) collective-permute-start(bf16[16,896]{1,0:T(8,128)(2,1)} %get-tuple-element.30), channel_id=1, source_target_pairs={{0,1},{1,0},{2,3},{3,2},{4,5},{5,4},{6,7},{7,6},{8,9},{9,8},{10,11... | collective-permute-start | bytes 86024 | tf_op jit(solution)/shard_map/ppermute | solution.py:281
  18.6 6.4 %collective-permute-start.3 = (bf16[16,896]{1,0:T(8,128)(2,1)}, bf16[16,896]{1,0:T(8,128)(2,1)S(1)}, u32[]{:S(2)}, u32[]{:S(2)}) collective-permute-start(bf16[16,896]{1,0:T(8,128)(2,1)} %get-tuple-element.31), channel_id=1, source_target_pairs={{1,2},{3,4},{5,6},{7,8},{9,10},{11,12},{13,14},{2,1},{4,3},{6,5},{... | collective-permute-start | bytes 86024 | tf_op jit(solution)/shard_map/ppermute | solution.py:281
  21.9 3.0 %copy-start.4 = (bf16[16,896]{1,0:T(8,128)(2,1)}, bf16[16,896]{1,0:T(8,128)(2,1)S(1)}, u32[]{:S(2)}) copy-start(bf16[16,896]{1,0:T(8,128)(2,1)S(1)} %collective-permute-done.2.pair_ref) | copy-start | bytes 86020
  25.0 0.6 copy-start.5
  27.5 18.5 %copy-start = (bf16[32,768]{1,0:T(8,128)(2,1)S(1)}, bf16[32,768]{1,0:T(8,128)(2,1)}, u32[]{:S(2)}) copy-start(bf16[32,768]{1,0:T(8,128)(2,1)} %get-tuple-element.33.norm_ref) | copy-start | bytes 147460
  27.5 5.6 %collective-permute-start.4 = (bf16[32,768]{1,0:T(8,128)(2,1)}, bf16[32,768]{1,0:T(8,128)(2,1)S(1)}, u32[]{:S(2)}, u32[]{:S(2)}) collective-permute-start(bf16[32,768]{1,0:T(8,128)(2,1)} %get-tuple-element.33.norm_ref), channel_id=1, source_target_pairs={{0,8},{1,9},{2,10},{3,11},{4,12},{5,13},{6,14},{7,15},{8,0},{9,1},... | collective-permute-start | bytes 147464 | tf_op jit(solution)/shard_map/ppermute | solution.py:299
  33.9 4.6 %collective-permute-start.5 = (bf16[64,768]{1,0:T(8,128)(2,1)S(1)}, bf16[64,768]{1,0:T(8,128)(2,1)S(1)}, u32[]{:S(2)}, u32[]{:S(2)}) collective-permute-start(bf16[64,768]{1,0:T(8,128)(2,1)S(1)} %pad_maximum_fusion.2), channel_id=1, source_target_pairs={{0,4},{1,3},{2,6},{3,1},{4,0},{5,7},{6,2},{7,5},{8,12},{9,11},{10,... | collective-permute-start | bytes 294920 | tf_op jit(solution)/shard_map/ppermute | solution.py:299
  39.3 5.7 %collective-permute-start.6 = (bf16[128,768]{1,0:T(8,128)(2,1)S(1)}, bf16[128,768]{1,0:T(8,128)(2,1)S(1)}, u32[]{:S(2)}, u32[]{:S(2)}) collective-permute-start(bf16[128,768]{1,0:T(8,128)(2,1)S(1)} %pad_maximum_fusion.1), channel_id=1, source_target_pairs={{0,2},{1,5},{2,0},{3,7},{4,6},{5,1},{6,4},{7,3},{8,10},{9,13},{10,... | collective-permute-start | bytes 589832 | tf_op jit(solution)/shard_map/ppermute | solution.py:299
  45.9 4.3 %collective-permute-start.7 = (bf16[256,768]{1,0:T(8,128)(2,1)S(1)}, bf16[256,768]{1,0:T(8,128)(2,1)S(1)}, u32[]{:S(2)}, u32[]{:S(2)}) collective-permute-start(bf16[256,768]{1,0:T(8,128)(2,1)S(1)} %pad_maximum_fusion), channel_id=1, source_target_pairs={{0,1},{1,0},{2,3},{3,2},{4,5},{5,4},{6,7},{7,6},{8,9},{9,8},{10,11... | collective-permute-start | bytes 1179656 | tf_op jit(solution)/shard_map/ppermute | solution.py:299
  50.2 0.9 %copy-start.1 = (bf16[512,768]{1,0:T(8,128)(2,1)}, bf16[512,768]{1,0:T(8,128)(2,1)S(1)}, u32[]{:S(2)}) copy-start(bf16[512,768]{1,0:T(8,128)(2,1)S(1)} %constant_dynamic-update-slice_fusion.all_ref) | copy-start | bytes 2359300
  57.6 2.9 %collective-permute-start.8 = (bf16[16,128]{1,0:T(8,128)(2,1)}, bf16[16,128]{1,0:T(8,128)(2,1)S(1)}, u32[]{:S(2)}, u32[]{:S(2)}) collective-permute-start(bf16[16,128]{1,0:T(8,128)(2,1)} %get-tuple-element.37), channel_id=1, source_target_pairs={{0,1},{1,0},{2,3},{3,2},{4,5},{5,4},{6,7},{7,6},{8,9},{9,8},{10,11... | collective-permute-start | bytes 12296 | tf_op jit(solution)/shard_map/ppermute | solution.py:281
  58.1 6.0 %collective-permute-start.9 = (bf16[16,128]{1,0:T(8,128)(2,1)}, bf16[16,128]{1,0:T(8,128)(2,1)S(1)}, u32[]{:S(2)}, u32[]{:S(2)}) collective-permute-start(bf16[16,128]{1,0:T(8,128)(2,1)} %get-tuple-element.38), channel_id=1, source_target_pairs={{1,2},{3,4},{5,6},{7,8},{9,10},{11,12},{13,14},{2,1},{4,3},{6,5},{... | collective-permute-start | bytes 12296 | tf_op jit(solution)/shard_map/ppermute | solution.py:281
  60.5 3.6 %copy-start.6 = (bf16[16,128]{1,0:T(8,128)(2,1)}, bf16[16,128]{1,0:T(8,128)(2,1)S(1)}, u32[]{:S(2)}) copy-start(bf16[16,128]{1,0:T(8,128)(2,1)S(1)} %collective-permute-done.8.pair_ref) | copy-start | bytes 12292
  64.1 0.6 copy-start.7

commit v2 on v1

--- a/solution.py
+++ b/solution.py
@@ -47,7 +47,7 @@
 SMEM = pl.BlockSpec(memory_space=pltpu.SMEM)
 
 
-def call(body, outs, name, specs, scratch=(), flops=10**7, limit=None):
+def call(body, outs, name, specs, scratch=(), flops=10**7, limit=8):
     moved = sum(o.size * o.dtype.itemsize for o in outs)
     return pl.pallas_call(
         body,
@@ -57,7 +57,7 @@
         scratch_shapes=list(scratch),
         name=name,
         cost_estimate=pl.CostEstimate(flops=flops, bytes_accessed=moved, transcendentals=0),
-        compiler_params=pltpu.CompilerParams(vmem_limit_bytes=limit),
+        compiler_params=pltpu.CompilerParams(vmem_limit_bytes=limit * 2**20),
     )
 
 

time: 67.2 us -> 60.7 us (0.903)
  Pallas kernels: 24.1 us -> 13.7 us
  local copies, waits for them, and re-layouts: 4.03 us -> 10.6 us
  other arithmetic: 3.03 us -> 0.06 us
    unnamed x20 -> x42, local copies, waits for them, and re-layouts: 2.75 us -> 9.86 us
    pallas_call x1, Pallas kernels: 4.13 us -> 0.96 us  [on_device(): call(query_body, [shape((TH * block_rows, model), BF16), shape((block_row...]
    pallas_call x1, Pallas kernels: 6.49 us -> 3.69 us  [on_device(): call(functools.partial(attend_body, orders, half), [shape((block_rows, mo...]
    concatenate x3, other arithmetic: 2.44 us -> 0.05 us  [gather(): norm = jnp.concatenate([norm, lax.ppermute(norm, 'row', perm)], axis=0)]
    pallas_call x1, Pallas kernels: 6.76 us -> 5.04 us  [on_device(): call(functools.partial(atoms_body, half), [shape((rows, width), F32), sha...]
    pallas_call x1, Pallas kernels: 2.74 us -> 1.48 us  [on_device(): call(embed_body, [shape((rows, width), F32), shape((rows, width), BF16),...]
    pallas_call x1, Pallas kernels: 1.89 us -> 0.88 us  [on_device(): call(token_body, [shape((block_rows, model), F32), shape((block_rows, mod...]
  transfers between devices with their start and end apart: 10 -> 10, of which waited for: 6 -> 6; matrix products, arithmetic and copies ran while one was open for 2% -> 1% of each run, Pallas kernels for 6% -> 2%
where the time goes in v2:
time: 60.7 us; the launch traced here: 60.1 us
  waiting for transfers between devices  23.8 us (39%)
  Pallas kernels  13.7 us (23%)
  local copies, waits for them, and re-layouts  10.6 us (17%)
  starting transfers between devices  10.4 us (17%)
  between operations  1.51 us (2%)
    ppermute x4, waiting for transfers between devices, gather(): norm = jnp.concatenate([norm, lax.ppermute(norm, 'row', perm)], axis=0)  15.3 us
    unnamed x42, local copies, waits for them, and re-layouts  9.86 us
    ppermute x6, starting transfers between devices, exchange(): return (lax.ppermute(pair, 'row', pairs), lax.ppermute(odd, 'row', odds))  9.72 us
    ppermute x6, waiting for transfers between devices, exchange(): return (lax.ppermute(pair, 'row', pairs), lax.ppermute(odd, 'row', odds))  8.57 us
    pallas_call x1, Pallas kernels, on_device(): call(functools.partial(atoms_body, half), [shape((rows, width), F32), sha...  5.04 us
    pallas_call x1, Pallas kernels, on_device(): call(functools.partial(attend_body, orders, half), [shape((block_rows, mo...  3.69 us
    pallas_call x1, Pallas kernels, on_device(): call(final_body, [shape(positions.shape, F32)], 'final', [SMEM] + [VMEM]...  1.69 us
    pallas_call x1, Pallas kernels, on_device(): call(embed_body, [shape((rows, width), F32), shape((rows, width), BF16),...  1.48 us
  transfers between devices with their start and end apart: 10, of which 6 were waited for; matrix products, arithmetic and copies ran while one was open for 1% of the time, Pallas kernels for 2%

profile of v2, /device:TPU:24, one launch (start us, length us, event | category | flops | bytes accessed | tf_op | source)
XLA Modules:
  0.0 60.1 jit_solution(3368577142867194335)
XLA Ops:
  1.3 0.9 %copy-done.7 = bf16[384,128]{1,0:T(8,128)(2,1)S(1)} copy-done((bf16[384,128]{1,0:T(8,128)(2,1)S(1)}, bf16[384,128]{1,0:T(8,128)(2,1)}, u32[]{:S(2)}) %copy-start.7) | copy-done | bytes 98328
  2.2 0.9 %copy-done.8 = bf16[128,384]{1,0:T(8,128)(2,1)S(1)} copy-done((bf16[128,384]{1,0:T(8,128)(2,1)S(1)}, bf16[128,384]{1,0:T(8,128)(2,1)}, u32[]{:S(2)}) %copy-start.8) | copy-done | bytes 98328
  3.1 0.7 %copy-done.12 = f32[3,384]{1,0:T(4,128)S(1)} copy-done((f32[3,384]{1,0:T(4,128)S(1)}, f32[3,384]{1,0:T(4,128)}, u32[]{:S(2)}) %copy-start.12) | copy-done | bytes 4632
  3.8 0.7 %copy-done.14 = f32[3,384]{1,0:T(4,128)S(1)} copy-done((f32[3,384]{1,0:T(4,128)S(1)}, f32[3,384]{1,0:T(4,128)}, u32[]{:S(2)}) %copy-start.14) | copy-done | bytes 4632
  5.1 1.5 %embed.1 = (f32[384,128]{1,0:T(8,128)S(1)}, bf16[384,128]{1,0:T(8,128)(2,1)S(1)}, f32[480,128]{1,0:T(8,128)S(1)}, f32[480,128]{1,0:T(8,128)S(1)}, bf16[96,256]{1...) custom-call(s32[8]{0:T(128)S(1)} %compare_select_fusion.1.info, f32[3,384]{1,0:T(4,128)S(1)} %copy-done.12, ...), custom_call_target="tpu_custom_call" | custom-call | flops 10000000 | bytes 884736 | tf_op jit(solution)/shard_map/embed/pallas_call | solution.py:334
  6.7 3.4 %collective-permute-start.1 = (bf16[96,256]{1,0:T(8,128)(2,1)S(1)}, bf16[96,256]{1,0:T(8,128)(2,1)S(1)}, u32[]{:S(2)}, u32[]{:S(2)}) collective-permute-start(bf16[96,256]{1,0:T(8,128)(2,1)S(1)} %get-tuple-element.26), channel_id=1, source_target_pairs={{1,2},{3,4},{5,6},{7,8},{9,10},{11,12},{13,14},{2,1},{4,3},{6,5},{... | collective-permute-start | bytes 147464 | tf_op jit(solution)/shard_map/ppermute | solution.py:281
  10.8 2.3 %collective-permute-done.1.odd_ref = bf16[96,256]{1,0:T(8,128)(2,1)S(1)} collective-permute-done((bf16[96,256]{1,0:T(8,128)(2,1)S(1)}, bf16[96,256]{1,0:T(8,128)(2,1)S(1)}, u32[]{:S(2)}, u32[]{:S(2)}) %collective-permute-start.1) | collective-permute-done | bytes 49184 | tf_op jit(solution)/shard_map/ppermute | solution.py:281
  13.1 1.1 %copy-done.4 = f32[4,384,128]{2,1,0:T(8,128)S(1)} copy-done((f32[4,384,128]{2,1,0:T(8,128)S(1)}, f32[4,384,128]{2,1,0:T(8,128)}, u32[]{:S(2)}) %copy-start.4) | copy-done | bytes 786456
  14.3 0.9 %copy-done.5 = bf16[128,768]{1,0:T(8,128)(2,1)S(1)} copy-done((bf16[128,768]{1,0:T(8,128)(2,1)S(1)}, bf16[128,768]{1,0:T(8,128)(2,1)}, u32[]{:S(2)}) %copy-start.5) | copy-done | bytes 196632
  15.2 0.8 %copy-done.11 = bf16[128,128]{1,0:T(8,128)(2,1)S(1)} copy-done((bf16[128,128]{1,0:T(8,128)(2,1)S(1)}, bf16[128,128]{1,0:T(8,128)(2,1)}, u32[]{:S(2)}) %copy-start.11) | copy-done | bytes 32792
  16.6 5.0 %atoms.1 = (f32[384,128]{1,0:T(8,128)S(1)}, f32[32,896]{1,0:T(8,128)S(1)}, bf16[16,896]{1,0:T(8,128)(2,1)S(1)}, bf16[16,896]{1,0:T(8,128)(2,1)S(1)}, bf16[64,384]{1,0:T(8,128)(2,1)S(1)}) custom-call(s32[8]{0:T(128)S(1)} %compare_select_fusion.1.info, s32[12]{0:T(128)S(1)} %copy-done.18, s32[1,384]{1,0:T(1,128)S(1)} %broadcast_in_dim.18.token_ref, ...), custom_call_target="tpu_custom_call" | custom-call | flops 10000000 | bytes 417792 | tf_op jit(solution)/shard_map/atoms/pallas_call | solution.py:349
  21.7 3.3 %collective-permute-start.3 = (bf16[16,896]{1,0:T(8,128)(2,1)S(1)}, bf16[16,896]{1,0:T(8,128)(2,1)S(1)}, u32[]{:S(2)}, u32[]{:S(2)}) collective-permute-start(bf16[16,896]{1,0:T(8,128)(2,1)S(1)} %get-tuple-element.31), channel_id=1, source_target_pairs={{1,2},{3,4},{5,6},{7,8},{9,10},{11,12},{13,14},{2,1},{4,3},{6,5},{... | collective-permute-start | bytes 86024 | tf_op jit(solution)/shard_map/ppermute | solution.py:281
  25.0 2.8 %collective-permute-done.3.odd_ref = bf16[16,896]{1,0:T(8,128)(2,1)S(1)} collective-permute-done((bf16[16,896]{1,0:T(8,128)(2,1)S(1)}, bf16[16,896]{1,0:T(8,128)(2,1)S(1)}, u32[]{:S(2)}, u32[]{:S(2)}) %collective-permute-start.3) | collective-permute-done | bytes 28704 | tf_op jit(solution)/shard_map/ppermute | solution.py:281
  27.9 0.9 %token_.1 = (f32[32,768]{1,0:T(8,128)S(1)}, bf16[32,768]{1,0:T(8,128)(2,1)S(1)}) custom-call(s32[8]{0:T(128)S(1)} %compare_select_fusion.1.info, f32[32,896]{1,0:T(8,128)S(1)} %get-tuple-element.29.own_ref, bf16[16,896]{1,0:T(8,128)(2,1)S(1)} %collective-permute-done.2.pair_ref, bf16[16,896]{1,0:T(8,128)(2,1)S(1)} %collective-permute-done.3.odd_ref, ...), custom_call_target="tpu_custom_call" | custom-call | flops 10000000 | bytes 147456 | tf_op jit(solution)/shard_map/token/pallas_call | solution.py:363
  29.2 5.1 %collective-permute-done.4 = bf16[32,768]{1,0:T(8,128)(2,1)S(1)} collective-permute-done((bf16[32,768]{1,0:T(8,128)(2,1)S(1)}, bf16[32,768]{1,0:T(8,128)(2,1)S(1)}, u32[]{:S(2)}, u32[]{:S(2)}) %collective-permute-start.4) | collective-permute-done | bytes 49184 | tf_op jit(solution)/shard_map/ppermute | solution.py:299
  34.4 4.5 %collective-permute-done.5 = bf16[64,768]{1,0:T(8,128)(2,1)S(1)} collective-permute-done((bf16[64,768]{1,0:T(8,128)(2,1)S(1)}, bf16[64,768]{1,0:T(8,128)(2,1)S(1)}, u32[]{:S(2)}, u32[]{:S(2)}) %collective-permute-start.5) | collective-permute-done | bytes 98336 | tf_op jit(solution)/shard_map/ppermute | solution.py:299
  39.0 5.7 %collective-permute-done.6 = bf16[128,768]{1,0:T(8,128)(2,1)S(1)} collective-permute-done((bf16[128,768]{1,0:T(8,128)(2,1)S(1)}, bf16[128,768]{1,0:T(8,128)(2,1)S(1)}, u32[]{:S(2)}, u32[]{:S(2)}) %collective-permute-start.6) | collective-permute-done | bytes 196640 | tf_op jit(solution)/shard_map/ppermute | solution.py:299
  44.8 1.3 %copy-done.1 = bf16[768,768]{1,0:T(8,128)(2,1)S(1)} copy-done((bf16[768,768]{1,0:T(8,128)(2,1)S(1)}, bf16[768,768]{1,0:T(8,128)(2,1)}, u32[]{:S(2)}) %copy-start.1) | copy-done | bytes 1179672
  46.1 1.0 %query.1 = (bf16[512,768]{1,0:T(8,128)(2,1)S(1)}, f32[32,768]{1,0:T(8,128)S(1)}) custom-call(bf16[32,768]{1,0:T(8,128)(2,1)S(1)} %get-tuple-element.33.norm_ref, bf16[768,2304]{1,0:T(8,128)(2,1)S(1)} %copy-done, bf16[768,768]{1,0:T(8,128)(2,1)S(1)} %copy-done.1), custom_call_target="tpu_custom_call" | custom-call | flops 10000000 | bytes 884736 | tf_op jit(solution)/shard_map/query/pallas_call | solution.py:370
  47.3 1.1 %copy-done.2 = bf16[768,768]{1,0:T(8,128)(2,1)S(1)} copy-done((bf16[768,768]{1,0:T(8,128)(2,1)S(1)}, bf16[768,768]{1,0:T(8,128)(2,1)}, u32[]{:S(2)}) %copy-start.2) | copy-done | bytes 1179672
  48.4 3.7 %attend.1 = (bf16[32,768]{1,0:T(8,128)(2,1)}, bf16[32,128]{1,0:T(8,128)(2,1)S(1)}, bf16[16,128]{1,0:T(8,128)(2,1)S(1)}, bf16[16,128]{1,0:T(8,128)(2,1)S(1)}) custom-call(s32[8]{0:T(128)S(1)} %compare_select_fusion.1.info, f32[32,768]{1,0:T(8,128)S(1)} %get-tuple-element.32.in_ref, bf16[512,768]{1,0:T(8,128)(2,1)S(1)} %get-tuple-element.34.query_ref, ...), custom_call_target="tpu_custom_call" | custom-call | flops 10000000 | bytes 65536 | tf_op jit(solution)/shard_map/attend/pallas_call | solution.py:376
  52.6 2.4 %collective-permute-start.9 = (bf16[16,128]{1,0:T(8,128)(2,1)S(1)}, bf16[16,128]{1,0:T(8,128)(2,1)S(1)}, u32[]{:S(2)}, u32[]{:S(2)}) collective-permute-start(bf16[16,128]{1,0:T(8,128)(2,1)S(1)} %get-tuple-element.38), channel_id=1, source_target_pairs={{1,2},{3,4},{5,6},{7,8},{9,10},{11,12},{13,14},{2,1},{4,3},{6,5},{... | collective-permute-start | bytes 12296 | tf_op jit(solution)/shard_map/ppermute | solution.py:281
  55.0 3.4 %collective-permute-done.9.odd_ref = bf16[16,128]{1,0:T(8,128)(2,1)S(1)} collective-permute-done((bf16[16,128]{1,0:T(8,128)(2,1)S(1)}, bf16[16,128]{1,0:T(8,128)(2,1)S(1)}, u32[]{:S(2)}, u32[]{:S(2)}) %collective-permute-start.9) | collective-permute-done | bytes 4128 | tf_op jit(solution)/shard_map/ppermute | solution.py:281
  58.4 1.7 %final.1 = f32[3,384]{1,0:T(4,128)} custom-call(s32[8]{0:T(128)S(1)} %compare_select_fusion.1.info, bf16[64,384]{1,0:T(8,128)(2,1)S(1)} %get-tuple-element.27.hot_ref, f32[384,128]{1,0:T(8,128)S(1)} %get-tuple-element.28.mid_ref, bf16[32,128]{1,0:T(8,128)(2,1)S(1)} %get-tuple-element.36.back_ref, bf16[16,128]{1,0:T(8,128)(2,1)S(1)} %collective-permute-done.8.pair_ref, ...), custom_call_target="tpu_custom_call" | custom-call | flops 10000000 | bytes 4608 | tf_op jit(solution)/shard_map/final/pallas_call | solution.py:389
  (50 shorter events, 3.7 us)
Async XLA Ops:
  1.3 0.9 %copy-start.7 = (bf16[384,128]{1,0:T(8,128)(2,1)S(1)}, bf16[384,128]{1,0:T(8,128)(2,1)}, u32[]{:S(2)}) copy-start(bf16[384,128]{1,0:T(8,128)(2,1)} %single_ref.2) | copy-start | bytes 294916
  2.2 0.9 %copy-start.8 = (bf16[128,384]{1,0:T(8,128)(2,1)S(1)}, bf16[128,384]{1,0:T(8,128)(2,1)}, u32[]{:S(2)}) copy-start(bf16[128,384]{1,0:T(8,128)(2,1)} %wqkv_ref.3) | copy-start | bytes 294916
  5.1 22.7 %copy-start.10 = (bf16[32,768]{1,0:T(8,128)(2,1)S(1)}, bf16[32,768]{1,0:T(8,128)(2,1)}, u32[]{:S(2)}) copy-start(bf16[32,768]{1,0:T(8,128)(2,1)} %single_ref.3) | copy-start | bytes 147460
  6.6 4.2 %collective-permute-start = (bf16[96,256]{1,0:T(8,128)(2,1)S(1)}, bf16[96,256]{1,0:T(8,128)(2,1)S(1)}, u32[]{:S(2)}, u32[]{:S(2)}) collective-permute-start(bf16[96,256]{1,0:T(8,128)(2,1)S(1)} %get-tuple-element.25), channel_id=1, source_target_pairs={{0,1},{1,0},{2,3},{3,2},{4,5},{5,4},{6,7},{7,6},{8,9},{9,8},{10,11... | collective-permute-start | bytes 147464 | tf_op jit(solution)/shard_map/ppermute | solution.py:281
  6.7 6.4 %collective-permute-start.1 = (bf16[96,256]{1,0:T(8,128)(2,1)S(1)}, bf16[96,256]{1,0:T(8,128)(2,1)S(1)}, u32[]{:S(2)}, u32[]{:S(2)}) collective-permute-start(bf16[96,256]{1,0:T(8,128)(2,1)S(1)} %get-tuple-element.26), channel_id=1, source_target_pairs={{1,2},{3,4},{5,6},{7,8},{9,10},{11,12},{13,14},{2,1},{4,3},{6,5},{... | collective-permute-start | bytes 147464 | tf_op jit(solution)/shard_map/ppermute | solution.py:281
  13.1 1.1 %copy-start.4 = (f32[4,384,128]{2,1,0:T(8,128)S(1)}, f32[4,384,128]{2,1,0:T(8,128)}, u32[]{:S(2)}) copy-start(f32[4,384,128]{2,1,0:T(8,128)} %bias_ref.2) | copy-start | bytes 2359300
  14.3 0.9 %copy-start.5 = (bf16[128,768]{1,0:T(8,128)(2,1)S(1)}, bf16[128,768]{1,0:T(8,128)(2,1)}, u32[]{:S(2)}) copy-start(bf16[128,768]{1,0:T(8,128)(2,1)} %wagg_ref.1) | copy-start | bytes 589828
  16.6 28.2 %copy-start = (bf16[768,2304]{1,0:T(8,128)(2,1)S(1)}, bf16[768,2304]{1,0:T(8,128)(2,1)}, u32[]{:S(2)}) copy-start(bf16[768,2304]{1,0:T(8,128)(2,1)} %wqkv_ref.5) | copy-start | bytes 10616836
  21.6 3.4 %collective-permute-start.2 = (bf16[16,896]{1,0:T(8,128)(2,1)S(1)}, bf16[16,896]{1,0:T(8,128)(2,1)S(1)}, u32[]{:S(2)}, u32[]{:S(2)}) collective-permute-start(bf16[16,896]{1,0:T(8,128)(2,1)S(1)} %get-tuple-element.30), channel_id=1, source_target_pairs={{0,1},{1,0},{2,3},{3,2},{4,5},{5,4},{6,7},{7,6},{8,9},{9,8},{10,11... | collective-permute-start | bytes 86024 | tf_op jit(solution)/shard_map/ppermute | solution.py:281
  21.7 6.2 %collective-permute-start.3 = (bf16[16,896]{1,0:T(8,128)(2,1)S(1)}, bf16[16,896]{1,0:T(8,128)(2,1)S(1)}, u32[]{:S(2)}, u32[]{:S(2)}) collective-permute-start(bf16[16,896]{1,0:T(8,128)(2,1)S(1)} %get-tuple-element.31), channel_id=1, source_target_pairs={{1,2},{3,4},{5,6},{7,8},{9,10},{11,12},{13,14},{2,1},{4,3},{6,5},{... | collective-permute-start | bytes 86024 | tf_op jit(solution)/shard_map/ppermute | solution.py:281
  28.8 5.5 %collective-permute-start.4 = (bf16[32,768]{1,0:T(8,128)(2,1)S(1)}, bf16[32,768]{1,0:T(8,128)(2,1)S(1)}, u32[]{:S(2)}, u32[]{:S(2)}) collective-permute-start(bf16[32,768]{1,0:T(8,128)(2,1)S(1)} %get-tuple-element.33.norm_ref), channel_id=1, source_target_pairs={{0,8},{1,9},{2,10},{3,11},{4,12},{5,13},{6,14},{7,15},{8,0},{9,1},... | collective-permute-start | bytes 147464 | tf_op jit(solution)/shard_map/ppermute | solution.py:299
  34.3 4.7 %collective-permute-start.5 = (bf16[64,768]{1,0:T(8,128)(2,1)S(1)}, bf16[64,768]{1,0:T(8,128)(2,1)S(1)}, u32[]{:S(2)}, u32[]{:S(2)}) collective-permute-start(bf16[64,768]{1,0:T(8,128)(2,1)S(1)} %pad_maximum_fusion.2), channel_id=1, source_target_pairs={{0,4},{1,3},{2,6},{3,1},{4,0},{5,7},{6,2},{7,5},{8,12},{9,11},{10,... | collective-permute-start | bytes 294920 | tf_op jit(solution)/shard_map/ppermute | solution.py:299
  39.0 5.7 %collective-permute-start.6 = (bf16[128,768]{1,0:T(8,128)(2,1)S(1)}, bf16[128,768]{1,0:T(8,128)(2,1)S(1)}, u32[]{:S(2)}, u32[]{:S(2)}) collective-permute-start(bf16[128,768]{1,0:T(8,128)(2,1)S(1)} %pad_maximum_fusion.1), channel_id=1, source_target_pairs={{0,2},{1,5},{2,0},{3,7},{4,6},{5,1},{6,4},{7,3},{8,10},{9,13},{10,... | collective-permute-start | bytes 589832 | tf_op jit(solution)/shard_map/ppermute | solution.py:299
  44.7 2.4 %collective-permute-start.7 = (bf16[256,768]{1,0:T(8,128)(2,1)S(1)}, bf16[256,768]{1,0:T(8,128)(2,1)S(1)}, u32[]{:S(2)}, u32[]{:S(2)}) collective-permute-start(bf16[256,768]{1,0:T(8,128)(2,1)S(1)} %pad_maximum_fusion), channel_id=1, source_target_pairs={{0,1},{1,0},{2,3},{3,2},{4,5},{5,4},{6,7},{7,6},{8,9},{9,8},{10,11... | collective-permute-start | bytes 1179656 | tf_op jit(solution)/shard_map/ppermute | solution.py:299
  44.8 1.3 %copy-start.1 = (bf16[768,768]{1,0:T(8,128)(2,1)S(1)}, bf16[768,768]{1,0:T(8,128)(2,1)}, u32[]{:S(2)}) copy-start(bf16[768,768]{1,0:T(8,128)(2,1)} %wgate_ref.1) | copy-start | bytes 3538948
  46.1 1.2 %copy-start.3 = (f32[16,32,512]{2,1,0:T(8,128)S(1)}, f32[16,32,512]{2,1,0:T(8,128)}, u32[]{:S(2)}) copy-start(f32[16,32,512]{2,1,0:T(8,128)} %bias_ref.3) | copy-start | bytes 3145732
  47.1 1.3 %copy-start.2 = (bf16[768,768]{1,0:T(8,128)(2,1)S(1)}, bf16[768,768]{1,0:T(8,128)(2,1)}, u32[]{:S(2)}) copy-start(bf16[768,768]{1,0:T(8,128)(2,1)} %wout_ref.3) | copy-start | bytes 3538948
  47.1 1.3 %copy-start.6 = (bf16[768,128]{1,0:T(8,128)(2,1)S(1)}, bf16[768,128]{1,0:T(8,128)(2,1)}, u32[]{:S(2)}) copy-start(bf16[768,128]{1,0:T(8,128)(2,1)} %wback_ref.1) | copy-start | bytes 589828
  47.1 1.3 %copy-start.9 = (s32[32,512]{1,0:T(8,128)S(1)}, s32[32,512]{1,0:T(8,128)}, u32[]{:S(2)}) copy-start(s32[32,512]{1,0:T(8,128)} %mask_ref.1) | copy-start | bytes 196612
  48.4 10.0 %copy-start.13 = (f32[3,384]{1,0:T(4,128)S(1)}, f32[3,384]{1,0:T(4,128)}, u32[]{:S(2)}) copy-start(f32[3,384]{1,0:T(4,128)} %pos_ref.3) | copy-start | bytes 13828
  48.4 10.0 %copy-start.15 = (f32[3,384]{1,0:T(4,128)S(1)}, f32[3,384]{1,0:T(4,128)}, u32[]{:S(2)}) copy-start(f32[3,384]{1,0:T(4,128)} %noise_ref.3) | copy-start | bytes 13828
  48.4 10.0 %copy-start.17 = (bf16[3,128]{1,0:T(4,128)(2,1)S(1)}, bf16[3,128]{1,0:T(4,128)(2,1)}, u32[]{:S(2)}) copy-start(bf16[3,128]{1,0:T(4,128)(2,1)} %wpos_ref.1) | copy-start | bytes 2308
  52.1 2.9 %collective-permute-start.8 = (bf16[16,128]{1,0:T(8,128)(2,1)S(1)}, bf16[16,128]{1,0:T(8,128)(2,1)S(1)}, u32[]{:S(2)}, u32[]{:S(2)}) collective-permute-start(bf16[16,128]{1,0:T(8,128)(2,1)S(1)} %get-tuple-element.37), channel_id=1, source_target_pairs={{0,1},{1,0},{2,3},{3,2},{4,5},{5,4},{6,7},{7,6},{8,9},{9,8},{10,11... | collective-permute-start | bytes 12296 | tf_op jit(solution)/shard_map/ppermute | solution.py:281
  52.6 5.8 %collective-permute-start.9 = (bf16[16,128]{1,0:T(8,128)(2,1)S(1)}, bf16[16,128]{1,0:T(8,128)(2,1)S(1)}, u32[]{:S(2)}, u32[]{:S(2)}) collective-permute-start(bf16[16,128]{1,0:T(8,128)(2,1)S(1)} %get-tuple-element.38), channel_id=1, source_target_pairs={{1,2},{3,4},{5,6},{7,8},{9,10},{11,12},{13,14},{2,1},{4,3},{6,5},{... | collective-permute-start | bytes 12296 | tf_op jit(solution)/shard_map/ppermute | solution.py:281
  (5 other events, 3.5 us)

commit v3 on v2

v3 whole, which is shorter than its diff:
```python
import functools

import jax
import jax.numpy as jnp
from jax import lax
from jax.experimental import pallas as pl
from jax.experimental.pallas import tpu as pltpu
from jax.sharding import PartitionSpec as P

AH = 4
TH = 16
QWIN = 32
KWIN = 128
BEHIND = KWIN // 2
AHEAD = KWIN - QWIN

noise_level = 2.0
input_scale = 1.0 / 5.0**0.5
skip_scale = 1.0 / 5.0
output_scale = 2.0 / 5.0**0.5
masked_score = -1e30

F32 = jnp.float32
BF16 = jnp.bfloat16
NT = (((1,), (1,)), ((), ()))


def dot(a, b):
    return jnp.dot(a, b, preferred_element_type=F32)


def dot_nt(a, b):
    return lax.dot_general(a, b, NT, preferred_element_type=F32)


def normalize(values):
    center = values - jnp.mean(values, axis=-1, keepdims=True)
    spread = jnp.mean(center * center, axis=-1, keepdims=True)
    return center * lax.rsqrt(spread + 1e-05)


def iota(shape, dim):
    return lax.broadcasted_iota(jnp.int32, shape, dim)


VMEM = pl.BlockSpec(memory_space=pltpu.VMEM)
SMEM = pl.BlockSpec(memory_space=pltpu.SMEM)
HBM = pl.BlockSpec(memory_space=pltpu.HBM)


def call(body, outs, name, specs, scratch=(), flops=10**7, limit=8, out_specs=None):
    moved = sum(o.size * o.dtype.itemsize for o in outs)
    return pl.pallas_call(
        body,
        out_shape=tuple(outs),
        in_specs=specs,
        out_specs=tuple(out_specs or [VMEM] * len(outs)),
        scratch_shapes=list(scratch),
        name=name,
        cost_estimate=pl.CostEstimate(flops=flops, bytes_accessed=moved, transcendentals=0),
        compiler_params=pltpu.CompilerParams(vmem_limit_bytes=limit * 2**20),
    )


def shape(dims, dtype):
    return jax.ShapeDtypeStruct(dims, dtype)


def fetch(sems, *moves):
    copies = [pltpu.make_async_copy(src, dst, sems.at[n]) for n, (src, dst) in enumerate(moves)]
    for copy in copies:
        copy.start()
    return copies


def embed_body(
    counts_hbm,
    pos_hbm,
    noise_hbm,
    single_hbm,
    wc_hbm,
    wqkv_hbm,
    info_ref,
    start_ref,
    q_ref,
    k_ref,
    v_ref,
    pair_ref,
    odd_ref,
    counts_ref,
    pos_ref,
    noise_ref,
    single_ref,
    wc_ref,
    wqkv_ref,
    sems,
):
    copies = fetch(
        sems,
        (pos_hbm, pos_ref),
        (noise_hbm, noise_ref),
        (wc_hbm, wc_ref),
        (single_hbm, single_ref),
        (wqkv_hbm, wqkv_ref),
        (counts_hbm, counts_ref),
    )
    rows, width = single_ref.shape
    for ref in (k_ref, v_ref):
        ref[rows:, :] = jnp.zeros((AHEAD, width), F32)
    for copy in copies[:3]:
        copy.wait()
    scaled = input_scale * (pos_ref[...] + noise_level * noise_ref[...])
    padded = jnp.concatenate([scaled, jnp.zeros((5, rows), F32)], axis=0)
    across = jnp.transpose(padded)
    copies[3].wait()
    start = single_ref[...].astype(F32)
    for c in range(3):
        start = start + across[:, c : c + 1] * wc_ref[c : c + 1, :]
    start_ref[...] = start
    normed = normalize(start).astype(BF16)
    copies[4].wait()
    qkv = dot(normed, wqkv_ref[...]).astype(BF16)
    q_ref[...] = qkv[:, :width]
    copies[5].wait()
    live = counts_ref[0]
    me = lax.axis_index("row")
    info_ref[0] = live
    info_ref[1] = me
    info_ref[2] = lax.axis_size("row") - 1
    tail = live - BEHIND
    even = me % 2 == 0
    for n, ref in enumerate((k_ref, v_ref)):
        at = slice(n * width, (n + 1) * width)
        ref[:rows, :] = qkv[:, (n + 1) * width : (n + 2) * width].astype(F32)
        pair_ref[:, at] = ref[pl.ds(jnp.where(even, tail, 0), AHEAD), :].astype(BF16)
        odd_ref[:, at] = ref[pl.ds(jnp.where(even, 0, tail), AHEAD), :].astype(BF16)


def one_window(queries, keys, values, bias, allowed):
    width = queries.shape[1]
    depth = width // AH
    rows = AH * QWIN
    own_head = iota((rows, width), 0) // QWIN == iota((rows, width), 1) // depth
    stacked = jnp.where(own_head, jnp.concatenate([queries] * AH, axis=0), 0.0).astype(BF16)
    scores = dot_nt(stacked, keys.astype(BF16)) * (1.0 / depth**0.5) + bias
    if allowed is not None:
        scores = jnp.where(allowed, scores, masked_score)
    scores = jnp.exp(scores - jnp.max(scores, axis=-1, keepdims=True))
    weights = (scores / jnp.sum(scores, axis=-1, keepdims=True)).astype(BF16)
    mixed = dot(weights, values.astype(BF16))
    lane_head = iota((QWIN, width), 1) // depth
    out = mixed[:QWIN]
    for h in range(1, AH):
        out = jnp.where(lane_head == h, mixed[h * QWIN : (h + 1) * QWIN], out)
    return out.astype(BF16)


def local_body(
    offsets_hbm,
    q_ref,
    k_ref,
    v_ref,
    bias_hbm,
    wout_hbm,
    wagg_hbm,
    offsets_ref,
    bias_ref,
    wout_ref,
    wagg_ref,
    att_ref,
    sems,
):
    copies = fetch(
        sems, (offsets_hbm, offsets_ref), (bias_hbm, bias_ref), (wout_hbm, wout_ref), (wagg_hbm, wagg_ref)
    )
    rows, width = q_ref.shape
    windows = rows // QWIN
    skip = BEHIND // QWIN
    stop = windows - (AHEAD - QWIN) // QWIN
    for part in (slice(0, skip * QWIN), slice(stop * QWIN, rows)):
        att_ref[part, :] = jnp.zeros((part.stop - part.start, width), BF16)
    copies[0].wait()
    copies[1].wait()
    for m in range(skip, stop):
        at = slice(m * QWIN, (m + 1) * QWIN)
        base = m * QWIN + offsets_ref[m]
        bias = bias_ref[:, at, :].reshape(AH * QWIN, KWIN)
        att_ref[at, :] = one_window(
            q_ref[at, :].astype(F32), k_ref[pl.ds(base, KWIN), :], v_ref[pl.ds(base, KWIN), :], bias, None
        )
    copies[2].wait()
    copies[3].wait()


def onehot(info, token_ref, half, block_rows):
    rows = token_ref.shape[1]
    relative = token_ref[...] - (info[1] * block_rows - half)
    living = iota((1, rows), 1) < info[0]
    hot = (iota((block_rows + 2 * half, rows), 0) == relative) & living
    return hot.astype(F32)


def atoms_body(
    half,
    info,
    offsets,
    token_ref,
    start_ref,
    q_ref,
    k_ref,
    v_ref,
    pair_ref,
    odd_ref,
    att_ref,
    bias_ref,
    wout_ref,
    wagg_ref,
    mid_ref,
    own_ref,
    pair_out,
    odd_out,
    hot_ref,
    k_ext,
    v_ext,
    att,
):
    rows, width = start_ref.shape
    live, me, last = info[0], info[1], info[2]
    even = me % 2 == 0
    pair = pair_ref[...].astype(F32)
    odd = odd_ref[...].astype(F32)
    for n, (ref, ext) in enumerate(((k_ref, k_ext), (v_ref, v_ext))):
        at = slice(n * width, (n + 1) * width)
        ext[:BEHIND, :] = jnp.where(even, odd[:BEHIND, at], pair[:BEHIND, at])
        ext[BEHIND : BEHIND + rows + AHEAD, :] = ref[...]
        ext[pl.ds(BEHIND + live, AHEAD), :] = jnp.where(even, pair[:, at], odd[:, at])
    low = jnp.where(me > 0, 0, BEHIND)
    high = BEHIND + live + jnp.where(me < last, AHEAD, 0)
    att[...] = att_ref[...]
    windows = rows // QWIN
    tails = AHEAD // QWIN
    first = jnp.minimum((live - BEHIND) // QWIN, windows - tails)
    for m in list(range(BEHIND // QWIN)) + [first + n for n in range(tails)]:
        at = pl.ds(pl.multiple_of(m * QWIN, QWIN), QWIN)
        base = BEHIND + QWIN * m + offsets[m]
        slots = base + iota((1, KWIN), 1)
        bias = bias_ref[:, at, :].reshape(AH * QWIN, KWIN)
        att[at, :] = one_window(
            q_ref[at, :].astype(F32),
            k_ext[pl.ds(base, KWIN), :],
            v_ext[pl.ds(base, KWIN), :],
            bias,
            (slots >= low) & (slots < high),
        )
    mid = start_ref[...] + dot(att[...], wout_ref[...])
    mid_ref[...] = mid
    spread = jnp.maximum(dot(mid.astype(BF16), wagg_ref[...]), 0.0).astype(BF16)
    block_rows = own_ref.shape[0]
    hot = onehot(info, token_ref, half, block_rows)
    hot_ref[...] = jnp.transpose(hot).astype(BF16)
    sums = dot(hot.astype(BF16), spread)
    counts = jnp.sum(hot, axis=1, keepdims=True)
    first = jnp.minimum(counts, 256.0)
    lane = iota((counts.shape[0], 128), 1)
    packed = jnp.where(lane == 0, first, jnp.where(lane == 1, counts - first, 0.0))
    model = wagg_ref.shape[1]
    own_ref[:, :model] = sums[half : half + block_rows]
    own_ref[:, model:] = packed[half : half + block_rows]
    lower = jnp.concatenate([sums[:half], packed[:half]], axis=1)
    upper = jnp.concatenate([sums[half + block_rows :], packed[half + block_rows :]], axis=1)
    pair_out[...] = jnp.where(even, upper, lower).astype(BF16)
    odd_out[...] = jnp.where(even, lower, upper).astype(BF16)


def token_body(info, own_ref, pair_ref, odd_ref, single_ref, in_ref, norm_ref):
    even = info[1] % 2 == 0
    model = single_ref.shape[1]
    pair = pair_ref[...].astype(F32)
    odd = odd_ref[...].astype(F32)
    lower = jnp.where(info[1] > 0, jnp.where(even, odd, pair), 0.0)
    upper = jnp.where(info[1] < info[2], jnp.where(even, pair, odd), 0.0)
    both = own_ref[...] + jnp.concatenate([lower, upper], axis=0)
    count = both[:, model : model + 1] + both[:, model + 1 : model + 2]
    token_in = single_ref[...].astype(F32) + both[:, :model] / jnp.maximum(count, 1.0)
    in_ref[...] = token_in
    norm_ref[...] = normalize(token_in).astype(BF16)


def query_body(norm_ref, wqkv_hbm, wgate_hbm, query_ref, gate_ref, wq_ref, wk_ref, wgate_ref, sems):
    rows, model = norm_ref.shape
    copies = fetch(
        sems,
        (wqkv_hbm.at[:, :model], wq_ref),
        (wqkv_hbm.at[:, model : 2 * model], wk_ref),
        (wgate_hbm, wgate_ref),
    )
    width = model // TH
    group = TH // 2
    span = group * width
    norm = norm_ref[...]
    own = iota((group * rows, span), 0) // rows == iota((group * rows, span), 1) // width
    copies[0].wait()
    tq = dot(norm, wq_ref[...])
    copies[1].wait()
    for g in range(2):
        part = tq[:, g * span : (g + 1) * span]
        stacked = jnp.where(own, jnp.concatenate([part] * group, axis=0), 0.0).astype(BF16)
        wk = wk_ref[:, g * span : (g + 1) * span]
        query_ref[g * group * rows : (g + 1) * group * rows, :] = dot_nt(stacked, wk).astype(BF16)
    copies[2].wait()
    gate_ref[...] = jax.nn.sigmoid(dot(norm, wgate_ref[...]))


def stage_body(
    after,
    bias_hbm,
    mask_hbm,
    wqkv_hbm,
    wout_hbm,
    wback_hbm,
    bias_ref,
    wv_ref,
    wout_ref,
    wback_ref,
    mask_ref,
    sems,
):
    model = wout_hbm.shape[0]
    copies = fetch(
        sems,
        (mask_hbm, mask_ref),
        (bias_hbm, bias_ref),
        (wqkv_hbm.at[:, 2 * model :], wv_ref),
        (wout_hbm, wout_ref),
        (wback_hbm, wback_ref),
    )
    copies[0].wait()
    copies[1].wait()
    allowed = mask_ref[...] == 1
    for h in range(TH):
        bias_ref[h] = jnp.where(allowed, bias_ref[h], masked_score)
    for copy in copies[2:]:
        copy.wait()


def attend_body(
    orders,
    half,
    info,
    in_ref,
    query_ref,
    gate_ref,
    all_ref,
    bias_ref,
    wv_ref,
    wout_ref,
    wback_ref,
    out_ref,
    back_ref,
    pair_out,
    odd_out,
    sorted_ref,
):
    rows, model = in_ref.shape
    keys = all_ref.shape[0]
    me = info[1]
    even = me % 2 == 0
    kind = (me ^ (me >> 1) ^ (me >> 2)) & 1
    if orders is None:
        sorted_ref[...] = all_ref[...]
    else:
        for j in range(keys // rows):
            block = me ^ jnp.where(kind == 0, orders[0][j], orders[1][j])
            sorted_ref[pl.ds(pl.multiple_of(block * rows, rows), rows), :] = all_ref[j * rows : (j + 1) * rows, :]
    width = model // TH
    group = TH // 2
    span = group * width
    scale = 1.0 / width**0.5
    values = sorted_ref[...]
    lane_head = iota((rows, span), 1) // width
    for g in range(2):
        at = slice(g * group * rows, (g + 1) * group * rows)
        bias = bias_ref[g * group : (g + 1) * group].reshape(group * rows, keys)
        scores = dot_nt(query_ref[at, :], values) * scale + bias
        scores = jnp.exp(scores - jnp.max(scores, axis=-1, keepdims=True))
        weights = (scores / jnp.sum(scores, axis=-1, keepdims=True)).astype(BF16)
        mixed = dot(weights, values).astype(BF16)
        wide = dot(mixed, wv_ref[:, g * span : (g + 1) * span])
        part = wide[:rows]
        for h in range(1, group):
            part = jnp.where(lane_head == h, wide[h * rows : (h + 1) * rows], part)
        gated = (gate_ref[:, g * span : (g + 1) * span] * part).astype(BF16)
        added = dot(gated, wout_ref[g * span : (g + 1) * span, :])
        total = added if g == 0 else total + added
    token_out = (in_ref[...] + total).astype(BF16)
    out_ref[...] = token_out
    back = dot(token_out, wback_ref[...])
    back_ref[...] = back.astype(BF16)
    lower, upper = back[:half], back[rows - half :]
    pair_out[...] = jnp.where(even, upper, lower).astype(BF16)
    odd_out[...] = jnp.where(even, lower, upper).astype(BF16)


def final_body(info, hot_ref, mid_ref, back_ref, pair_ref, odd_ref, wpos_ref, pos_ref, noise_ref, out_ref):
    even = info[1] % 2 == 0
    pair = pair_ref[...].astype(F32)
    odd = odd_ref[...].astype(F32)
    near = jnp.concatenate(
        [jnp.where(even, odd, pair), back_ref[...].astype(F32), jnp.where(even, pair, odd)], axis=0
    ).astype(BF16)
    last = mid_ref[...] + dot(hot_ref[...], near)
    update = dot_nt(wpos_ref[...], normalize(last).astype(BF16))
    noisy = pos_ref[...] + noise_level * noise_ref[...]
    living = iota((1, noisy.shape[1]), 1) < info[0]
    out_ref[...] = jnp.where(living, skip_scale * noisy + output_scale * update, 0.0)


def exchange(pair, odd, groups, count):
    near = [(i, i ^ 1) for i in range(count) if i ^ 1 < count]
    odds = [(i, i + 1) for i in range(1, count - 1, 2)]
    far = [(g * count + a, g * count + b) for g in range(groups) for a, b in odds + [(b, a) for a, b in odds]]
    if groups % 2 == 0 and count % 2 == 0:
        far += [(g * count + i, (g ^ 1) * count + i) for g in range(groups) for i in (0, count - 1)]
    return lax.ppermute(pair, "row", near), lax.ppermute(odd, ("grp", "row"), far)


def kind_of(i):
    return (i ^ (i >> 1) ^ (i >> 2)) & 1


def gather_plan(count):
    bits = [1 << b for b in range(count.bit_length() - 1, 0, -1) if 1 << b < count]
    steps = [[b | 1, b | 1] for b in bits]
    if len(bits) > 1:
        high, low = bits[-2] | 1, bits[-1] | 1
        steps[-2:] = [[high, low], [low, high]]
    return steps + [[1, 1]]


def gather(norm, count, between):
    orders = [[0], [0]]
    for n, step in enumerate(gather_plan(count)):
        perm = [(i, i ^ step[kind_of(i)]) for i in range(count)]
        arrived = lax.ppermute(norm, "row", perm)
        if n < len(between):
            arrived, between[n] = lax.optimization_barrier((arrived, between[n](n, norm)))
        norm = jnp.concatenate([norm, arrived], axis=0)
        orders = [orders[p] + [x ^ step[p] for x in orders[kind_of(p ^ step[p])]] for p in range(2)]
    return norm, orders, between


def on_device(
    groups,
    count,
    positions,
    noise,
    atom_single,
    atom_token,
    atom_counts,
    window_offsets,
    atom_bias,
    token_single,
    token_bias,
    pair_mask,
    w_coord,
    w_atom_qkv,
    w_atom_out,
    w_agg,
    w_tok_qkv,
    w_tok_gate,
    w_tok_out,
    w_back,
    w_pos,
):
    rows, width = atom_single.shape
    block_rows, model = token_single.shape
    half = block_rows // 2
    info_shape = shape((8,), jnp.int32)
    info, start, q, keys, values, pair, odd = call(
        embed_body,
        [
            info_shape,
            shape((rows, width), F32),
            shape((rows, width), BF16),
            shape((rows + AHEAD, width), F32),
            shape((rows + AHEAD, width), F32),
            shape((AHEAD, 2 * width), BF16),
            shape((AHEAD, 2 * width), BF16),
        ],
        "embed",
        [HBM] * 6,
        [
            pltpu.SMEM(atom_counts.shape, jnp.int32),
            pltpu.VMEM(positions.shape, F32),
            pltpu.VMEM(noise.shape, F32),
            pltpu.VMEM(atom_single.shape, BF16),
            pltpu.VMEM(w_coord.shape, F32),
            pltpu.VMEM(w_atom_qkv.shape, BF16),
            pltpu.SemaphoreType.DMA((6,)),
        ],
        out_specs=[SMEM] + [VMEM] * 6,
    )(atom_counts, positions, noise, atom_single, w_coord, w_atom_qkv)
    pair, odd = exchange(pair, odd, groups, count)
    offsets, bias, wout, wagg, att = call(
        local_body,
        [
            shape(window_offsets.shape, jnp.int32),
            shape(atom_bias.shape, F32),
            shape(w_atom_out.shape, BF16),
            shape(w_agg.shape, BF16),
            shape((rows, width), BF16),
        ],
        "local",
        [HBM] + [VMEM] * 3 + [HBM] * 3,
        [pltpu.SemaphoreType.DMA((4,))],
        flops=10**9,
        out_specs=[SMEM] + [VMEM] * 4,
    )(window_offsets, q, keys, values, atom_bias, w_atom_out, w_agg)
    packed = model + 128
    mid, own, pair, odd, hot = call(
        functools.partial(atoms_body, half),
        [
            shape((rows, width), F32),
            shape((block_rows, packed), F32),
            shape((half, packed), BF16),
            shape((half, packed), BF16),
            shape((rows, block_rows + 2 * half), BF16),
        ],
        "atoms",
        [SMEM, SMEM] + [VMEM] * 11,
        [pltpu.VMEM((BEHIND + rows + AHEAD, width), F32)] * 2 + [pltpu.VMEM((rows, width), BF16)],
    )(info, offsets, atom_token[None], start, q, keys, values, pair, odd, att, bias, wout, wagg)
    pair, odd = exchange(pair, odd, groups, count)
    token_in, norm = call(
        token_body,
        [shape((block_rows, model), F32), shape((block_rows, model), BF16)],
        "token",
        [SMEM] + [VMEM] * 4,
    )(info, own, pair, odd, token_single)

    def query(n, seen):
        return call(
            query_body,
            [shape((TH * block_rows, model), BF16), shape((block_rows, model), F32)],
            "query",
            [VMEM, HBM, HBM],
            [pltpu.VMEM((model, model), BF16)] * 3 + [pltpu.SemaphoreType.DMA((3,))],
            flops=10**9,
            limit=10,
        )(norm, w_tok_qkv, w_tok_gate)

    def stage(n, seen):
        return call(
            stage_body,
            [
                shape(token_bias.shape, F32),
                shape((model, model), BF16),
                shape((model, model), BF16),
                shape(w_back.shape, BF16),
            ],
            "stage",
            [VMEM] + [HBM] * 5,
            [pltpu.VMEM(pair_mask.shape, jnp.int32), pltpu.SemaphoreType.DMA((5,))],
            flops=10**9,
        )(seen, token_bias, pair_mask, w_tok_qkv, w_tok_out, w_back)

    if count & (count - 1) or count < 8:
        everyone, orders = lax.all_gather(norm, "row", axis=0, tiled=True), None
        between = [query(0, norm), stage(1, norm)]
    else:
        everyone, orders, between = gather(norm, count, [query, stage])
    (query_rows, gate), (bias, wv, wout, wback) = between
    token_out, back, pair, odd = call(
        functools.partial(attend_body, orders, half),
        [
            shape((block_rows, model), BF16),
            shape((block_rows, width), BF16),
            shape((half, width), BF16),
            shape((half, width), BF16),
        ],
        "attend",
        [SMEM] + [VMEM] * 8,
        [pltpu.VMEM((count * block_rows, model), BF16)],
    )(info, token_in, query_rows, gate, everyone, bias, wv, wout, wback)
    pair, odd = exchange(pair, odd, groups, count)
    (denoised,) = call(
        final_body,
        [shape(positions.shape, F32)],
        "final",
        [SMEM] + [VMEM] * 8,
    )(info, hot, mid, back, pair, odd, w_pos, positions, noise)
    return (denoised, token_out)


def solution(mesh):
    placed = (
        P(None, ("grp", "row")),
        P(None, ("grp", "row")),
        P(("grp", "row"), None),
        P(("grp", "row")),
        P(("grp", "row")),
        P(("grp", "row")),
        P(None, ("grp", "row"), None),
        P(("grp", "row"), None),
        P(None, ("grp", "row"), None),
        P(("grp", "row"), None),
    ) + (P(),) * 9
    return jax.shard_map(
        functools.partial(on_device, mesh.shape["grp"], mesh.shape["row"]),
        mesh=mesh,
        in_specs=placed,
        out_specs=(P(None, ("grp", "row")), P(("grp", "row"), None)),
        check_vma=False,
    )
```

time: 60.7 us -> 51.7 us (0.85)
  starting transfers between devices: 10.4 us -> 3.46 us
  Pallas kernels: 13.7 us -> 17.2 us
  waiting for transfers between devices: 23.8 us -> 20.7 us
  local copies, waits for them, and re-layouts: 10.6 us -> 8.12 us
    ppermute x10, starting transfers between devices: 10.4 us -> 3.46 us  [the longest x3 2.6 us: exchange(): lax.ppermute(odd, ('grp', 'row'), far)]
    pallas_call x2 -> x4, Pallas kernels: 2.43 us -> 8.17 us  [the longest x1 3.87 us: on_device(): call(local_body, [shape(window_offsets.shape, jnp.int32), shape(atom_bias...]
    ppermute x10, waiting for transfers between devices: 23.8 us -> 20.7 us  [the longest x4 13.7 us: gather(): arrived = lax.ppermute(norm, 'row', perm)]
    unnamed x42 -> x41, local copies, waits for them, and re-layouts: 9.86 us -> 7.4 us
    pallas_call x1, Pallas kernels: 5.04 us -> 2.9 us  [on_device(): call(functools.partial(atoms_body, half), [shape((rows, width), F32), sha...]
  transfers between devices with their start and end apart: 10 -> 10, of which waited for: 6 -> 7; matrix products, arithmetic and copies ran while one was open for 1% -> 1% of each run, Pallas kernels for 2% -> 13%
where the time goes in v3:
time: 51.7 us; the launch traced here: 51.1 us
  waiting for transfers between devices  20.7 us (40%)
  Pallas kernels  17.2 us (33%)
  local copies, waits for them, and re-layouts  8.12 us (16%)
  starting transfers between devices  3.46 us (7%)
  between operations  1.54 us (3%)
    ppermute x4, waiting for transfers between devices, gather(): arrived = lax.ppermute(norm, 'row', perm)  13.7 us
    unnamed x41, local copies, waits for them, and re-layouts  7.4 us
    ppermute x3, waiting for transfers between devices, exchange(): lax.ppermute(odd, ('grp', 'row'), far)  6 us
    pallas_call x1, Pallas kernels, on_device(): call(local_body, [shape(window_offsets.shape, jnp.int32), shape(atom_bias...  3.87 us
    pallas_call x1, Pallas kernels, on_device(): call(functools.partial(attend_body, orders, half), [shape((block_rows, mo...  3.67 us
    pallas_call x1, Pallas kernels, on_device(): call(functools.partial(atoms_body, half), [shape((rows, width), F32), sha...  2.9 us
    ppermute x3, starting transfers between devices, exchange(): lax.ppermute(odd, ('grp', 'row'), far)  2.6 us
    pallas_call x1, Pallas kernels, query(): call(query_body, [shape((TH * block_rows, model), BF16), shape((block_row...  1.75 us
  transfers between devices with their start and end apart: 10, of which 7 were waited for; matrix products, arithmetic and copies ran while one was open for 1% of the time, Pallas kernels for 13%

profile of v3, /device:TPU:24, one launch (start us, length us, event | category | flops | bytes accessed | tf_op | source)
XLA Modules:
  0.0 51.1 jit_solution(3933912021744908170)
XLA Ops:
  1.3 0.9 %copy-done.5 = bf16[384,128]{1,0:T(8,128)(2,1)S(1)} copy-done((bf16[384,128]{1,0:T(8,128)(2,1)S(1)}, bf16[384,128]{1,0:T(8,128)(2,1)}, u32[]{:S(2)}) %copy-start.5) | copy-done | bytes 98328
  2.2 0.9 %copy-done.6 = bf16[128,384]{1,0:T(8,128)(2,1)S(1)} copy-done((bf16[128,384]{1,0:T(8,128)(2,1)S(1)}, bf16[128,384]{1,0:T(8,128)(2,1)}, u32[]{:S(2)}) %copy-start.6) | copy-done | bytes 98328
  3.1 0.7 %copy-done.9 = f32[3,384]{1,0:T(4,128)S(1)} copy-done((f32[3,384]{1,0:T(4,128)S(1)}, f32[3,384]{1,0:T(4,128)}, u32[]{:S(2)}) %copy-start.9) | copy-done | bytes 4632
  3.8 0.7 %copy-done.11 = f32[3,384]{1,0:T(4,128)S(1)} copy-done((f32[3,384]{1,0:T(4,128)S(1)}, f32[3,384]{1,0:T(4,128)}, u32[]{:S(2)}) %copy-start.11) | copy-done | bytes 4632
  5.1 1.7 %embed.1 = (s32[8]{0:T(128)S(1)}, f32[384,128]{1,0:T(8,128)S(1)}, bf16[384,128]{1,0:T(8,128)(2,1)S(1)}, f32[480,128]{1,0:T(8,128)S(1)}, f32[480,128]{1,0:T(8,128...) custom-call(s32[1]{0:T(128)S(6)} %copy.26.counts_hbm, f32[3,384]{1,0:T(4,128)S(1)} %copy-done.9, ...), custom_call_target="tpu_custom_call" | custom-call | flops 10000000 | bytes 884768 | tf_op jit(solution)/shard_map/embed/pallas_call | solution.py:479
  6.9 1.5 %collective-permute-start.1 = (bf16[96,256]{1,0:T(8,128)(2,1)S(1)}, bf16[96,256]{1,0:T(8,128)(2,1)S(1)}, u32[]{:S(2)}, u32[]{:S(2)}) collective-permute-start(bf16[96,256]{1,0:T(8,128)(2,1)S(1)} %get-tuple-element.46), channel_id=1, source_target_pairs={{1,2},{3,4},{5,6},{7,8},{9,10},{11,12},{13,14},{2,1},{4,3},{6,5},{... | collective-permute-start | bytes 147464 | tf_op jit(solution)/shard_map/ppermute | solution.py:424
  9.1 1.1 %copy-done.15 = f32[4,384,128]{2,1,0:T(8,128)S(1)} copy-done((f32[4,384,128]{2,1,0:T(8,128)S(1)}, f32[4,384,128]{2,1,0:T(8,128)}, u32[]{:S(2)}) %copy-start.15) | copy-done | bytes 786456
  10.2 0.9 %copy-done.16 = bf16[128,768]{1,0:T(8,128)(2,1)S(1)} copy-done((bf16[128,768]{1,0:T(8,128)(2,1)S(1)}, bf16[128,768]{1,0:T(8,128)(2,1)}, u32[]{:S(2)}) %copy-start.16) | copy-done | bytes 196632
  11.1 0.8 %copy-done.17 = bf16[128,128]{1,0:T(8,128)(2,1)S(1)} copy-done((bf16[128,128]{1,0:T(8,128)(2,1)S(1)}, bf16[128,128]{1,0:T(8,128)(2,1)}, u32[]{:S(2)}) %copy-start.17) | copy-done | bytes 32792
  12.6 3.9 %local.1 = (s32[12]{0:T(128)S(1)}, f32[4,384,128]{2,1,0:T(8,128)S(1)}, bf16[128,128]{1,0:T(8,128)(2,1)S(1)}, bf16[128,768]{1,0:T(8,128)(2,1)S(1)}, bf16[384,128]{1,0:T(8,128)(2,1)S(1)}) custom-call(s32[12]{0:T(128)S(1)} %copy-done.18, bf16[384,128]{1,0:T(8,128)(2,1)S(1)} %get-tuple-element.40.q_ref, f32[480,128]{1,0:T(8,128)S(1)} %get-tuple-element.41.k_ref, ...), custom_call_target="tpu_custom_call" | custom-call | flops 1000000000 | bytes 1114160 | tf_op jit(solution)/shard_map/local/pallas_call | solution.py:504
  16.5 2.9 %atoms.1 = (f32[384,128]{1,0:T(8,128)S(1)}, f32[32,896]{1,0:T(8,128)S(1)}, bf16[16,896]{1,0:T(8,128)(2,1)S(1)}, bf16[16,896]{1,0:T(8,128)(2,1)S(1)}, bf16[384,64]{1,0:T(8,128)(2,1)S(1)}) custom-call(s32[8]{0:T(128)S(1)} %get-tuple-element.39.info, s32[12]{0:T(128)S(1)} %get-tuple-element.43.offsets, s32[1,384]{1,0:T(1,128)S(1)} %broadcast_in_dim.3.token_ref, ...), custom_call_target="tpu_custom_call" | custom-call | flops 10000000 | bytes 417792 | tf_op jit(solution)/shard_map/atoms/pallas_call | solution.py:520
  19.6 1.1 %collective-permute-start.3 = (bf16[16,896]{1,0:T(8,128)(2,1)S(1)}, bf16[16,896]{1,0:T(8,128)(2,1)S(1)}, u32[]{:S(2)}, u32[]{:S(2)}) collective-permute-start(bf16[16,896]{1,0:T(8,128)(2,1)S(1)} %get-tuple-element.55), channel_id=1, source_target_pairs={{1,2},{3,4},{5,6},{7,8},{9,10},{11,12},{13,14},{2,1},{4,3},{6,5},{... | collective-permute-start | bytes 86024 | tf_op jit(solution)/shard_map/ppermute | solution.py:424
  20.7 3.1 %collective-permute-done.3.odd_ref = bf16[16,896]{1,0:T(8,128)(2,1)S(1)} collective-permute-done((bf16[16,896]{1,0:T(8,128)(2,1)S(1)}, bf16[16,896]{1,0:T(8,128)(2,1)S(1)}, u32[]{:S(2)}, u32[]{:S(2)}) %collective-permute-start.3) | collective-permute-done | bytes 28704 | tf_op jit(solution)/shard_map/ppermute | solution.py:424
  23.8 0.9 %token_.1 = (f32[32,768]{1,0:T(8,128)S(1)}, bf16[32,768]{1,0:T(8,128)(2,1)S(1)}) custom-call(s32[8]{0:T(128)S(1)} %get-tuple-element.39.info, f32[32,896]{1,0:T(8,128)S(1)} %get-tuple-element.53.own_ref, bf16[16,896]{1,0:T(8,128)(2,1)S(1)} %collective-permute-done.2.pair_ref, bf16[16,896]{1,0:T(8,128)(2,1)S(1)} %collective-permute-done.3.odd_ref, ...), custom_call_target="tpu_custom_call" | custom-call | flops 10000000 | bytes 147456 | tf_op jit(solution)/shard_map/token/pallas_call | solution.py:534
  24.9 1.8 %query.1 = (bf16[512,768]{1,0:T(8,128)(2,1)S(1)}, f32[32,768]{1,0:T(8,128)S(1)}) custom-call(bf16[32,768]{1,0:T(8,128)(2,1)S(1)} %get-tuple-element.57.norm_ref, bf16[768,2304]{1,0:T(8,128)(2,1)S(1)} %copy-done, bf16[768,768]{1,0:T(8,128)(2,1)S(1)} %copy-done.1), custom_call_target="tpu_custom_call" | custom-call | flops 1000000000 | bytes 884736 | tf_op jit(solution)/shard_map/query/pallas_call | solution.py:542
  26.6 3.9 %collective-permute-done.4 = bf16[32,768]{1,0:T(8,128)(2,1)S(1)} collective-permute-done((bf16[32,768]{1,0:T(8,128)(2,1)S(1)}, bf16[32,768]{1,0:T(8,128)(2,1)S(1)}, u32[]{:S(2)}, u32[]{:S(2)}) %collective-permute-start.4) | collective-permute-done | bytes 49184 | tf_op jit(solution)/shard_map/ppermute | solution.py:444
  30.7 0.9 %stage.1 = (f32[16,32,512]{2,1,0:T(8,128)S(1)}, bf16[768,768]{1,0:T(8,128)(2,1)S(1)}, bf16[768,768]{1,0:T(8,128)(2,1)S(1)}, bf16[768,128]{1,0:T(8,128)(2,1)S(1)}) custom-call(bf16[64,768]{1,0:T(8,128)(2,1)S(1)} %get-tuple-element.76.after, f32[16,32,512]{2,1,0:T(8,128)S(1)} %copy-done.3, s32[32,512]{1,0:T(8,128)S(1)} %copy-done.7, ...), custom_call_target="tpu_custom_call" | custom-call | flops 1000000000 | bytes 3604480 | tf_op jit(solution)/shard_map/stage/pallas_call | solution.py:553
  31.6 3.1 %collective-permute-done.5 = bf16[64,768]{1,0:T(8,128)(2,1)S(1)} collective-permute-done((bf16[64,768]{1,0:T(8,128)(2,1)S(1)}, bf16[64,768]{1,0:T(8,128)(2,1)S(1)}, u32[]{:S(2)}, u32[]{:S(2)}) %collective-permute-start.5) | collective-permute-done | bytes 98336 | tf_op jit(solution)/shard_map/ppermute | solution.py:444
  34.8 5.1 %collective-permute-done.6 = bf16[128,768]{1,0:T(8,128)(2,1)S(1)} collective-permute-done((bf16[128,768]{1,0:T(8,128)(2,1)S(1)}, bf16[128,768]{1,0:T(8,128)(2,1)S(1)}, u32[]{:S(2)}, u32[]{:S(2)}) %collective-permute-start.6) | collective-permute-done | bytes 196640 | tf_op jit(solution)/shard_map/ppermute | solution.py:444
  40.1 1.6 %collective-permute-done.7 = bf16[256,768]{1,0:T(8,128)(2,1)S(1)} collective-permute-done((bf16[256,768]{1,0:T(8,128)(2,1)S(1)}, bf16[256,768]{1,0:T(8,128)(2,1)S(1)}, u32[]{:S(2)}, u32[]{:S(2)}) %collective-permute-start.7) | collective-permute-done | bytes 393248 | tf_op jit(solution)/shard_map/ppermute | solution.py:444
  41.7 3.7 %attend.1 = (bf16[32,768]{1,0:T(8,128)(2,1)}, bf16[32,128]{1,0:T(8,128)(2,1)S(1)}, bf16[16,128]{1,0:T(8,128)(2,1)S(1)}, bf16[16,128]{1,0:T(8,128)(2,1)S(1)}) custom-call(s32[8]{0:T(128)S(1)} %get-tuple-element.39.info, f32[32,768]{1,0:T(8,128)S(1)} %get-tuple-element.56.in_ref, bf16[512,768]{1,0:T(8,128)(2,1)S(1)} %get-tuple-element.60.query_ref, ...), custom_call_target="tpu_custom_call" | custom-call | flops 10000000 | bytes 65536 | tf_op jit(solution)/shard_map/attend/pallas_call | solution.py:573
  45.6 1.0 %collective-permute-done.8.pair_ref = bf16[16,128]{1,0:T(8,128)(2,1)S(1)} collective-permute-done((bf16[16,128]{1,0:T(8,128)(2,1)S(1)}, bf16[16,128]{1,0:T(8,128)(2,1)S(1)}, u32[]{:S(2)}, u32[]{:S(2)}) %collective-permute-start.8) | collective-permute-done | bytes 4128 | tf_op jit(solution)/shard_map/ppermute | solution.py:424
  46.6 2.9 %collective-permute-done.9.odd_ref = bf16[16,128]{1,0:T(8,128)(2,1)S(1)} collective-permute-done((bf16[16,128]{1,0:T(8,128)(2,1)S(1)}, bf16[16,128]{1,0:T(8,128)(2,1)S(1)}, u32[]{:S(2)}, u32[]{:S(2)}) %collective-permute-start.9) | collective-permute-done | bytes 4128 | tf_op jit(solution)/shard_map/ppermute | solution.py:424
  49.5 1.6 %final.1 = f32[3,384]{1,0:T(4,128)} custom-call(s32[8]{0:T(128)S(1)} %get-tuple-element.39.info, bf16[384,64]{1,0:T(8,128)(2,1)S(1)} %get-tuple-element.51.hot_ref, f32[384,128]{1,0:T(8,128)S(1)} %get-tuple-element.52.mid_ref, bf16[32,128]{1,0:T(8,128)(2,1)S(1)} %get-tuple-element.72.back_ref, bf16[16,128]{1,0:T(8,128)(2,1)S(1)} %collective-permute-done.8.pair_ref, ...), custom_call_target="tpu_custom_call" | custom-call | flops 10000000 | bytes 4608 | tf_op jit(solution)/shard_map/final/pallas_call | solution.py:586
  (50 shorter events, 3.1 us)
Async XLA Ops:
  1.3 0.9 %copy-start.5 = (bf16[384,128]{1,0:T(8,128)(2,1)S(1)}, bf16[384,128]{1,0:T(8,128)(2,1)}, u32[]{:S(2)}) copy-start(bf16[384,128]{1,0:T(8,128)(2,1)} %single_hbm.1) | copy-start | bytes 294916
  2.2 0.9 %copy-start.6 = (bf16[128,384]{1,0:T(8,128)(2,1)S(1)}, bf16[128,384]{1,0:T(8,128)(2,1)}, u32[]{:S(2)}) copy-start(bf16[128,384]{1,0:T(8,128)(2,1)} %wqkv_hbm.3) | copy-start | bytes 294916
  6.8 9.6 %collective-permute-start = (bf16[96,256]{1,0:T(8,128)(2,1)S(1)}, bf16[96,256]{1,0:T(8,128)(2,1)S(1)}, u32[]{:S(2)}, u32[]{:S(2)}) collective-permute-start(bf16[96,256]{1,0:T(8,128)(2,1)S(1)} %get-tuple-element.45), channel_id=1, source_target_pairs={{0,1},{1,0},{2,3},{3,2},{4,5},{5,4},{6,7},{7,6},{8,9},{9,8},{10,11... | collective-permute-start | bytes 147464 | tf_op jit(solution)/shard_map/ppermute | solution.py:424
  6.9 9.6 %collective-permute-start.1 = (bf16[96,256]{1,0:T(8,128)(2,1)S(1)}, bf16[96,256]{1,0:T(8,128)(2,1)S(1)}, u32[]{:S(2)}, u32[]{:S(2)}) collective-permute-start(bf16[96,256]{1,0:T(8,128)(2,1)S(1)} %get-tuple-element.46), channel_id=1, source_target_pairs={{1,2},{3,4},{5,6},{7,8},{9,10},{11,12},{13,14},{2,1},{4,3},{6,5},{... | collective-permute-start | bytes 147464 | tf_op jit(solution)/shard_map/ppermute | solution.py:424
  9.1 1.1 %copy-start.15 = (f32[4,384,128]{2,1,0:T(8,128)S(1)}, f32[4,384,128]{2,1,0:T(8,128)}, u32[]{:S(2)}) copy-start(f32[4,384,128]{2,1,0:T(8,128)} %bias_hbm.2) | copy-start | bytes 2359300
  10.2 0.9 %copy-start.16 = (bf16[128,768]{1,0:T(8,128)(2,1)S(1)}, bf16[128,768]{1,0:T(8,128)(2,1)}, u32[]{:S(2)}) copy-start(bf16[128,768]{1,0:T(8,128)(2,1)} %wagg_hbm.1) | copy-start | bytes 589828
  12.6 12.3 %copy-start = (bf16[768,2304]{1,0:T(8,128)(2,1)S(1)}, bf16[768,2304]{1,0:T(8,128)(2,1)}, u32[]{:S(2)}) copy-start(bf16[768,2304]{1,0:T(8,128)(2,1)} %wqkv_hbm.5) | copy-start | bytes 10616836
  16.4 7.4 %copy-start.8 = (bf16[32,768]{1,0:T(8,128)(2,1)S(1)}, bf16[32,768]{1,0:T(8,128)(2,1)}, u32[]{:S(2)}) copy-start(bf16[32,768]{1,0:T(8,128)(2,1)} %single_ref.1) | copy-start | bytes 147460
  16.5 8.4 %copy-start.1 = (bf16[768,768]{1,0:T(8,128)(2,1)S(1)}, bf16[768,768]{1,0:T(8,128)(2,1)}, u32[]{:S(2)}) copy-start(bf16[768,768]{1,0:T(8,128)(2,1)} %wgate_hbm.1) | copy-start | bytes 3538948
  19.4 1.4 %collective-permute-start.2 = (bf16[16,896]{1,0:T(8,128)(2,1)S(1)}, bf16[16,896]{1,0:T(8,128)(2,1)S(1)}, u32[]{:S(2)}, u32[]{:S(2)}) collective-permute-start(bf16[16,896]{1,0:T(8,128)(2,1)S(1)} %get-tuple-element.54), channel_id=1, source_target_pairs={{0,1},{1,0},{2,3},{3,2},{4,5},{5,4},{6,7},{7,6},{8,9},{9,8},{10,11... | collective-permute-start | bytes 86024 | tf_op jit(solution)/shard_map/ppermute | solution.py:424
  19.6 4.2 %collective-permute-start.3 = (bf16[16,896]{1,0:T(8,128)(2,1)S(1)}, bf16[16,896]{1,0:T(8,128)(2,1)S(1)}, u32[]{:S(2)}, u32[]{:S(2)}) collective-permute-start(bf16[16,896]{1,0:T(8,128)(2,1)S(1)} %get-tuple-element.55), channel_id=1, source_target_pairs={{1,2},{3,4},{5,6},{7,8},{9,10},{11,12},{13,14},{2,1},{4,3},{6,5},{... | collective-permute-start | bytes 86024 | tf_op jit(solution)/shard_map/ppermute | solution.py:424
  24.7 5.8 %collective-permute-start.4 = (bf16[32,768]{1,0:T(8,128)(2,1)S(1)}, bf16[32,768]{1,0:T(8,128)(2,1)S(1)}, u32[]{:S(2)}, u32[]{:S(2)}) collective-permute-start(bf16[32,768]{1,0:T(8,128)(2,1)S(1)} %get-tuple-element.57.norm_ref), channel_id=1, source_target_pairs={{0,9},{1,8},{2,11},{3,10},{4,13},{5,12},{6,15},{7,14},{8,1},{9,0},... | collective-permute-start | bytes 147464 | tf_op jit(solution)/shard_map/ppermute | solution.py:444
  24.8 5.8 %copy-start.2 = (bf16[768,768]{1,0:T(8,128)(2,1)S(1)}, bf16[768,768]{1,0:T(8,128)(2,1)}, u32[]{:S(2)}) copy-start(bf16[768,768]{1,0:T(8,128)(2,1)} %wout_hbm.3) | copy-start | bytes 3538948
  24.8 5.8 %copy-start.3 = (f32[16,32,512]{2,1,0:T(8,128)S(1)}, f32[16,32,512]{2,1,0:T(8,128)}, u32[]{:S(2)}) copy-start(f32[16,32,512]{2,1,0:T(8,128)} %bias_hbm.3) | copy-start | bytes 3145732
  24.9 5.8 %copy-start.4 = (bf16[768,128]{1,0:T(8,128)(2,1)S(1)}, bf16[768,128]{1,0:T(8,128)(2,1)}, u32[]{:S(2)}) copy-start(bf16[768,128]{1,0:T(8,128)(2,1)} %wback_hbm.1) | copy-start | bytes 589828
  24.9 5.8 %copy-start.7 = (s32[32,512]{1,0:T(8,128)S(1)}, s32[32,512]{1,0:T(8,128)}, u32[]{:S(2)}) copy-start(s32[32,512]{1,0:T(8,128)} %mask_hbm.1) | copy-start | bytes 196612
  30.6 4.1 %collective-permute-start.5 = (bf16[64,768]{1,0:T(8,128)(2,1)S(1)}, bf16[64,768]{1,0:T(8,128)(2,1)S(1)}, u32[]{:S(2)}, u32[]{:S(2)}) collective-permute-start(bf16[64,768]{1,0:T(8,128)(2,1)S(1)} %get-tuple-element.76.after), channel_id=1, source_target_pairs={{0,5},{1,2},{2,1},{3,6},{4,7},{5,0},{6,3},{7,4},{8,13},{9,10},{10,... | collective-permute-start | bytes 294920 | tf_op jit(solution)/shard_map/ppermute | solution.py:444
  34.7 5.2 %collective-permute-start.6 = (bf16[128,768]{1,0:T(8,128)(2,1)S(1)}, bf16[128,768]{1,0:T(8,128)(2,1)S(1)}, u32[]{:S(2)}, u32[]{:S(2)}) collective-permute-start(bf16[128,768]{1,0:T(8,128)(2,1)S(1)} %pad_maximum_fusion.1), channel_id=1, source_target_pairs={{0,3},{1,4},{2,7},{3,0},{4,1},{5,6},{6,5},{7,2},{8,11},{9,12},{10,... | collective-permute-start | bytes 589832 | tf_op jit(solution)/shard_map/ppermute | solution.py:444
  39.9 1.8 %collective-permute-start.7 = (bf16[256,768]{1,0:T(8,128)(2,1)S(1)}, bf16[256,768]{1,0:T(8,128)(2,1)S(1)}, u32[]{:S(2)}, u32[]{:S(2)}) collective-permute-start(bf16[256,768]{1,0:T(8,128)(2,1)S(1)} %pad_maximum_fusion), channel_id=1, source_target_pairs={{0,1},{1,0},{2,3},{3,2},{4,5},{5,4},{6,7},{7,6},{8,9},{9,8},{10,11... | collective-permute-start | bytes 1179656 | tf_op jit(solution)/shard_map/ppermute | solution.py:444
  41.7 7.8 %copy-start.10 = (f32[3,384]{1,0:T(4,128)S(1)}, f32[3,384]{1,0:T(4,128)}, u32[]{:S(2)}) copy-start(f32[3,384]{1,0:T(4,128)} %pos_ref.1) | copy-start | bytes 13828
  41.7 7.8 %copy-start.12 = (f32[3,384]{1,0:T(4,128)S(1)}, f32[3,384]{1,0:T(4,128)}, u32[]{:S(2)}) copy-start(f32[3,384]{1,0:T(4,128)} %noise_ref.1) | copy-start | bytes 13828
  41.7 7.8 %copy-start.14 = (bf16[3,128]{1,0:T(4,128)(2,1)S(1)}, bf16[3,128]{1,0:T(4,128)(2,1)}, u32[]{:S(2)}) copy-start(bf16[3,128]{1,0:T(4,128)(2,1)} %wpos_ref.1) | copy-start | bytes 2308
  45.4 1.2 %collective-permute-start.8 = (bf16[16,128]{1,0:T(8,128)(2,1)S(1)}, bf16[16,128]{1,0:T(8,128)(2,1)S(1)}, u32[]{:S(2)}, u32[]{:S(2)}) collective-permute-start(bf16[16,128]{1,0:T(8,128)(2,1)S(1)} %get-tuple-element.73), channel_id=1, source_target_pairs={{0,1},{1,0},{2,3},{3,2},{4,5},{5,4},{6,7},{7,6},{8,9},{9,8},{10,11... | collective-permute-start | bytes 12296 | tf_op jit(solution)/shard_map/ppermute | solution.py:424
  45.6 3.9 %collective-permute-start.9 = (bf16[16,128]{1,0:T(8,128)(2,1)S(1)}, bf16[16,128]{1,0:T(8,128)(2,1)S(1)}, u32[]{:S(2)}, u32[]{:S(2)}) collective-permute-start(bf16[16,128]{1,0:T(8,128)(2,1)S(1)} %get-tuple-element.74), channel_id=1, source_target_pairs={{1,2},{3,4},{5,6},{7,8},{9,10},{11,12},{13,14},{2,1},{4,3},{6,5},{... | collective-permute-start | bytes 12296 | tf_op jit(solution)/shard_map/ppermute | solution.py:424
  (5 other events, 3.5 us)

commit v4 on v3

--- a/solution.py
+++ b/solution.py
@@ -50,7 +50,8 @@
 
 def call(body, outs, name, specs, scratch=(), flops=10**7, limit=8, out_specs=None):
     moved = sum(o.size * o.dtype.itemsize for o in outs)
-    return pl.pallas_call(
+    held = [spec is HBM for spec in specs]
+    run = pl.pallas_call(
         body,
         out_shape=tuple(outs),
         in_specs=specs,
@@ -60,6 +61,7 @@
         cost_estimate=pl.CostEstimate(flops=flops, bytes_accessed=moved, transcendentals=0),
         compiler_params=pltpu.CompilerParams(vmem_limit_bytes=limit * 2**20),
     )
+    return lambda *args: run(*[pltpu.with_memory_space_constraint(x, pltpu.HBM) if h and x.ndim > 1 else x for x, h in zip(args, held)])
 
 
 def shape(dims, dtype):

time: 51.7 us -> 46.5 us (0.90)
  local copies, waits for them, and re-layouts: 8.12 us -> 1.43 us
  Pallas kernels: 17.2 us -> 20.4 us
  waiting for transfers between devices: 20.7 us -> 18.8 us
    unnamed x41 -> x13, local copies, waits for them, and re-layouts: 7.4 us -> 0.71 us
    pallas_call x8, Pallas kernels: 17.2 us -> 20.4 us  [call(): run(*[pltpu.with_memory_space_constraint(x, pltpu.HBM) if h and x.ndim >...]
    ppermute x4, waiting for transfers between devices: 13.7 us -> 11.7 us  [gather(): arrived = lax.ppermute(norm, 'row', perm)]
  transfers between devices with their start and end apart: 10 -> 10, of which waited for: 7 -> 7; matrix products, arithmetic and copies ran while one was open for 1% -> 2% of each run, Pallas kernels for 13% -> 20%
where the time goes in v4:
time: 46.5 us; the launch traced here: 45.6 us
  Pallas kernels  20.4 us (44%)
  waiting for transfers between devices  18.8 us (40%)
  starting transfers between devices  3.46 us (7%)
  between operations  1.44 us (3%)
  local copies, waits for them, and re-layouts  1.43 us (3%)
    pallas_call x8, Pallas kernels, call(): run(*[pltpu.with_memory_space_constraint(x, pltpu.HBM) if h and x.ndim >...  20.4 us
    ppermute x4, waiting for transfers between devices, gather(): arrived = lax.ppermute(norm, 'row', perm)  11.7 us
    ppermute x3, waiting for transfers between devices, exchange(): lax.ppermute(odd, ('grp', 'row'), far)  6 us
    ppermute x3, starting transfers between devices, exchange(): lax.ppermute(odd, ('grp', 'row'), far)  2.59 us
    ppermute x3, waiting for transfers between devices, exchange(): lax.ppermute(pair, 'row', near)  1.04 us
  transfers between devices with their start and end apart: 10, of which 7 were waited for; matrix products, arithmetic and copies ran while one was open for 2% of the time, Pallas kernels for 20%

profile of v4, /device:TPU:24, one launch (start us, length us, event | category | flops | bytes accessed | tf_op | source)
XLA Modules:
  0.0 45.6 jit_solution(2036328351360771024)
XLA Ops:
  1.3 2.2 %embed.1 = (s32[8]{0:T(128)S(1)}, f32[384,128]{1,0:T(8,128)S(1)}, bf16[384,128]{1,0:T(8,128)(2,1)S(1)}, f32[480,128]{1,0:T(8,128)S(1)}, f32[480,128]{1,0:T(8,128...) custom-call(s32[1]{0:T(128)S(6)} %copy.26.counts_hbm, f32[3,384]{1,0:T(4,128)} %pos_ref.1, ...), custom_call_target="tpu_custom_call" | custom-call | flops 10000000 | bytes 884768 | tf_op jit(solution)/shard_map/embed/pallas_call | solution.py:64
  3.5 0.1 collective-permute-start
  3.6 1.5 %collective-permute-start.1 = (bf16[96,256]{1,0:T(8,128)(2,1)S(1)}, bf16[96,256]{1,0:T(8,128)(2,1)S(1)}, u32[]{:S(2)}, u32[]{:S(2)}) collective-permute-start(bf16[96,256]{1,0:T(8,128)(2,1)S(1)} %get-tuple-element.46), channel_id=1, source_target_pairs={{1,2},{3,4},{5,6},{7,8},{9,10},{11,12},{13,14},{2,1},{4,3},{6,5},{... | collective-permute-start | bytes 147464 | tf_op jit(solution)/shard_map/ppermute | solution.py:426
  5.1 0.7 %broadcast_in_dim.3.token_ref = s32[1,384]{1,0:T(1,128)S(1)} reshape(s32[384]{0:T(512)} %param.22) | data formatting | bytes 3072 | tf_op jit(solution)/shard_map/broadcast_in_dim | solution.py:534
  5.8 0.7 %copy-done.4 = s32[12]{0:T(128)S(1)} copy-done((s32[12]{0:T(128)S(1)}, s32[12]{0:T(128)}, u32[]{:S(2)}) %copy-start.4) | copy-done | bytes 72
  6.4 4.5 %local.1 = (s32[12]{0:T(128)S(1)}, f32[4,384,128]{2,1,0:T(8,128)S(1)}, bf16[128,128]{1,0:T(8,128)(2,1)S(1)}, bf16[128,768]{1,0:T(8,128)(2,1)S(1)}, bf16[384,128]{1,0:T(8,128)(2,1)S(1)}) custom-call(s32[12]{0:T(128)S(1)} %copy-done.4, bf16[384,128]{1,0:T(8,128)(2,1)S(1)} %get-tuple-element.40.q_ref, f32[480,128]{1,0:T(8,128)S(1)} %get-tuple-element.41.k_ref, ...), custom_call_target="tpu_custom_call" | custom-call | flops 1000000000 | bytes 1114160 | tf_op jit(solution)/shard_map/local/pallas_call | solution.py:64
  10.9 2.9 %atoms.1 = (f32[384,128]{1,0:T(8,128)S(1)}, f32[32,896]{1,0:T(8,128)S(1)}, bf16[16,896]{1,0:T(8,128)(2,1)S(1)}, bf16[16,896]{1,0:T(8,128)(2,1)S(1)}, bf16[384,64]{1,0:T(8,128)(2,1)S(1)}) custom-call(s32[8]{0:T(128)S(1)} %get-tuple-element.39.info, s32[12]{0:T(128)S(1)} %get-tuple-element.43.offsets, s32[1,384]{1,0:T(1,128)S(1)} %broadcast_in_dim.3.token_ref, ...), custom_call_target="tpu_custom_call" | custom-call | flops 10000000 | bytes 417792 | tf_op jit(solution)/shard_map/atoms/pallas_call | solution.py:64
  13.8 0.3 collective-permute-start.2
  14.1 1.1 %collective-permute-start.3 = (bf16[16,896]{1,0:T(8,128)(2,1)S(1)}, bf16[16,896]{1,0:T(8,128)(2,1)S(1)}, u32[]{:S(2)}, u32[]{:S(2)}) collective-permute-start(bf16[16,896]{1,0:T(8,128)(2,1)S(1)} %get-tuple-element.55), channel_id=1, source_target_pairs={{1,2},{3,4},{5,6},{7,8},{9,10},{11,12},{13,14},{2,1},{4,3},{6,5},{... | collective-permute-start | bytes 86024 | tf_op jit(solution)/shard_map/ppermute | solution.py:426
  15.2 3.1 %collective-permute-done.3.odd_ref = bf16[16,896]{1,0:T(8,128)(2,1)S(1)} collective-permute-done((bf16[16,896]{1,0:T(8,128)(2,1)S(1)}, bf16[16,896]{1,0:T(8,128)(2,1)S(1)}, u32[]{:S(2)}, u32[]{:S(2)}) %collective-permute-start.3) | collective-permute-done | bytes 28704 | tf_op jit(solution)/shard_map/ppermute | solution.py:426
  18.3 0.9 %token_.1 = (f32[32,768]{1,0:T(8,128)S(1)}, bf16[32,768]{1,0:T(8,128)(2,1)S(1)}) custom-call(s32[8]{0:T(128)S(1)} %get-tuple-element.39.info, f32[32,896]{1,0:T(8,128)S(1)} %get-tuple-element.53.own_ref, bf16[16,896]{1,0:T(8,128)(2,1)S(1)} %collective-permute-done.2.pair_ref, bf16[16,896]{1,0:T(8,128)(2,1)S(1)} %collective-permute-done.3.odd_ref, ...), custom_call_target="tpu_custom_call" | custom-call | flops 10000000 | bytes 147456 | tf_op jit(solution)/shard_map/token/pallas_call | solution.py:64
  19.3 2.6 %query.1 = (bf16[512,768]{1,0:T(8,128)(2,1)S(1)}, f32[32,768]{1,0:T(8,128)S(1)}) custom-call(bf16[32,768]{1,0:T(8,128)(2,1)S(1)} %get-tuple-element.57.norm_ref, bf16[768,2304]{1,0:T(8,128)(2,1)} %wqkv_hbm.5, bf16[768,768]{1,0:T(8,128)(2,1)} %wgate_hbm.1), custom_call_target="tpu_custom_call" | custom-call | flops 1000000000 | bytes 884736 | tf_op jit(solution)/shard_map/query/pallas_call | solution.py:64
  21.9 3.1 %collective-permute-done.4 = bf16[32,768]{1,0:T(8,128)(2,1)S(1)} collective-permute-done((bf16[32,768]{1,0:T(8,128)(2,1)S(1)}, bf16[32,768]{1,0:T(8,128)(2,1)S(1)}, u32[]{:S(2)}, u32[]{:S(2)}) %collective-permute-start.4) | collective-permute-done | bytes 49184 | tf_op jit(solution)/shard_map/ppermute | solution.py:446
  25.0 0.1 collective-permute-start.5
  25.1 2.0 %stage.1 = (f32[16,32,512]{2,1,0:T(8,128)S(1)}, bf16[768,768]{1,0:T(8,128)(2,1)S(1)}, bf16[768,768]{1,0:T(8,128)(2,1)S(1)}, bf16[768,128]{1,0:T(8,128)(2,1)S(1)}) custom-call(bf16[64,768]{1,0:T(8,128)(2,1)S(1)} %get-tuple-element.76.after, f32[16,32,512]{2,1,0:T(8,128)} %bias_hbm.3, s32[32,512]{1,0:T(8,128)} %mask_hbm.1, bf16[768,2304]{1,0:T(8,128)(2,1)} %wqkv_hbm.5, ...), custom_call_target="tpu_custom_call" | custom-call | flops 1000000000 | bytes 3604480 | tf_op jit(solution)/shard_map/stage/pallas_call | solution.py:64
  27.1 2.0 %collective-permute-done.5 = bf16[64,768]{1,0:T(8,128)(2,1)S(1)} collective-permute-done((bf16[64,768]{1,0:T(8,128)(2,1)S(1)}, bf16[64,768]{1,0:T(8,128)(2,1)S(1)}, u32[]{:S(2)}, u32[]{:S(2)}) %collective-permute-start.5) | collective-permute-done | bytes 98336 | tf_op jit(solution)/shard_map/ppermute | solution.py:446
  29.2 5.1 %collective-permute-done.6 = bf16[128,768]{1,0:T(8,128)(2,1)S(1)} collective-permute-done((bf16[128,768]{1,0:T(8,128)(2,1)S(1)}, bf16[128,768]{1,0:T(8,128)(2,1)S(1)}, u32[]{:S(2)}, u32[]{:S(2)}) %collective-permute-start.6) | collective-permute-done | bytes 196640 | tf_op jit(solution)/shard_map/ppermute | solution.py:446
  34.3 0.2 collective-permute-start.7
  34.5 1.6 %collective-permute-done.7 = bf16[256,768]{1,0:T(8,128)(2,1)S(1)} collective-permute-done((bf16[256,768]{1,0:T(8,128)(2,1)S(1)}, bf16[256,768]{1,0:T(8,128)(2,1)S(1)}, u32[]{:S(2)}, u32[]{:S(2)}) %collective-permute-start.7) | collective-permute-done | bytes 393248 | tf_op jit(solution)/shard_map/ppermute | solution.py:446
  36.2 3.7 %attend.1 = (bf16[32,768]{1,0:T(8,128)(2,1)}, bf16[32,128]{1,0:T(8,128)(2,1)S(1)}, bf16[16,128]{1,0:T(8,128)(2,1)S(1)}, bf16[16,128]{1,0:T(8,128)(2,1)S(1)}) custom-call(s32[8]{0:T(128)S(1)} %get-tuple-element.39.info, f32[32,768]{1,0:T(8,128)S(1)} %get-tuple-element.56.in_ref, bf16[512,768]{1,0:T(8,128)(2,1)S(1)} %get-tuple-element.60.query_ref, ...), custom_call_target="tpu_custom_call" | custom-call | flops 10000000 | bytes 65536 | tf_op jit(solution)/shard_map/attend/pallas_call | solution.py:64
  39.9 0.1 collective-permute-start.8
  40.0 1.0 %collective-permute-done.8.pair_ref = bf16[16,128]{1,0:T(8,128)(2,1)S(1)} collective-permute-done((bf16[16,128]{1,0:T(8,128)(2,1)S(1)}, bf16[16,128]{1,0:T(8,128)(2,1)S(1)}, u32[]{:S(2)}, u32[]{:S(2)}) %collective-permute-start.8) | collective-permute-done | bytes 4128 | tf_op jit(solution)/shard_map/ppermute | solution.py:426
  41.1 2.9 %collective-permute-done.9.odd_ref = bf16[16,128]{1,0:T(8,128)(2,1)S(1)} collective-permute-done((bf16[16,128]{1,0:T(8,128)(2,1)S(1)}, bf16[16,128]{1,0:T(8,128)(2,1)S(1)}, u32[]{:S(2)}, u32[]{:S(2)}) %collective-permute-start.9) | collective-permute-done | bytes 4128 | tf_op jit(solution)/shard_map/ppermute | solution.py:426
  44.0 1.6 %final.1 = f32[3,384]{1,0:T(4,128)} custom-call(s32[8]{0:T(128)S(1)} %get-tuple-element.39.info, bf16[384,64]{1,0:T(8,128)(2,1)S(1)} %get-tuple-element.51.hot_ref, f32[384,128]{1,0:T(8,128)S(1)} %get-tuple-element.52.mid_ref, bf16[32,128]{1,0:T(8,128)(2,1)S(1)} %get-tuple-element.72.back_ref, bf16[16,128]{1,0:T(8,128)(2,1)S(1)} %collective-permute-done.8.pair_ref, ...), custom_call_target="tpu_custom_call" | custom-call | flops 10000000 | bytes 4608 | tf_op jit(solution)/shard_map/final/pallas_call | solution.py:64
  (22 shorter events, 0.3 us)
Async XLA Ops:
  3.5 7.4 %collective-permute-start = (bf16[96,256]{1,0:T(8,128)(2,1)S(1)}, bf16[96,256]{1,0:T(8,128)(2,1)S(1)}, u32[]{:S(2)}, u32[]{:S(2)}) collective-permute-start(bf16[96,256]{1,0:T(8,128)(2,1)S(1)} %get-tuple-element.45), channel_id=1, source_target_pairs={{0,1},{1,0},{2,3},{3,2},{4,5},{5,4},{6,7},{7,6},{8,9},{9,8},{10,11... | collective-permute-start | bytes 147464 | tf_op jit(solution)/shard_map/ppermute | solution.py:426
  3.6 7.3 %collective-permute-start.1 = (bf16[96,256]{1,0:T(8,128)(2,1)S(1)}, bf16[96,256]{1,0:T(8,128)(2,1)S(1)}, u32[]{:S(2)}, u32[]{:S(2)}) collective-permute-start(bf16[96,256]{1,0:T(8,128)(2,1)S(1)} %get-tuple-element.46), channel_id=1, source_target_pairs={{1,2},{3,4},{5,6},{7,8},{9,10},{11,12},{13,14},{2,1},{4,3},{6,5},{... | collective-permute-start | bytes 147464 | tf_op jit(solution)/shard_map/ppermute | solution.py:426
  5.8 0.7 %copy-start.4 = (s32[12]{0:T(128)S(1)}, s32[12]{0:T(128)}, u32[]{:S(2)}) copy-start(s32[12]{0:T(128)} %offsets_hbm.1) | copy-start | bytes 148
  10.9 7.4 %copy-start = (bf16[32,768]{1,0:T(8,128)(2,1)S(1)}, bf16[32,768]{1,0:T(8,128)(2,1)}, u32[]{:S(2)}) copy-start(bf16[32,768]{1,0:T(8,128)(2,1)} %single_ref.1) | copy-start | bytes 147460
  13.8 1.4 %collective-permute-start.2 = (bf16[16,896]{1,0:T(8,128)(2,1)S(1)}, bf16[16,896]{1,0:T(8,128)(2,1)S(1)}, u32[]{:S(2)}, u32[]{:S(2)}) collective-permute-start(bf16[16,896]{1,0:T(8,128)(2,1)S(1)} %get-tuple-element.54), channel_id=1, source_target_pairs={{0,1},{1,0},{2,3},{3,2},{4,5},{5,4},{6,7},{7,6},{8,9},{9,8},{10,11... | collective-permute-start | bytes 86024 | tf_op jit(solution)/shard_map/ppermute | solution.py:426
  14.1 4.2 %collective-permute-start.3 = (bf16[16,896]{1,0:T(8,128)(2,1)S(1)}, bf16[16,896]{1,0:T(8,128)(2,1)S(1)}, u32[]{:S(2)}, u32[]{:S(2)}) collective-permute-start(bf16[16,896]{1,0:T(8,128)(2,1)S(1)} %get-tuple-element.55), channel_id=1, source_target_pairs={{1,2},{3,4},{5,6},{7,8},{9,10},{11,12},{13,14},{2,1},{4,3},{6,5},{... | collective-permute-start | bytes 86024 | tf_op jit(solution)/shard_map/ppermute | solution.py:426
  19.2 5.8 %collective-permute-start.4 = (bf16[32,768]{1,0:T(8,128)(2,1)S(1)}, bf16[32,768]{1,0:T(8,128)(2,1)S(1)}, u32[]{:S(2)}, u32[]{:S(2)}) collective-permute-start(bf16[32,768]{1,0:T(8,128)(2,1)S(1)} %get-tuple-element.57.norm_ref), channel_id=1, source_target_pairs={{0,9},{1,8},{2,11},{3,10},{4,13},{5,12},{6,15},{7,14},{8,1},{9,0},... | collective-permute-start | bytes 147464 | tf_op jit(solution)/shard_map/ppermute | solution.py:446
  25.0 4.1 %collective-permute-start.5 = (bf16[64,768]{1,0:T(8,128)(2,1)S(1)}, bf16[64,768]{1,0:T(8,128)(2,1)S(1)}, u32[]{:S(2)}, u32[]{:S(2)}) collective-permute-start(bf16[64,768]{1,0:T(8,128)(2,1)S(1)} %get-tuple-element.76.after), channel_id=1, source_target_pairs={{0,5},{1,2},{2,1},{3,6},{4,7},{5,0},{6,3},{7,4},{8,13},{9,10},{10,... | collective-permute-start | bytes 294920 | tf_op jit(solution)/shard_map/ppermute | solution.py:446
  29.1 5.2 %collective-permute-start.6 = (bf16[128,768]{1,0:T(8,128)(2,1)S(1)}, bf16[128,768]{1,0:T(8,128)(2,1)S(1)}, u32[]{:S(2)}, u32[]{:S(2)}) collective-permute-start(bf16[128,768]{1,0:T(8,128)(2,1)S(1)} %pad_maximum_fusion.1), channel_id=1, source_target_pairs={{0,3},{1,4},{2,7},{3,0},{4,1},{5,6},{6,5},{7,2},{8,11},{9,12},{10,... | collective-permute-start | bytes 589832 | tf_op jit(solution)/shard_map/ppermute | solution.py:446
  34.3 1.8 %collective-permute-start.7 = (bf16[256,768]{1,0:T(8,128)(2,1)S(1)}, bf16[256,768]{1,0:T(8,128)(2,1)S(1)}, u32[]{:S(2)}, u32[]{:S(2)}) collective-permute-start(bf16[256,768]{1,0:T(8,128)(2,1)S(1)} %pad_maximum_fusion), channel_id=1, source_target_pairs={{0,1},{1,0},{2,3},{3,2},{4,5},{5,4},{6,7},{7,6},{8,9},{9,8},{10,11... | collective-permute-start | bytes 1179656 | tf_op jit(solution)/shard_map/ppermute | solution.py:446
  36.2 7.8 %copy-start.1 = (f32[3,384]{1,0:T(4,128)S(1)}, f32[3,384]{1,0:T(4,128)}, u32[]{:S(2)}) copy-start(f32[3,384]{1,0:T(4,128)} %pos_ref.1) | copy-start | bytes 13828
  36.2 7.8 %copy-start.2 = (f32[3,384]{1,0:T(4,128)S(1)}, f32[3,384]{1,0:T(4,128)}, u32[]{:S(2)}) copy-start(f32[3,384]{1,0:T(4,128)} %noise_ref.1) | copy-start | bytes 13828
  36.2 7.8 %copy-start.3 = (bf16[3,128]{1,0:T(4,128)(2,1)S(1)}, bf16[3,128]{1,0:T(4,128)(2,1)}, u32[]{:S(2)}) copy-start(bf16[3,128]{1,0:T(4,128)(2,1)} %wpos_ref.1) | copy-start | bytes 2308
  39.9 1.2 %collective-permute-start.8 = (bf16[16,128]{1,0:T(8,128)(2,1)S(1)}, bf16[16,128]{1,0:T(8,128)(2,1)S(1)}, u32[]{:S(2)}, u32[]{:S(2)}) collective-permute-start(bf16[16,128]{1,0:T(8,128)(2,1)S(1)} %get-tuple-element.73), channel_id=1, source_target_pairs={{0,1},{1,0},{2,3},{3,2},{4,5},{5,4},{6,7},{7,6},{8,9},{9,8},{10,11... | collective-permute-start | bytes 12296 | tf_op jit(solution)/shard_map/ppermute | solution.py:426
  40.0 3.9 %collective-permute-start.9 = (bf16[16,128]{1,0:T(8,128)(2,1)S(1)}, bf16[16,128]{1,0:T(8,128)(2,1)S(1)}, u32[]{:S(2)}, u32[]{:S(2)}) collective-permute-start(bf16[16,128]{1,0:T(8,128)(2,1)S(1)} %get-tuple-element.74), channel_id=1, source_target_pairs={{1,2},{3,4},{5,6},{7,8},{9,10},{11,12},{13,14},{2,1},{4,3},{6,5},{... | collective-permute-start | bytes 12296 | tf_op jit(solution)/shard_map/ppermute | solution.py:426

commit v5 on v4

--- a/solution.py
+++ b/solution.py
@@ -61,7 +61,7 @@
         cost_estimate=pl.CostEstimate(flops=flops, bytes_accessed=moved, transcendentals=0),
         compiler_params=pltpu.CompilerParams(vmem_limit_bytes=limit * 2**20),
     )
-    return lambda *args: run(*[pltpu.with_memory_space_constraint(x, pltpu.HBM) if h and x.ndim > 1 else x for x, h in zip(args, held)])
+    return lambda *args: run(*[pltpu.with_memory_space_constraint(x, pltpu.HBM) if h and x.size > 1 else x for x, h in zip(args, held)])
 
 
 def shape(dims, dtype):
@@ -82,6 +82,11 @@
     single_hbm,
     wc_hbm,
     wqkv_hbm,
+    offsets_hbm,
+    token_hbm,
+    bias_hbm,
+    wout_hbm,
+    wagg_hbm,
     info_ref,
     start_ref,
     q_ref,
@@ -89,6 +94,11 @@
     v_ref,
     pair_ref,
     odd_ref,
+    offsets_ref,
+    token_ref,
+    bias_ref,
+    wout_ref,
+    wagg_ref,
     counts_ref,
     pos_ref,
     noise_ref,
@@ -105,6 +115,11 @@
         (single_hbm, single_ref),
         (wqkv_hbm, wqkv_ref),
         (counts_hbm, counts_ref),
+        (offsets_hbm, offsets_ref),
+        (token_hbm, token_ref.at[0]),
+        (bias_hbm, bias_ref),
+        (wout_hbm, wout_ref),
+        (wagg_hbm, wagg_ref),
     )
     rows, width = single_ref.shape
     for ref in (k_ref, v_ref):
@@ -124,7 +139,7 @@
     qkv = dot(normed, wqkv_ref[...]).astype(BF16)
     q_ref[...] = qkv[:, :width]
     copies[5].wait()
-    live = counts_ref[0]
+    live = counts_ref[0, 0]
     me = lax.axis_index("row")
     info_ref[0] = live
     info_ref[1] = me
@@ -136,70 +151,52 @@
         ref[:rows, :] = qkv[:, (n + 1) * width : (n + 2) * width].astype(F32)
         pair_ref[:, at] = ref[pl.ds(jnp.where(even, tail, 0), AHEAD), :].astype(BF16)
         odd_ref[:, at] = ref[pl.ds(jnp.where(even, 0, tail), AHEAD), :].astype(BF16)
-
-
-def one_window(queries, keys, values, bias, allowed):
-    width = queries.shape[1]
+    for copy in copies[6:]:
+        copy.wait()
+
+
+def windows_of(queries, keys, values, biases, masks):
+    width = queries[0].shape[1]
     depth = width // AH
     rows = AH * QWIN
     own_head = iota((rows, width), 0) // QWIN == iota((rows, width), 1) // depth
-    stacked = jnp.where(own_head, jnp.concatenate([queries] * AH, axis=0), 0.0).astype(BF16)
-    scores = dot_nt(stacked, keys.astype(BF16)) * (1.0 / depth**0.5) + bias
-    if allowed is not None:
-        scores = jnp.where(allowed, scores, masked_score)
-    scores = jnp.exp(scores - jnp.max(scores, axis=-1, keepdims=True))
-    weights = (scores / jnp.sum(scores, axis=-1, keepdims=True)).astype(BF16)
-    mixed = dot(weights, values.astype(BF16))
     lane_head = iota((QWIN, width), 1) // depth
-    out = mixed[:QWIN]
-    for h in range(1, AH):
-        out = jnp.where(lane_head == h, mixed[h * QWIN : (h + 1) * QWIN], out)
-    return out.astype(BF16)
-
-
-def local_body(
-    offsets_hbm,
-    q_ref,
-    k_ref,
-    v_ref,
-    bias_hbm,
-    wout_hbm,
-    wagg_hbm,
-    offsets_ref,
-    bias_ref,
-    wout_ref,
-    wagg_ref,
-    att_ref,
-    sems,
-):
-    copies = fetch(
-        sems, (offsets_hbm, offsets_ref), (bias_hbm, bias_ref), (wout_hbm, wout_ref), (wagg_hbm, wagg_ref)
-    )
+    stacked = [jnp.where(own_head, jnp.concatenate([q] * AH, axis=0), 0.0).astype(BF16) for q in queries]
+    scores = [dot_nt(q, k) * (1.0 / depth**0.5) + b for q, k, b in zip(stacked, keys, biases)]
+    if masks is not None:
+        scores = [jnp.where(m, s, masked_score) for m, s in zip(masks, scores)]
+    tops = [jnp.max(s, axis=-1, keepdims=True) for s in scores]
+    scores = [jnp.exp(s - t) for s, t in zip(scores, tops)]
+    shares = [1.0 / jnp.sum(s, axis=-1, keepdims=True) for s in scores]
+    weights = [(s * r).astype(BF16) for s, r in zip(scores, shares)]
+    mixed = [dot(w, v) for w, v in zip(weights, values)]
+    outs = []
+    for mix in mixed:
+        out = mix[:QWIN]
+        for h in range(1, AH):
+            out = jnp.where(lane_head == h, mix[h * QWIN : (h + 1) * QWIN], out)
+        outs.append(out.astype(BF16))
+    return outs
+
+
+def local_body(offsets, q_ref, k_ref, v_ref, bias_ref, att_ref):
     rows, width = q_ref.shape
     windows = rows // QWIN
     skip = BEHIND // QWIN
     stop = windows - (AHEAD - QWIN) // QWIN
     for part in (slice(0, skip * QWIN), slice(stop * QWIN, rows)):
         att_ref[part, :] = jnp.zeros((part.stop - part.start, width), BF16)
-    copies[0].wait()
-    copies[1].wait()
-    for m in range(skip, stop):
-        at = slice(m * QWIN, (m + 1) * QWIN)
-        base = m * QWIN + offsets_ref[m]
-        bias = bias_ref[:, at, :].reshape(AH * QWIN, KWIN)
-        att_ref[at, :] = one_window(
-            q_ref[at, :].astype(F32), k_ref[pl.ds(base, KWIN), :], v_ref[pl.ds(base, KWIN), :], bias, None
-        )
-    copies[2].wait()
-    copies[3].wait()
-
-
-def onehot(info, token_ref, half, block_rows):
-    rows = token_ref.shape[1]
-    relative = token_ref[...] - (info[1] * block_rows - half)
-    living = iota((1, rows), 1) < info[0]
-    hot = (iota((block_rows + 2 * half, rows), 0) == relative) & living
-    return hot.astype(F32)
+    at = [slice(m * QWIN, (m + 1) * QWIN) for m in range(skip, stop)]
+    base = [m * QWIN + offsets[0, m] for m in range(skip, stop)]
+    outs = windows_of(
+        [q_ref[a, :].astype(F32) for a in at],
+        [k_ref[pl.ds(b, KWIN), :].astype(BF16) for b in base],
+        [v_ref[pl.ds(b, KWIN), :].astype(BF16) for b in base],
+        [bias_ref[:, a, :].reshape(AH * QWIN, KWIN) for a in at],
+        None,
+    )
+    for a, out in zip(at, outs):
+        att_ref[a, :] = out
 
 
 def atoms_body(
@@ -222,6 +219,7 @@
     pair_out,
     odd_out,
     hot_ref,
+    living_ref,
     k_ext,
     v_ext,
     att,
@@ -242,23 +240,27 @@
     windows = rows // QWIN
     tails = AHEAD // QWIN
     first = jnp.minimum((live - BEHIND) // QWIN, windows - tails)
-    for m in list(range(BEHIND // QWIN)) + [first + n for n in range(tails)]:
-        at = pl.ds(pl.multiple_of(m * QWIN, QWIN), QWIN)
-        base = BEHIND + QWIN * m + offsets[m]
-        slots = base + iota((1, KWIN), 1)
-        bias = bias_ref[:, at, :].reshape(AH * QWIN, KWIN)
-        att[at, :] = one_window(
-            q_ref[at, :].astype(F32),
-            k_ext[pl.ds(base, KWIN), :],
-            v_ext[pl.ds(base, KWIN), :],
-            bias,
-            (slots >= low) & (slots < high),
-        )
+    chosen = list(range(BEHIND // QWIN)) + [first + n for n in range(tails)]
+    at = [pl.ds(pl.multiple_of(m * QWIN, QWIN), QWIN) for m in chosen]
+    base = [BEHIND + QWIN * m + offsets[0, m] for m in chosen]
+    slots = [b + iota((1, KWIN), 1) for b in base]
+    outs = windows_of(
+        [q_ref[a, :].astype(F32) for a in at],
+        [k_ext[pl.ds(b, KWIN), :].astype(BF16) for b in base],
+        [v_ext[pl.ds(b, KWIN), :].astype(BF16) for b in base],
+        [bias_ref[:, a, :].reshape(AH * QWIN, KWIN) for a in at],
+        [(s >= low) & (s < high) for s in slots],
+    )
+    for a, out in zip(at, outs):
+        att[a, :] = out
     mid = start_ref[...] + dot(att[...], wout_ref[...])
     mid_ref[...] = mid
     spread = jnp.maximum(dot(mid.astype(BF16), wagg_ref[...]), 0.0).astype(BF16)
     block_rows = own_ref.shape[0]
-    hot = onehot(info, token_ref, half, block_rows)
+    living = iota((1, rows), 1) < live
+    living_ref[...] = living.astype(F32)
+    relative = token_ref[...] - (me * block_rows - half)
+    hot = ((iota((block_rows + 2 * half, rows), 0) == relative) & living).astype(F32)
     hot_ref[...] = jnp.transpose(hot).astype(BF16)
     sums = dot(hot.astype(BF16), spread)
     counts = jnp.sum(hot, axis=1, keepdims=True)
@@ -274,13 +276,14 @@
     odd_out[...] = jnp.where(even, lower, upper).astype(BF16)
 
 
-def token_body(info, own_ref, pair_ref, odd_ref, single_ref, in_ref, norm_ref):
-    even = info[1] % 2 == 0
+def token_body(own_ref, pair_ref, odd_ref, single_ref, in_ref, norm_ref):
+    me = lax.axis_index("row")
+    even = me % 2 == 0
     model = single_ref.shape[1]
     pair = pair_ref[...].astype(F32)
     odd = odd_ref[...].astype(F32)
-    lower = jnp.where(info[1] > 0, jnp.where(even, odd, pair), 0.0)
-    upper = jnp.where(info[1] < info[2], jnp.where(even, pair, odd), 0.0)
+    lower = jnp.where(me > 0, jnp.where(even, odd, pair), 0.0)
+    upper = jnp.where(me < lax.axis_size("row") - 1, jnp.where(even, pair, odd), 0.0)
     both = own_ref[...] + jnp.concatenate([lower, upper], axis=0)
     count = both[:, model : model + 1] + both[:, model + 1 : model + 2]
     token_in = single_ref[...].astype(F32) + both[:, :model] / jnp.maximum(count, 1.0)
@@ -348,7 +351,6 @@
 def attend_body(
     orders,
     half,
-    info,
     in_ref,
     query_ref,
     gate_ref,
@@ -365,7 +367,7 @@
 ):
     rows, model = in_ref.shape
     keys = all_ref.shape[0]
-    me = info[1]
+    me = lax.axis_index("row")
     even = me % 2 == 0
     kind = (me ^ (me >> 1) ^ (me >> 2)) & 1
     if orders is None:
@@ -385,7 +387,7 @@
         bias = bias_ref[g * group : (g + 1) * group].reshape(group * rows, keys)
         scores = dot_nt(query_ref[at, :], values) * scale + bias
         scores = jnp.exp(scores - jnp.max(scores, axis=-1, keepdims=True))
-        weights = (scores / jnp.sum(scores, axis=-1, keepdims=True)).astype(BF16)
+        weights = (scores * (1.0 / jnp.sum(scores, axis=-1, keepdims=True))).astype(BF16)
         mixed = dot(weights, values).astype(BF16)
         wide = dot(mixed, wv_ref[:, g * span : (g + 1) * span])
         part = wide[:rows]
@@ -403,8 +405,8 @@
     odd_out[...] = jnp.where(even, lower, upper).astype(BF16)
 
 
-def final_body(info, hot_ref, mid_ref, back_ref, pair_ref, odd_ref, wpos_ref, pos_ref, noise_ref, out_ref):
-    even = info[1] % 2 == 0
+def final_body(living_ref, hot_ref, mid_ref, back_ref, pair_ref, odd_ref, wpos_ref, pos_ref, noise_ref, out_ref):
+    even = lax.axis_index("row") % 2 == 0
     pair = pair_ref[...].astype(F32)
     odd = odd_ref[...].astype(F32)
     near = jnp.concatenate(
@@ -413,8 +415,7 @@
     last = mid_ref[...] + dot(hot_ref[...], near)
     update = dot_nt(wpos_ref[...], normalize(last).astype(BF16))
     noisy = pos_ref[...] + noise_level * noise_ref[...]
-    living = iota((1, noisy.shape[1]), 1) < info[0]
-    out_ref[...] = jnp.where(living, skip_scale * noisy + output_scale * update, 0.0)
+    out_ref[...] = jnp.where(living_ref[...] > 0.0, skip_scale * noisy + output_scale * update, 0.0)
 
 
 def exchange(pair, odd, groups, count):
@@ -478,7 +479,7 @@
     block_rows, model = token_single.shape
     half = block_rows // 2
     info_shape = shape((8,), jnp.int32)
-    info, start, q, keys, values, pair, odd = call(
+    info, start, q, keys, values, pair, odd, offsets, tokens, bias, wout, wagg = call(
         embed_body,
         [
             info_shape,
@@ -488,38 +489,47 @@
             shape((rows + AHEAD, width), F32),
             shape((AHEAD, 2 * width), BF16),
             shape((AHEAD, 2 * width), BF16),
+            shape((1, rows // QWIN), jnp.int32),
+            shape((1, rows), jnp.int32),
+            shape(atom_bias.shape, F32),
+            shape(w_atom_out.shape, BF16),
+            shape(w_agg.shape, BF16),
         ],
         "embed",
-        [HBM] * 6,
+        [HBM] * 11,
         [
-            pltpu.SMEM(atom_counts.shape, jnp.int32),
+            pltpu.SMEM((1, 1), jnp.int32),
             pltpu.VMEM(positions.shape, F32),
             pltpu.VMEM(noise.shape, F32),
             pltpu.VMEM(atom_single.shape, BF16),
             pltpu.VMEM(w_coord.shape, F32),
             pltpu.VMEM(w_atom_qkv.shape, BF16),
-            pltpu.SemaphoreType.DMA((6,)),
+            pltpu.SemaphoreType.DMA((11,)),
         ],
-        out_specs=[SMEM] + [VMEM] * 6,
-    )(atom_counts, positions, noise, atom_single, w_coord, w_atom_qkv)
+        out_specs=[SMEM] + [VMEM] * 6 + [SMEM] + [VMEM] * 4,
+    )(
+        atom_counts[None],
+        positions,
+        noise,
+        atom_single,
+        w_coord,
+        w_atom_qkv,
+        window_offsets[None],
+        atom_token,
+        atom_bias,
+        w_atom_out,
+        w_agg,
+    )
     pair, odd = exchange(pair, odd, groups, count)
-    offsets, bias, wout, wagg, att = call(
+    (att,) = call(
         local_body,
-        [
-            shape(window_offsets.shape, jnp.int32),
-            shape(atom_bias.shape, F32),
-            shape(w_atom_out.shape, BF16),
-            shape(w_agg.shape, BF16),
-            shape((rows, width), BF16),
-        ],
+        [shape((rows, width), BF16)],
         "local",
-        [HBM] + [VMEM] * 3 + [HBM] * 3,
-        [pltpu.SemaphoreType.DMA((4,))],
+        [SMEM] + [VMEM] * 4,
         flops=10**9,
-        out_specs=[SMEM] + [VMEM] * 4,
-    )(window_offsets, q, keys, values, atom_bias, w_atom_out, w_agg)
+    )(offsets, q, keys, values, bias)
     packed = model + 128
-    mid, own, pair, odd, hot = call(
+    mid, own, pair, odd, hot, living = call(
         functools.partial(atoms_body, half),
         [
             shape((rows, width), F32),
@@ -527,18 +537,19 @@
             shape((half, packed), BF16),
             shape((half, packed), BF16),
             shape((rows, block_rows + 2 * half), BF16),
+            shape((1, rows), F32),
         ],
         "atoms",
         [SMEM, SMEM] + [VMEM] * 11,
         [pltpu.VMEM((BEHIND + rows + AHEAD, width), F32)] * 2 + [pltpu.VMEM((rows, width), BF16)],
-    )(info, offsets, atom_token[None], start, q, keys, values, pair, odd, att, bias, wout, wagg)
+    )(info, offsets, tokens, start, q, keys, values, pair, odd, att, bias, wout, wagg)
     pair, odd = exchange(pair, odd, groups, count)
     token_in, norm = call(
         token_body,
         [shape((block_rows, model), F32), shape((block_rows, model), BF16)],
         "token",
-        [SMEM] + [VMEM] * 4,
-    )(info, own, pair, odd, token_single)
+        [VMEM] * 4,
+    )(own, pair, odd, token_single)
 
     def query(n, seen):
         return call(
@@ -581,16 +592,16 @@
             shape((half, width), BF16),
         ],
         "attend",
-        [SMEM] + [VMEM] * 8,
+        [VMEM] * 8,
         [pltpu.VMEM((count * block_rows, model), BF16)],
-    )(info, token_in, query_rows, gate, everyone, bias, wv, wout, wback)
+    )(token_in, query_rows, gate, everyone, bias, wv, wout, wback)
     pair, odd = exchange(pair, odd, groups, count)
     (denoised,) = call(
         final_body,
         [shape(positions.shape, F32)],
         "final",
-        [SMEM] + [VMEM] * 8,
-    )(info, hot, mid, back, pair, odd, w_pos, positions, noise)
+        [VMEM] * 9,
+    )(living, hot, mid, back, pair, odd, w_pos, positions, noise)
     return (denoised, token_out)
 
 

time: 46.5 us -> 40.9 us (0.88)
  Pallas kernels: 20.4 us -> 14.5 us
  waiting for transfers between devices: 18.8 us -> 20.5 us
  local copies, waits for them, and re-layouts: 1.43 us -> 0.09 us
    pallas_call x8, Pallas kernels: 20.4 us -> 14.5 us  [call(): run(*[pltpu.with_memory_space_constraint(x, pltpu.HBM) if h and x.size >...]
    ppermute x3, waiting for transfers between devices: 6 us -> 7.59 us  [exchange(): lax.ppermute(odd, ('grp', 'row'), far)]
    broadcast_in_dim x1 -> x0, local copies, waits for them, and re-layouts: 0.68 us -> none  [on_device(): atom_token[None]]
    unnamed x13 -> x11, local copies, waits for them, and re-layouts: 0.71 us -> 0.06 us
  transfers between devices with their start and end apart: 10 -> 10, of which waited for: 7 -> 8; matrix products, arithmetic and copies ran while one was open for 2% -> 0% of each run, Pallas kernels for 20% -> 15%
where the time goes in v5:
time: 40.9 us; the launch traced here: 40.1 us
  waiting for transfers between devices  20.5 us (50%)
  Pallas kernels  14.5 us (35%)
  starting transfers between devices  3.58 us (9%)
  between operations  1.43 us (3%)
    pallas_call x8, Pallas kernels, call(): run(*[pltpu.with_memory_space_constraint(x, pltpu.HBM) if h and x.size >...  14.5 us
    ppermute x4, waiting for transfers between devices, gather(): arrived = lax.ppermute(norm, 'row', perm)  11.8 us
    ppermute x3, waiting for transfers between devices, exchange(): lax.ppermute(odd, ('grp', 'row'), far)  7.59 us
    ppermute x3, starting transfers between devices, exchange(): lax.ppermute(odd, ('grp', 'row'), far)  2.91 us
    ppermute x3, waiting for transfers between devices, exchange(): lax.ppermute(pair, 'row', near)  1.04 us
  transfers between devices with their start and end apart: 10, of which 8 were waited for; matrix products, arithmetic and copies ran while one was open for 0% of the time, Pallas kernels for 15%

profile of v5, /device:TPU:24, one launch (start us, length us, event | category | flops | bytes accessed | tf_op | source)
XLA Modules:
  0.0 40.1 jit_solution(1300051503378469608)
XLA Ops:
  1.3 2.3 %embed.1 = (s32[8]{0:T(128)S(1)}, f32[384,128]{1,0:T(8,128)S(1)}, bf16[384,128]{1,0:T(8,128)(2,1)S(1)}, f32[480,128]{1,0:T(8,128)S(1)}, f32[480,128]{1,0:T(8,128...) custom-call(s32[1,1]{1,0:T(1,128)} %bitcast.2.counts_hbm, ...), custom_call_target="tpu_custom_call" | custom-call | flops 10000000 | bytes 1902160 | tf_op jit(solution)/shard_map/embed/pallas_call | solution.py:64
  3.6 0.1 collective-permute-start
  3.7 1.5 %collective-permute-start.1 = (bf16[96,256]{1,0:T(8,128)(2,1)S(1)}, bf16[96,256]{1,0:T(8,128)(2,1)S(1)}, u32[]{:S(2)}, u32[]{:S(2)}) collective-permute-start(bf16[96,256]{1,0:T(8,128)(2,1)S(1)} %get-tuple-element.48), channel_id=1, source_target_pairs={{1,2},{3,4},{5,6},{7,8},{9,10},{11,12},{13,14},{2,1},{4,3},{6,5},{... | collective-permute-start | bytes 147464 | tf_op jit(solution)/shard_map/ppermute | solution.py:427
  5.2 1.2 %local.1.att_ref = bf16[384,128]{1,0:T(8,128)(2,1)S(1)} custom-call(s32[1,12]{1,0:T(1,128)S(1)} %get-tuple-element.41.offsets, bf16[384,128]{1,0:T(8,128)(2,1)S(1)} %get-tuple-element.44.q_ref, f32[480,128]{1,0:T(8,128)S(1)} %get-tuple-element.45.k_ref, f32[480,128]{1,0:T(8,128)S(1)} %get-tuple-element.46.v_ref, f32[4,384,128]{2,1,0:T(8,128)S(1)} %get-tuple-element.49.bias_ref), custom_call_target="tpu_custom_call" | custom-call | flops 1000000000 | bytes 98304 | tf_op jit(solution)/shard_map/local/pallas_call | solution.py:64
  6.5 1.8 %collective-permute-done.1.odd_ref = bf16[96,256]{1,0:T(8,128)(2,1)S(1)} collective-permute-done((bf16[96,256]{1,0:T(8,128)(2,1)S(1)}, bf16[96,256]{1,0:T(8,128)(2,1)S(1)}, u32[]{:S(2)}, u32[]{:S(2)}) %collective-permute-start.1) | collective-permute-done | bytes 49184 | tf_op jit(solution)/shard_map/ppermute | solution.py:427
  8.3 1.7 %atoms.1 = (f32[384,128]{1,0:T(8,128)S(1)}, f32[32,896]{1,0:T(8,128)S(1)}, bf16[16,896]{1,0:T(8,128)(2,1)S(1)}, bf16[16,896]{1,0:T(8,128)(2,1)S(1)}, bf16[384,64]{1,0:T(8,128)(2,1)S(1)}, /*index=5*/f32[1,384]{1,0:T(1,128)S(1)}) custom-call(s32[8]{0:T(128)S(1)} %get-tuple-element.40.info, s32[1,12]{1,0:T(1,128)S(1)} %get-tuple-element.41.offsets, ...), custom_call_target="tpu_custom_call" | custom-call | flops 10000000 | bytes 419328 | tf_op jit(solution)/shard_map/atoms/pallas_call | solution.py:64
  10.0 0.1 collective-permute-start.2
  10.1 1.4 %collective-permute-start.3 = (bf16[16,896]{1,0:T(8,128)(2,1)S(1)}, bf16[16,896]{1,0:T(8,128)(2,1)S(1)}, u32[]{:S(2)}, u32[]{:S(2)}) collective-permute-start(bf16[16,896]{1,0:T(8,128)(2,1)S(1)} %get-tuple-element.57), channel_id=1, source_target_pairs={{1,2},{3,4},{5,6},{7,8},{9,10},{11,12},{13,14},{2,1},{4,3},{6,5},{... | collective-permute-start | bytes 86024 | tf_op jit(solution)/shard_map/ppermute | solution.py:427
  11.5 2.9 %collective-permute-done.3.odd_ref = bf16[16,896]{1,0:T(8,128)(2,1)S(1)} collective-permute-done((bf16[16,896]{1,0:T(8,128)(2,1)S(1)}, bf16[16,896]{1,0:T(8,128)(2,1)S(1)}, u32[]{:S(2)}, u32[]{:S(2)}) %collective-permute-start.3) | collective-permute-done | bytes 28704 | tf_op jit(solution)/shard_map/ppermute | solution.py:427
  14.4 0.3 token_.1
  14.7 0.1 collective-permute-start.4
  14.8 2.6 %query.1 = (bf16[512,768]{1,0:T(8,128)(2,1)S(1)}, f32[32,768]{1,0:T(8,128)S(1)}) custom-call(bf16[32,768]{1,0:T(8,128)(2,1)S(1)} %get-tuple-element.59.norm_ref, bf16[768,2304]{1,0:T(8,128)(2,1)} %wqkv_hbm.5, bf16[768,768]{1,0:T(8,128)(2,1)} %wgate_hbm.1), custom_call_target="tpu_custom_call" | custom-call | flops 1000000000 | bytes 884736 | tf_op jit(solution)/shard_map/query/pallas_call | solution.py:64
  17.4 3.2 %collective-permute-done.4 = bf16[32,768]{1,0:T(8,128)(2,1)S(1)} collective-permute-done((bf16[32,768]{1,0:T(8,128)(2,1)S(1)}, bf16[32,768]{1,0:T(8,128)(2,1)S(1)}, u32[]{:S(2)}, u32[]{:S(2)}) %collective-permute-start.4) | collective-permute-done | bytes 49184 | tf_op jit(solution)/shard_map/ppermute | solution.py:447
  20.6 0.1 collective-permute-start.5
  20.7 2.0 %stage.1 = (f32[16,32,512]{2,1,0:T(8,128)S(1)}, bf16[768,768]{1,0:T(8,128)(2,1)S(1)}, bf16[768,768]{1,0:T(8,128)(2,1)S(1)}, bf16[768,128]{1,0:T(8,128)(2,1)S(1)}) custom-call(bf16[64,768]{1,0:T(8,128)(2,1)S(1)} %get-tuple-element.78.after, f32[16,32,512]{2,1,0:T(8,128)} %bias_hbm.3, s32[32,512]{1,0:T(8,128)} %mask_hbm.1, bf16[768,2304]{1,0:T(8,128)(2,1)} %wqkv_hbm.5, ...), custom_call_target="tpu_custom_call" | custom-call | flops 1000000000 | bytes 3604480 | tf_op jit(solution)/shard_map/stage/pallas_call | solution.py:64
  22.8 2.0 %collective-permute-done.5 = bf16[64,768]{1,0:T(8,128)(2,1)S(1)} collective-permute-done((bf16[64,768]{1,0:T(8,128)(2,1)S(1)}, bf16[64,768]{1,0:T(8,128)(2,1)S(1)}, u32[]{:S(2)}, u32[]{:S(2)}) %collective-permute-start.5) | collective-permute-done | bytes 98336 | tf_op jit(solution)/shard_map/ppermute | solution.py:447
  24.9 5.1 %collective-permute-done.6 = bf16[128,768]{1,0:T(8,128)(2,1)S(1)} collective-permute-done((bf16[128,768]{1,0:T(8,128)(2,1)S(1)}, bf16[128,768]{1,0:T(8,128)(2,1)S(1)}, u32[]{:S(2)}, u32[]{:S(2)}) %collective-permute-start.6) | collective-permute-done | bytes 196640 | tf_op jit(solution)/shard_map/ppermute | solution.py:447
  30.0 0.2 collective-permute-start.7
  30.2 1.6 %collective-permute-done.7 = bf16[256,768]{1,0:T(8,128)(2,1)S(1)} collective-permute-done((bf16[256,768]{1,0:T(8,128)(2,1)S(1)}, bf16[256,768]{1,0:T(8,128)(2,1)S(1)}, u32[]{:S(2)}, u32[]{:S(2)}) %collective-permute-start.7) | collective-permute-done | bytes 393248 | tf_op jit(solution)/shard_map/ppermute | solution.py:447
  31.8 3.1 %attend.1 = (bf16[32,768]{1,0:T(8,128)(2,1)}, bf16[32,128]{1,0:T(8,128)(2,1)S(1)}, bf16[16,128]{1,0:T(8,128)(2,1)S(1)}, bf16[16,128]{1,0:T(8,128)(2,1)S(1)}) custom-call(f32[32,768]{1,0:T(8,128)S(1)} %get-tuple-element.58.in_ref, bf16[512,768]{1,0:T(8,128)(2,1)S(1)} %get-tuple-element.62.query_ref, f32[32,768]{1,0:T(8,128)S(1)} %get-tuple-element.63.gate_ref, ...), custom_call_target="tpu_custom_call" | custom-call | flops 10000000 | bytes 65536 | tf_op jit(solution)/shard_map/attend/pallas_call | solution.py:64
  35.0 0.1 collective-permute-start.8
  35.1 1.0 %collective-permute-done.8.pair_ref = bf16[16,128]{1,0:T(8,128)(2,1)S(1)} collective-permute-done((bf16[16,128]{1,0:T(8,128)(2,1)S(1)}, bf16[16,128]{1,0:T(8,128)(2,1)S(1)}, u32[]{:S(2)}, u32[]{:S(2)}) %collective-permute-start.8) | collective-permute-done | bytes 4128 | tf_op jit(solution)/shard_map/ppermute | solution.py:427
  36.1 2.9 %collective-permute-done.9.odd_ref = bf16[16,128]{1,0:T(8,128)(2,1)S(1)} collective-permute-done((bf16[16,128]{1,0:T(8,128)(2,1)S(1)}, bf16[16,128]{1,0:T(8,128)(2,1)S(1)}, u32[]{:S(2)}, u32[]{:S(2)}) %collective-permute-start.9) | collective-permute-done | bytes 4128 | tf_op jit(solution)/shard_map/ppermute | solution.py:427
  39.0 1.1 %final.1 = f32[3,384]{1,0:T(4,128)} custom-call(f32[1,384]{1,0:T(1,128)S(1)} %get-tuple-element.52.living_ref, bf16[384,64]{1,0:T(8,128)(2,1)S(1)} %get-tuple-element.53.hot_ref, f32[384,128]{1,0:T(8,128)S(1)} %get-tuple-element.54.mid_ref, bf16[32,128]{1,0:T(8,128)(2,1)S(1)} %get-tuple-element.74.back_ref, ...), custom_call_target="tpu_custom_call" | custom-call | flops 10000000 | bytes 4608 | tf_op jit(solution)/shard_map/final/pallas_call | solution.py:64
  (19 shorter events, 0.2 us)
Async XLA Ops:
  3.6 2.8 %collective-permute-start = (bf16[96,256]{1,0:T(8,128)(2,1)S(1)}, bf16[96,256]{1,0:T(8,128)(2,1)S(1)}, u32[]{:S(2)}, u32[]{:S(2)}) collective-permute-start(bf16[96,256]{1,0:T(8,128)(2,1)S(1)} %get-tuple-element.47), channel_id=1, source_target_pairs={{0,1},{1,0},{2,3},{3,2},{4,5},{5,4},{6,7},{7,6},{8,9},{9,8},{10,11... | collective-permute-start | bytes 147464 | tf_op jit(solution)/shard_map/ppermute | solution.py:427
  3.7 4.6 %collective-permute-start.1 = (bf16[96,256]{1,0:T(8,128)(2,1)S(1)}, bf16[96,256]{1,0:T(8,128)(2,1)S(1)}, u32[]{:S(2)}, u32[]{:S(2)}) collective-permute-start(bf16[96,256]{1,0:T(8,128)(2,1)S(1)} %get-tuple-element.48), channel_id=1, source_target_pairs={{1,2},{3,4},{5,6},{7,8},{9,10},{11,12},{13,14},{2,1},{4,3},{6,5},{... | collective-permute-start | bytes 147464 | tf_op jit(solution)/shard_map/ppermute | solution.py:427
  6.4 7.9 %copy-start = (bf16[32,768]{1,0:T(8,128)(2,1)S(1)}, bf16[32,768]{1,0:T(8,128)(2,1)}, u32[]{:S(2)}) copy-start(bf16[32,768]{1,0:T(8,128)(2,1)} %single_ref.1) | copy-start | bytes 147460
  10.0 1.5 %collective-permute-start.2 = (bf16[16,896]{1,0:T(8,128)(2,1)S(1)}, bf16[16,896]{1,0:T(8,128)(2,1)S(1)}, u32[]{:S(2)}, u32[]{:S(2)}) collective-permute-start(bf16[16,896]{1,0:T(8,128)(2,1)S(1)} %get-tuple-element.56), channel_id=1, source_target_pairs={{0,1},{1,0},{2,3},{3,2},{4,5},{5,4},{6,7},{7,6},{8,9},{9,8},{10,11... | collective-permute-start | bytes 86024 | tf_op jit(solution)/shard_map/ppermute | solution.py:427
  10.1 4.3 %collective-permute-start.3 = (bf16[16,896]{1,0:T(8,128)(2,1)S(1)}, bf16[16,896]{1,0:T(8,128)(2,1)S(1)}, u32[]{:S(2)}, u32[]{:S(2)}) collective-permute-start(bf16[16,896]{1,0:T(8,128)(2,1)S(1)} %get-tuple-element.57), channel_id=1, source_target_pairs={{1,2},{3,4},{5,6},{7,8},{9,10},{11,12},{13,14},{2,1},{4,3},{6,5},{... | collective-permute-start | bytes 86024 | tf_op jit(solution)/shard_map/ppermute | solution.py:427
  14.7 5.9 %collective-permute-start.4 = (bf16[32,768]{1,0:T(8,128)(2,1)S(1)}, bf16[32,768]{1,0:T(8,128)(2,1)S(1)}, u32[]{:S(2)}, u32[]{:S(2)}) collective-permute-start(bf16[32,768]{1,0:T(8,128)(2,1)S(1)} %get-tuple-element.59.norm_ref), channel_id=1, source_target_pairs={{0,9},{1,8},{2,11},{3,10},{4,13},{5,12},{6,15},{7,14},{8,1},{9,0},... | collective-permute-start | bytes 147464 | tf_op jit(solution)/shard_map/ppermute | solution.py:447
  20.6 4.1 %collective-permute-start.5 = (bf16[64,768]{1,0:T(8,128)(2,1)S(1)}, bf16[64,768]{1,0:T(8,128)(2,1)S(1)}, u32[]{:S(2)}, u32[]{:S(2)}) collective-permute-start(bf16[64,768]{1,0:T(8,128)(2,1)S(1)} %get-tuple-element.78.after), channel_id=1, source_target_pairs={{0,5},{1,2},{2,1},{3,6},{4,7},{5,0},{6,3},{7,4},{8,13},{9,10},{10,... | collective-permute-start | bytes 294920 | tf_op jit(solution)/shard_map/ppermute | solution.py:447
  24.8 5.2 %collective-permute-start.6 = (bf16[128,768]{1,0:T(8,128)(2,1)S(1)}, bf16[128,768]{1,0:T(8,128)(2,1)S(1)}, u32[]{:S(2)}, u32[]{:S(2)}) collective-permute-start(bf16[128,768]{1,0:T(8,128)(2,1)S(1)} %pad_maximum_fusion.1), channel_id=1, source_target_pairs={{0,3},{1,4},{2,7},{3,0},{4,1},{5,6},{6,5},{7,2},{8,11},{9,12},{10,... | collective-permute-start | bytes 589832 | tf_op jit(solution)/shard_map/ppermute | solution.py:447
  30.0 1.8 %collective-permute-start.7 = (bf16[256,768]{1,0:T(8,128)(2,1)S(1)}, bf16[256,768]{1,0:T(8,128)(2,1)S(1)}, u32[]{:S(2)}, u32[]{:S(2)}) collective-permute-start(bf16[256,768]{1,0:T(8,128)(2,1)S(1)} %pad_maximum_fusion), channel_id=1, source_target_pairs={{0,1},{1,0},{2,3},{3,2},{4,5},{5,4},{6,7},{7,6},{8,9},{9,8},{10,11... | collective-permute-start | bytes 1179656 | tf_op jit(solution)/shard_map/ppermute | solution.py:447
  31.8 7.2 %copy-start.1 = (f32[3,384]{1,0:T(4,128)S(1)}, f32[3,384]{1,0:T(4,128)}, u32[]{:S(2)}) copy-start(f32[3,384]{1,0:T(4,128)} %pos_ref.1) | copy-start | bytes 13828
  31.8 7.2 %copy-start.2 = (f32[3,384]{1,0:T(4,128)S(1)}, f32[3,384]{1,0:T(4,128)}, u32[]{:S(2)}) copy-start(f32[3,384]{1,0:T(4,128)} %noise_ref.1) | copy-start | bytes 13828
  31.8 7.2 %copy-start.3 = (bf16[3,128]{1,0:T(4,128)(2,1)S(1)}, bf16[3,128]{1,0:T(4,128)(2,1)}, u32[]{:S(2)}) copy-start(bf16[3,128]{1,0:T(4,128)(2,1)} %wpos_ref.1) | copy-start | bytes 2308
  35.0 1.2 %collective-permute-start.8 = (bf16[16,128]{1,0:T(8,128)(2,1)S(1)}, bf16[16,128]{1,0:T(8,128)(2,1)S(1)}, u32[]{:S(2)}, u32[]{:S(2)}) collective-permute-start(bf16[16,128]{1,0:T(8,128)(2,1)S(1)} %get-tuple-element.75), channel_id=1, source_target_pairs={{0,1},{1,0},{2,3},{3,2},{4,5},{5,4},{6,7},{7,6},{8,9},{9,8},{10,11... | collective-permute-start | bytes 12296 | tf_op jit(solution)/shard_map/ppermute | solution.py:427
  35.1 3.9 %collective-permute-start.9 = (bf16[16,128]{1,0:T(8,128)(2,1)S(1)}, bf16[16,128]{1,0:T(8,128)(2,1)S(1)}, u32[]{:S(2)}, u32[]{:S(2)}) collective-permute-start(bf16[16,128]{1,0:T(8,128)(2,1)S(1)} %get-tuple-element.76), channel_id=1, source_target_pairs={{1,2},{3,4},{5,6},{7,8},{9,10},{11,12},{13,14},{2,1},{4,3},{6,5},{... | collective-permute-start | bytes 12296 | tf_op jit(solution)/shard_map/ppermute | solution.py:427

commit v6 on v5

--- a/solution.py
+++ b/solution.py
@@ -179,7 +179,8 @@
     return outs
 
 
-def local_body(offsets, q_ref, k_ref, v_ref, bias_ref, att_ref):
+def local_body(offsets, q_ref, k_ref, v_ref, bias_ref, wgate_hbm, att_ref, wgate_ref, sems):
+    copies = fetch(sems, (wgate_hbm, wgate_ref))
     rows, width = q_ref.shape
     windows = rows // QWIN
     skip = BEHIND // QWIN
@@ -197,6 +198,7 @@
     )
     for a, out in zip(at, outs):
         att_ref[a, :] = out
+    copies[0].wait()
 
 
 def atoms_body(
@@ -291,112 +293,124 @@
     norm_ref[...] = normalize(token_in).astype(BF16)
 
 
-def query_body(norm_ref, wqkv_hbm, wgate_hbm, query_ref, gate_ref, wq_ref, wk_ref, wgate_ref, sems):
+def query_body(norm_ref, wqkv_ref, wgate_ref, query_ref, gate_ref):
     rows, model = norm_ref.shape
-    copies = fetch(
-        sems,
-        (wqkv_hbm.at[:, :model], wq_ref),
-        (wqkv_hbm.at[:, model : 2 * model], wk_ref),
-        (wgate_hbm, wgate_ref),
-    )
     width = model // TH
     group = TH // 2
     span = group * width
     norm = norm_ref[...]
     own = iota((group * rows, span), 0) // rows == iota((group * rows, span), 1) // width
-    copies[0].wait()
-    tq = dot(norm, wq_ref[...])
-    copies[1].wait()
+    tq = dot(norm, wqkv_ref[:, :model])
     for g in range(2):
         part = tq[:, g * span : (g + 1) * span]
         stacked = jnp.where(own, jnp.concatenate([part] * group, axis=0), 0.0).astype(BF16)
-        wk = wk_ref[:, g * span : (g + 1) * span]
+        wk = wqkv_ref[:, model + g * span : model + (g + 1) * span]
         query_ref[g * group * rows : (g + 1) * group * rows, :] = dot_nt(stacked, wk).astype(BF16)
-    copies[2].wait()
     gate_ref[...] = jax.nn.sigmoid(dot(norm, wgate_ref[...]))
 
 
 def stage_body(
+    lists,
     after,
     bias_hbm,
     mask_hbm,
-    wqkv_hbm,
     wout_hbm,
     wback_hbm,
-    bias_ref,
-    wv_ref,
+    out_ref,
     wout_ref,
     wback_ref,
+    bias_ref,
     mask_ref,
     sems,
 ):
-    model = wout_hbm.shape[0]
     copies = fetch(
-        sems,
-        (mask_hbm, mask_ref),
-        (bias_hbm, bias_ref),
-        (wqkv_hbm.at[:, 2 * model :], wv_ref),
-        (wout_hbm, wout_ref),
-        (wback_hbm, wback_ref),
+        sems, (mask_hbm, mask_ref), (bias_hbm, bias_ref), (wout_hbm, wout_ref), (wback_hbm, wback_ref)
     )
     copies[0].wait()
     copies[1].wait()
     allowed = mask_ref[...] == 1
-    for h in range(TH):
-        bias_ref[h] = jnp.where(allowed, bias_ref[h], masked_score)
+    heads, rows, keys = bias_ref.shape
+    if lists is None:
+        for h in range(heads):
+            out_ref[0, h * rows : (h + 1) * rows, :] = jnp.where(allowed, bias_ref[h], masked_score)
+    else:
+        for h in range(heads):
+            bias_ref[h] = jnp.where(allowed, bias_ref[h], masked_score)
+        me = lax.axis_index("row")
+        kind = kind_of(me)
+        per = 128 // rows
+        lane_block = iota((heads * rows, 128), 1) // rows
+        for c in range(len(lists[0])):
+            for tile in range(len(lists[0][c]) // per):
+                for j in range(per):
+                    n = tile * per + j
+                    block = me ^ jnp.where(kind == 0, lists[0][c][n], lists[1][c][n])
+                    source = pl.ds(pl.multiple_of((block // per) * 128, 128), 128)
+                    piece = bias_ref[:, :, source].reshape(heads * rows, 128)
+                    piece = pltpu.roll(piece, ((j + per - block % per) % per) * rows, 1)
+                    merged = piece if j == 0 else jnp.where(lane_block == j, piece, merged)
+                out_ref[c, :, tile * 128 : (tile + 1) * 128] = merged
     for copy in copies[2:]:
         copy.wait()
 
 
+def part_of(rows, query_ref, keys_ref, bias, wqkv_ref):
+    model = query_ref.shape[1]
+    width = model // TH
+    group = TH // 2
+    span = group * width
+    keys = keys_ref[...]
+    values = dot(keys, wqkv_ref[:, 2 * model :]).astype(BF16)
+    lane_head = iota((rows, span), 1) // width
+
+    def by_head(stacked):
+        out = jnp.broadcast_to(stacked[:rows], (rows, span))
+        for h in range(1, group):
+            out = jnp.where(lane_head == h, stacked[h * rows : (h + 1) * rows], out)
+        return out
+
+    found = []
+    for g in range(2):
+        at = slice(g * group * rows, (g + 1) * group * rows)
+        scores = dot_nt(query_ref[at, :], keys) * (1.0 / width**0.5) + bias(at)
+        top = jnp.max(scores, axis=-1, keepdims=True)
+        scores = jnp.exp(scores - top)
+        total = jnp.sum(scores, axis=-1, keepdims=True)
+        mixed = dot(scores.astype(BF16), values[:, g * span : (g + 1) * span])
+        found.append((by_head(top), by_head(total), by_head(mixed)))
+    return [jnp.concatenate([found[0][n], found[1][n]], axis=1) for n in range(3)]
+
+
+def part_body(chunk, query_ref, keys_ref, bias_ref, wqkv_ref, part_ref):
+    found = part_of(part_ref.shape[1], query_ref, keys_ref, lambda at: bias_ref[chunk, at, :], wqkv_ref)
+    for n in range(3):
+        part_ref[n] = found[n]
+
+
 def attend_body(
-    orders,
     half,
+    chunk,
     in_ref,
     query_ref,
     gate_ref,
-    all_ref,
+    keys_ref,
     bias_ref,
-    wv_ref,
+    wqkv_ref,
     wout_ref,
     wback_ref,
-    out_ref,
-    back_ref,
-    pair_out,
-    odd_out,
-    sorted_ref,
+    *rest,
 ):
+    parts, (out_ref, back_ref, pair_out, odd_out) = rest[:-4], rest[-4:]
     rows, model = in_ref.shape
-    keys = all_ref.shape[0]
-    me = lax.axis_index("row")
-    even = me % 2 == 0
-    kind = (me ^ (me >> 1) ^ (me >> 2)) & 1
-    if orders is None:
-        sorted_ref[...] = all_ref[...]
-    else:
-        for j in range(keys // rows):
-            block = me ^ jnp.where(kind == 0, orders[0][j], orders[1][j])
-            sorted_ref[pl.ds(pl.multiple_of(block * rows, rows), rows), :] = all_ref[j * rows : (j + 1) * rows, :]
-    width = model // TH
-    group = TH // 2
-    span = group * width
-    scale = 1.0 / width**0.5
-    values = sorted_ref[...]
-    lane_head = iota((rows, span), 1) // width
-    for g in range(2):
-        at = slice(g * group * rows, (g + 1) * group * rows)
-        bias = bias_ref[g * group : (g + 1) * group].reshape(group * rows, keys)
-        scores = dot_nt(query_ref[at, :], values) * scale + bias
-        scores = jnp.exp(scores - jnp.max(scores, axis=-1, keepdims=True))
-        weights = (scores * (1.0 / jnp.sum(scores, axis=-1, keepdims=True))).astype(BF16)
-        mixed = dot(weights, values).astype(BF16)
-        wide = dot(mixed, wv_ref[:, g * span : (g + 1) * span])
-        part = wide[:rows]
-        for h in range(1, group):
-            part = jnp.where(lane_head == h, wide[h * rows : (h + 1) * rows], part)
-        gated = (gate_ref[:, g * span : (g + 1) * span] * part).astype(BF16)
-        added = dot(gated, wout_ref[g * span : (g + 1) * span, :])
-        total = added if g == 0 else total + added
-    token_out = (in_ref[...] + total).astype(BF16)
+    even = lax.axis_index("row") % 2 == 0
+    found = part_of(rows, query_ref, keys_ref, lambda at: bias_ref[chunk, at, :], wqkv_ref)
+    found = [[part[n] for n in range(3)] for part in parts] + [found]
+    top = functools.reduce(jnp.maximum, [f[0] for f in found])
+    shares = [jnp.exp(f[0] - top) for f in found]
+    total = sum(f[1] * w for f, w in zip(found, shares))
+    mixed = sum(f[2] * w for f, w in zip(found, shares))
+    gated = (gate_ref[...] * (mixed / total)).astype(BF16)
+    token_out = (in_ref[...] + dot(gated, wout_ref[...])).astype(BF16)
     out_ref[...] = token_out
     back = dot(token_out, wback_ref[...])
     back_ref[...] = back.astype(BF16)
@@ -434,22 +448,19 @@
 def gather_plan(count):
     bits = [1 << b for b in range(count.bit_length() - 1, 0, -1) if 1 << b < count]
     steps = [[b | 1, b | 1] for b in bits]
-    if len(bits) > 1:
-        high, low = bits[-2] | 1, bits[-1] | 1
-        steps[-2:] = [[high, low], [low, high]]
-    return steps + [[1, 1]]
-
-
-def gather(norm, count, between):
-    orders = [[0], [0]]
-    for n, step in enumerate(gather_plan(count)):
-        perm = [(i, i ^ step[kind_of(i)]) for i in range(count)]
-        arrived = lax.ppermute(norm, "row", perm)
-        if n < len(between):
-            arrived, between[n] = lax.optimization_barrier((arrived, between[n](n, norm)))
-        norm = jnp.concatenate([norm, arrived], axis=0)
-        orders = [orders[p] + [x ^ step[p] for x in orders[kind_of(p ^ step[p])]] for p in range(2)]
-    return norm, orders, between
+    high, low = bits[-2] | 1, bits[-1] | 1
+    steps[-2:] = [[high, low], [low, high]]
+    lists = [[0], [0]]
+    for step in steps[:-1]:
+        lists = [lists[p] + [x ^ step[p] for x in lists[p ^ kind_of(step[p])]] for p in range(2)]
+    near = [[1 ^ x for x in lists[1 - p]] for p in range(2)]
+    last = [[x ^ steps[-1][p] for x in lists[p]] for p in range(2)]
+    end = [[1 ^ x for x in last[1 - p]] for p in range(2)]
+    return steps, [[lists[p], near[p], last[p], end[p]] for p in range(2)]
+
+
+def swap(value, count, step):
+    return lax.ppermute(value, "row", [(i, i ^ step[kind_of(i)]) for i in range(count)])
 
 
 def on_device(
@@ -521,13 +532,14 @@
         w_agg,
     )
     pair, odd = exchange(pair, odd, groups, count)
-    (att,) = call(
+    att, wgate = call(
         local_body,
-        [shape((rows, width), BF16)],
+        [shape((rows, width), BF16), shape(w_tok_gate.shape, BF16)],
         "local",
-        [SMEM] + [VMEM] * 4,
+        [SMEM] + [VMEM] * 4 + [HBM],
+        [pltpu.SemaphoreType.DMA((1,))],
         flops=10**9,
-    )(offsets, q, keys, values, bias)
+    )(offsets, q, keys, values, bias, w_tok_gate)
     packed = model + 128
     mid, own, pair, odd, hot, living = call(
         functools.partial(atoms_body, half),
@@ -551,40 +563,69 @@
         [VMEM] * 4,
     )(own, pair, odd, token_single)
 
-    def query(n, seen):
+    doubling = count & (count - 1) == 0 and count >= 16 and 128 % block_rows == 0
+    steps, lists = gather_plan(count) if doubling else ([], None)
+    chunks = 4 if doubling else 1
+    span = count * block_rows // chunks
+
+    def query(seen):
         return call(
             query_body,
             [shape((TH * block_rows, model), BF16), shape((block_rows, model), F32)],
             "query",
-            [VMEM, HBM, HBM],
-            [pltpu.VMEM((model, model), BF16)] * 3 + [pltpu.SemaphoreType.DMA((3,))],
+            [VMEM, VMEM, VMEM],
             flops=10**9,
-            limit=10,
-        )(norm, w_tok_qkv, w_tok_gate)
-
-    def stage(n, seen):
+        )(seen, w_tok_qkv, wgate)
+
+    def stage(seen):
         return call(
-            stage_body,
+            functools.partial(stage_body, lists),
             [
-                shape(token_bias.shape, F32),
-                shape((model, model), BF16),
-                shape((model, model), BF16),
+                shape((chunks, TH * block_rows, span), F32),
+                shape(w_tok_out.shape, BF16),
                 shape(w_back.shape, BF16),
             ],
             "stage",
-            [VMEM] + [HBM] * 5,
-            [pltpu.VMEM(pair_mask.shape, jnp.int32), pltpu.SemaphoreType.DMA((5,))],
+            [VMEM] + [HBM] * 4,
+            [
+                pltpu.VMEM(token_bias.shape, F32),
+                pltpu.VMEM(pair_mask.shape, jnp.int32),
+                pltpu.SemaphoreType.DMA((4,)),
+            ],
             flops=10**9,
-        )(seen, token_bias, pair_mask, w_tok_qkv, w_tok_out, w_back)
-
-    if count & (count - 1) or count < 8:
-        everyone, orders = lax.all_gather(norm, "row", axis=0, tiled=True), None
-        between = [query(0, norm), stage(1, norm)]
+        )(seen, token_bias, pair_mask, w_tok_out, w_back)
+
+    def part(chunk, seen):
+        return call(
+            functools.partial(part_body, chunk),
+            [shape((3, block_rows, model), F32)],
+            "part",
+            [VMEM] * 4,
+            flops=10**9,
+        )(query_rows, seen, score_bias, w_tok_qkv)[0]
+
+    if doubling:
+        held = norm
+        for n, step in enumerate(steps[:-1]):
+            arrived = swap(held, count, step)
+            if n == 0:
+                arrived, (query_rows, gate) = lax.optimization_barrier((arrived, query(norm)))
+            if n == 1:
+                arrived, (score_bias, wout, wback) = lax.optimization_barrier((arrived, stage(held)))
+            held = jnp.concatenate([held, arrived], axis=0)
+        last = swap(held, count, steps[-1])
+        near = swap(held, count, [1, 1])
+        parts = [part(0, held), part(1, near)]
+        last, parts = lax.optimization_barrier((last, parts))
+        end = swap(last, count, [1, 1])
+        parts = parts + [part(2, last)]
     else:
-        everyone, orders, between = gather(norm, count, [query, stage])
-    (query_rows, gate), (bias, wv, wout, wback) = between
+        end = lax.all_gather(norm, "row", axis=0, tiled=True)
+        query_rows, gate = query(norm)
+        score_bias, wout, wback = stage(norm)
+        parts = []
     token_out, back, pair, odd = call(
-        functools.partial(attend_body, orders, half),
+        functools.partial(attend_body, half, chunks - 1),
         [
             shape((block_rows, model), BF16),
             shape((block_rows, width), BF16),
@@ -592,9 +633,8 @@
             shape((half, width), BF16),
         ],
         "attend",
-        [VMEM] * 8,
-        [pltpu.VMEM((count * block_rows, model), BF16)],
-    )(token_in, query_rows, gate, everyone, bias, wv, wout, wback)
+        [VMEM] * (8 + len(parts)),
+    )(token_in, query_rows, gate, end, score_bias, w_tok_qkv, wout, wback, *parts)
     pair, odd = exchange(pair, odd, groups, count)
     (denoised,) = call(
         final_body,

time: 40.9 us -> 39.4 us (0.963)
  waiting for transfers between devices: 20.5 us -> 16.6 us
  Pallas kernels: 14.5 us -> 16.6 us
  starting transfers between devices: 3.58 us -> 4.34 us
    ppermute x4 -> x5, waiting for transfers between devices: 11.8 us -> 8.83 us  [swap(): lax.ppermute(value, 'row', [(i, i ^ step[kind_of(i)]) for i in range(coun...]
    pallas_call x8 -> x11, Pallas kernels: 14.5 us -> 16.6 us  [call(): run(*[pltpu.with_memory_space_constraint(x, pltpu.HBM) if h and x.size >...]
    ppermute x3, waiting for transfers between devices: 7.59 us -> 6.84 us  [exchange(): lax.ppermute(odd, ('grp', 'row'), far)]
    ppermute x4 -> x5, starting transfers between devices: 0.39 us -> 1.01 us  [swap(): lax.ppermute(value, 'row', [(i, i ^ step[kind_of(i)]) for i in range(coun...]
  transfers between devices with their start and end apart: 10 -> 11, of which waited for: 8 -> 7; matrix products, arithmetic and copies ran while one was open for 0% -> 0% of each run, Pallas kernels for 15% -> 23%
where the time goes in v6:
time: 39.4 us; the launch traced here: 39 us
  Pallas kernels  16.6 us (42%)
  waiting for transfers between devices  16.6 us (42%)
  starting transfers between devices  4.34 us (11%)
  between operations  1.45 us (4%)
    pallas_call x11, Pallas kernels, call(): run(*[pltpu.with_memory_space_constraint(x, pltpu.HBM) if h and x.size >...  16.6 us
    ppermute x5, waiting for transfers between devices, swap(): lax.ppermute(value, 'row', [(i, i ^ step[kind_of(i)]) for i in range(coun...  8.83 us
    ppermute x3, waiting for transfers between devices, exchange(): lax.ppermute(odd, ('grp', 'row'), far)  6.84 us
    ppermute x3, starting transfers between devices, exchange(): lax.ppermute(odd, ('grp', 'row'), far)  2.91 us
    ppermute x5, starting transfers between devices, swap(): lax.ppermute(value, 'row', [(i, i ^ step[kind_of(i)]) for i in range(coun...  1.01 us
    ppermute x3, waiting for transfers between devices, exchange(): lax.ppermute(pair, 'row', near)  0.91 us
  transfers between devices with their start and end apart: 11, of which 7 were waited for; matrix products, arithmetic and copies ran while one was open for 0% of the time, Pallas kernels for 23%

profile of v6, /device:TPU:24, one launch (start us, length us, event | category | flops | bytes accessed | tf_op | source)
XLA Modules:
  0.0 39.0 jit_solution(2633827498419854363)
XLA Ops:
  1.3 2.3 %embed.1 = (s32[8]{0:T(128)S(1)}, f32[384,128]{1,0:T(8,128)S(1)}, bf16[384,128]{1,0:T(8,128)(2,1)S(1)}, f32[480,128]{1,0:T(8,128)S(1)}, f32[480,128]{1,0:T(8,128...) custom-call(s32[1,1]{1,0:T(1,128)} %bitcast.2.counts_hbm, ...), custom_call_target="tpu_custom_call" | custom-call | flops 10000000 | bytes 1902160 | tf_op jit(solution)/shard_map/embed/pallas_call | solution.py:64
  3.7 1.5 %collective-permute-start.1 = (bf16[96,256]{1,0:T(8,128)(2,1)S(1)}, bf16[96,256]{1,0:T(8,128)(2,1)S(1)}, u32[]{:S(2)}, u32[]{:S(2)}) collective-permute-start(bf16[96,256]{1,0:T(8,128)(2,1)S(1)} %get-tuple-element.51), channel_id=1, source_target_pairs={{1,2},{3,4},{5,6},{7,8},{9,10},{11,12},{13,14},{2,1},{4,3},{6,5},{... | collective-permute-start | bytes 147464 | tf_op jit(solution)/shard_map/ppermute | solution.py:441
  5.2 2.1 %local.1 = (bf16[384,128]{1,0:T(8,128)(2,1)S(1)}, bf16[768,768]{1,0:T(8,128)(2,1)S(1)}) custom-call(s32[1,12]{1,0:T(1,128)S(1)} %get-tuple-element.44.offsets, bf16[384,128]{1,0:T(8,128)(2,1)S(1)} %get-tuple-element.47.q_ref, f32[480,128]{1,0:T(8,128)S(1)} %get-tuple-element.48.k_ref, f32[480,128]{1,0:T(8,128)S(1)} %get-tuple-element.49.v_ref, ...), custom_call_target="tpu_custom_call" | custom-call | flops 1000000000 | bytes 1277952 | tf_op jit(solution)/shard_map/local/pallas_call | solution.py:64
  7.3 0.9 %collective-permute-done.1.odd_ref = bf16[96,256]{1,0:T(8,128)(2,1)S(1)} collective-permute-done((bf16[96,256]{1,0:T(8,128)(2,1)S(1)}, bf16[96,256]{1,0:T(8,128)(2,1)S(1)}, u32[]{:S(2)}, u32[]{:S(2)}) %collective-permute-start.1) | collective-permute-done | bytes 49184 | tf_op jit(solution)/shard_map/ppermute | solution.py:441
  8.3 1.7 %atoms.1 = (f32[384,128]{1,0:T(8,128)S(1)}, f32[32,896]{1,0:T(8,128)S(1)}, bf16[16,896]{1,0:T(8,128)(2,1)S(1)}, bf16[16,896]{1,0:T(8,128)(2,1)S(1)}, bf16[384,64]{1,0:T(8,128)(2,1)S(1)}, /*index=5*/f32[1,384]{1,0:T(1,128)S(1)}) custom-call(s32[8]{0:T(128)S(1)} %get-tuple-element.43.info, s32[1,12]{1,0:T(1,128)S(1)} %get-tuple-element.44.offsets, ...), custom_call_target="tpu_custom_call" | custom-call | flops 10000000 | bytes 419328 | tf_op jit(solution)/shard_map/atoms/pallas_call | solution.py:64
  10.1 1.4 %collective-permute-start.3 = (bf16[16,896]{1,0:T(8,128)(2,1)S(1)}, bf16[16,896]{1,0:T(8,128)(2,1)S(1)}, u32[]{:S(2)}, u32[]{:S(2)}) collective-permute-start(bf16[16,896]{1,0:T(8,128)(2,1)S(1)} %get-tuple-element.61), channel_id=1, source_target_pairs={{1,2},{3,4},{5,6},{7,8},{9,10},{11,12},{13,14},{2,1},{4,3},{6,5},{... | collective-permute-start | bytes 86024 | tf_op jit(solution)/shard_map/ppermute | solution.py:441
  11.5 2.9 %collective-permute-done.3.odd_ref = bf16[16,896]{1,0:T(8,128)(2,1)S(1)} collective-permute-done((bf16[16,896]{1,0:T(8,128)(2,1)S(1)}, bf16[16,896]{1,0:T(8,128)(2,1)S(1)}, u32[]{:S(2)}, u32[]{:S(2)}) %collective-permute-start.3) | collective-permute-done | bytes 28704 | tf_op jit(solution)/shard_map/ppermute | solution.py:441
  14.4 0.3 token_.1
  14.8 1.0 %query.1 = (bf16[512,768]{1,0:T(8,128)(2,1)S(1)}, f32[32,768]{1,0:T(8,128)S(1)}) custom-call(bf16[32,768]{1,0:T(8,128)(2,1)S(1)} %get-tuple-element.63.norm_ref, bf16[768,2304]{1,0:T(8,128)(2,1)S(1)} %copy-done, bf16[768,768]{1,0:T(8,128)(2,1)S(1)} %get-tuple-element.64.wgate_ref), custom_call_target="tpu_custom_call" | custom-call | flops 1000000000 | bytes 884736 | tf_op jit(solution)/shard_map/query/pallas_call | solution.py:64
  15.8 4.9 %collective-permute-done.4 = bf16[32,768]{1,0:T(8,128)(2,1)S(1)} collective-permute-done((bf16[32,768]{1,0:T(8,128)(2,1)S(1)}, bf16[32,768]{1,0:T(8,128)(2,1)S(1)}, u32[]{:S(2)}, u32[]{:S(2)}) %collective-permute-start.4) | collective-permute-done | bytes 49184 | tf_op jit(solution)/shard_map/ppermute | solution.py:463
  20.7 2.6 %stage.1 = (f32[4,512,128]{2,1,0:T(8,128)S(1)}, bf16[768,768]{1,0:T(8,128)(2,1)S(1)}, bf16[768,128]{1,0:T(8,128)(2,1)S(1)}) custom-call(bf16[64,768]{1,0:T(8,128)(2,1)S(1)} %get-tuple-element.84.after, f32[16,32,512]{2,1,0:T(8,128)} %bias_hbm.3, s32[32,512]{1,0:T(8,128)} %mask_hbm.1, bf16[768,768]{1,0:T(8,128)(2,1)} %wout_hbm.3, bf16[768,128]{1,0:T(8,128)(2,1)} %wback_hbm.1), custom_call_target="tpu_custom_call" | custom-call | flops 1000000000 | bytes 2424832 | tf_op jit(solution)/shard_map/stage/pallas_call | solution.py:64
  23.3 1.4 %collective-permute-done.5 = bf16[64,768]{1,0:T(8,128)(2,1)S(1)} collective-permute-done((bf16[64,768]{1,0:T(8,128)(2,1)S(1)}, bf16[64,768]{1,0:T(8,128)(2,1)S(1)}, u32[]{:S(2)}, u32[]{:S(2)}) %collective-permute-start.5) | collective-permute-done | bytes 98336 | tf_op jit(solution)/shard_map/ppermute | solution.py:463
  24.8 0.2 collective-permute-start.7
  24.9 0.3 collective-permute-start.6
  25.2 1.1 %part.3.rest_0_ = f32[3,32,768]{2,1,0:T(8,128)S(1)} custom-call(bf16[512,768]{1,0:T(8,128)(2,1)S(1)} %get-tuple-element.67.query_ref, bf16[128,768]{1,0:T(8,128)(2,1)S(1)} %constant_dynamic-update-slice_fusion.2.keys_ref, f32[4,512,128]{2,1,0:T(8,128)S(1)} %get-tuple-element.74.bias_ref, bf16[768,2304]{1,0:T(8,128)(2,1)S(1)} %copy-done), custom_call_target="tpu_custom_call" | custom-call | flops 1000000000 | bytes 294912 | tf_op jit(solution)/shard_map/part/pallas_call | solution.py:64
  26.4 1.1 %part.4.rest_1_ = f32[3,32,768]{2,1,0:T(8,128)S(1)} custom-call(bf16[512,768]{1,0:T(8,128)(2,1)S(1)} %get-tuple-element.67.query_ref, bf16[128,768]{1,0:T(8,128)(2,1)S(1)} %collective-permute-done.7.keys_ref, f32[4,512,128]{2,1,0:T(8,128)S(1)} %get-tuple-element.74.bias_ref, bf16[768,2304]{1,0:T(8,128)(2,1)S(1)} %copy-done), custom_call_target="tpu_custom_call" | custom-call | flops 1000000000 | bytes 294912 | tf_op jit(solution)/shard_map/part/pallas_call | solution.py:64
  27.5 2.5 %collective-permute-done.6.keys_ref = bf16[128,768]{1,0:T(8,128)(2,1)S(1)} collective-permute-done((bf16[128,768]{1,0:T(8,128)(2,1)S(1)}, bf16[128,768]{1,0:T(8,128)(2,1)S(1)}, u32[]{:S(2)}, u32[]{:S(2)}) %collective-permute-start.6) | collective-permute-done | bytes 196640 | tf_op jit(solution)/shard_map/ppermute | solution.py:463
  30.0 0.4 %collective-permute-start.8 = (bf16[128,768]{1,0:T(8,128)(2,1)S(1)}, bf16[128,768]{1,0:T(8,128)(2,1)S(1)}, u32[]{:S(2)}, u32[]{:S(2)}) collective-permute-start(bf16[128,768]{1,0:T(8,128)(2,1)S(1)} %collective-permute-done.6.keys_ref), channel_id=1, source_target_pairs={{0,1},{1,0},{2,3},{3,2},{4,5},{5,4},{6,7},{7,6},{8,9},{9,8},{10,11... | collective-permute-start | bytes 589832 | tf_op jit(solution)/shard_map/ppermute | solution.py:463
  30.4 1.1 %part.5.rest_2_ = f32[3,32,768]{2,1,0:T(8,128)S(1)} custom-call(bf16[512,768]{1,0:T(8,128)(2,1)S(1)} %get-tuple-element.67.query_ref, bf16[128,768]{1,0:T(8,128)(2,1)S(1)} %collective-permute-done.6.keys_ref, f32[4,512,128]{2,1,0:T(8,128)S(1)} %get-tuple-element.74.bias_ref, bf16[768,2304]{1,0:T(8,128)(2,1)S(1)} %copy-done), custom_call_target="tpu_custom_call" | custom-call | flops 1000000000 | bytes 294912 | tf_op jit(solution)/shard_map/part/pallas_call | solution.py:64
  31.6 2.1 %attend.1 = (bf16[32,768]{1,0:T(8,128)(2,1)}, bf16[32,128]{1,0:T(8,128)(2,1)S(1)}, bf16[16,128]{1,0:T(8,128)(2,1)S(1)}, bf16[16,128]{1,0:T(8,128)(2,1)S(1)}) custom-call(f32[32,768]{1,0:T(8,128)S(1)} %get-tuple-element.62.in_ref, bf16[512,768]{1,0:T(8,128)(2,1)S(1)} %get-tuple-element.67.query_ref, f32[32,768]{1,0:T(8,128)S(1)} %get-tuple-element.68.gate_ref, ...), custom_call_target="tpu_custom_call" | custom-call | flops 10000000 | bytes 65536 | tf_op jit(solution)/shard_map/attend/pallas_call | solution.py:64
  33.7 0.3 collective-permute-start.9
  34.0 0.9 %collective-permute-done.9.pair_ref = bf16[16,128]{1,0:T(8,128)(2,1)S(1)} collective-permute-done((bf16[16,128]{1,0:T(8,128)(2,1)S(1)}, bf16[16,128]{1,0:T(8,128)(2,1)S(1)}, u32[]{:S(2)}, u32[]{:S(2)}) %collective-permute-start.9) | collective-permute-done | bytes 4128 | tf_op jit(solution)/shard_map/ppermute | solution.py:441
  34.9 3.0 %collective-permute-done.10.odd_ref = bf16[16,128]{1,0:T(8,128)(2,1)S(1)} collective-permute-done((bf16[16,128]{1,0:T(8,128)(2,1)S(1)}, bf16[16,128]{1,0:T(8,128)(2,1)S(1)}, u32[]{:S(2)}, u32[]{:S(2)}) %collective-permute-start.10) | collective-permute-done | bytes 4128 | tf_op jit(solution)/shard_map/ppermute | solution.py:441
  37.9 1.1 %final.1 = f32[3,384]{1,0:T(4,128)} custom-call(f32[1,384]{1,0:T(1,128)S(1)} %get-tuple-element.56.living_ref, bf16[384,64]{1,0:T(8,128)(2,1)S(1)} %get-tuple-element.57.hot_ref, f32[384,128]{1,0:T(8,128)S(1)} %get-tuple-element.58.mid_ref, bf16[32,128]{1,0:T(8,128)(2,1)S(1)} %get-tuple-element.80.back_ref, ...), custom_call_target="tpu_custom_call" | custom-call | flops 10000000 | bytes 4608 | tf_op jit(solution)/shard_map/final/pallas_call | solution.py:64
  (22 shorter events, 0.4 us)
Async XLA Ops:
  3.6 3.7 %collective-permute-start = (bf16[96,256]{1,0:T(8,128)(2,1)S(1)}, bf16[96,256]{1,0:T(8,128)(2,1)S(1)}, u32[]{:S(2)}, u32[]{:S(2)}) collective-permute-start(bf16[96,256]{1,0:T(8,128)(2,1)S(1)} %get-tuple-element.50), channel_id=1, source_target_pairs={{0,1},{1,0},{2,3},{3,2},{4,5},{5,4},{6,7},{7,6},{8,9},{9,8},{10,11... | collective-permute-start | bytes 147464 | tf_op jit(solution)/shard_map/ppermute | solution.py:441
  3.7 4.6 %collective-permute-start.1 = (bf16[96,256]{1,0:T(8,128)(2,1)S(1)}, bf16[96,256]{1,0:T(8,128)(2,1)S(1)}, u32[]{:S(2)}, u32[]{:S(2)}) collective-permute-start(bf16[96,256]{1,0:T(8,128)(2,1)S(1)} %get-tuple-element.51), channel_id=1, source_target_pairs={{1,2},{3,4},{5,6},{7,8},{9,10},{11,12},{13,14},{2,1},{4,3},{6,5},{... | collective-permute-start | bytes 147464 | tf_op jit(solution)/shard_map/ppermute | solution.py:441
  5.2 9.6 %copy-start = (bf16[768,2304]{1,0:T(8,128)(2,1)S(1)}, bf16[768,2304]{1,0:T(8,128)(2,1)}, u32[]{:S(2)}) copy-start(bf16[768,2304]{1,0:T(8,128)(2,1)} %wqkv_ref.9) | copy-start | bytes 10616836
  7.3 7.0 %copy-start.1 = (bf16[32,768]{1,0:T(8,128)(2,1)S(1)}, bf16[32,768]{1,0:T(8,128)(2,1)}, u32[]{:S(2)}) copy-start(bf16[32,768]{1,0:T(8,128)(2,1)} %single_ref.1) | copy-start | bytes 147460
  10.0 1.5 %collective-permute-start.2 = (bf16[16,896]{1,0:T(8,128)(2,1)S(1)}, bf16[16,896]{1,0:T(8,128)(2,1)S(1)}, u32[]{:S(2)}, u32[]{:S(2)}) collective-permute-start(bf16[16,896]{1,0:T(8,128)(2,1)S(1)} %get-tuple-element.60), channel_id=1, source_target_pairs={{0,1},{1,0},{2,3},{3,2},{4,5},{5,4},{6,7},{7,6},{8,9},{9,8},{10,11... | collective-permute-start | bytes 86024 | tf_op jit(solution)/shard_map/ppermute | solution.py:441
  10.1 4.3 %collective-permute-start.3 = (bf16[16,896]{1,0:T(8,128)(2,1)S(1)}, bf16[16,896]{1,0:T(8,128)(2,1)S(1)}, u32[]{:S(2)}, u32[]{:S(2)}) collective-permute-start(bf16[16,896]{1,0:T(8,128)(2,1)S(1)} %get-tuple-element.61), channel_id=1, source_target_pairs={{1,2},{3,4},{5,6},{7,8},{9,10},{11,12},{13,14},{2,1},{4,3},{6,5},{... | collective-permute-start | bytes 86024 | tf_op jit(solution)/shard_map/ppermute | solution.py:441
  14.7 5.9 %collective-permute-start.4 = (bf16[32,768]{1,0:T(8,128)(2,1)S(1)}, bf16[32,768]{1,0:T(8,128)(2,1)S(1)}, u32[]{:S(2)}, u32[]{:S(2)}) collective-permute-start(bf16[32,768]{1,0:T(8,128)(2,1)S(1)} %get-tuple-element.63.norm_ref), channel_id=1, source_target_pairs={{0,9},{1,8},{2,11},{3,10},{4,13},{5,12},{6,15},{7,14},{8,1},{9,0},... | collective-permute-start | bytes 147464 | tf_op jit(solution)/shard_map/ppermute | solution.py:463
  20.6 4.1 %collective-permute-start.5 = (bf16[64,768]{1,0:T(8,128)(2,1)S(1)}, bf16[64,768]{1,0:T(8,128)(2,1)S(1)}, u32[]{:S(2)}, u32[]{:S(2)}) collective-permute-start(bf16[64,768]{1,0:T(8,128)(2,1)S(1)} %get-tuple-element.84.after), channel_id=1, source_target_pairs={{0,5},{1,2},{2,1},{3,6},{4,7},{5,0},{6,3},{7,4},{8,13},{9,10},{10,... | collective-permute-start | bytes 294920 | tf_op jit(solution)/shard_map/ppermute | solution.py:463
  24.8 1.6 %collective-permute-start.7 = (bf16[128,768]{1,0:T(8,128)(2,1)S(1)}, bf16[128,768]{1,0:T(8,128)(2,1)S(1)}, u32[]{:S(2)}, u32[]{:S(2)}) collective-permute-start(bf16[128,768]{1,0:T(8,128)(2,1)S(1)} %constant_dynamic-update-slice_fusion.2.keys_ref), channel_id=1, source_target_pairs={{0,1},{1,0},{2,3},{3,2},{4,5},{5,4},{6,7},{7,6},{8,9},{9,8},{10,11... | collective-permute-start | bytes 589832 | tf_op jit(solution)/shard_map/ppermute | solution.py:463
  24.9 5.1 %collective-permute-start.6 = (bf16[128,768]{1,0:T(8,128)(2,1)S(1)}, bf16[128,768]{1,0:T(8,128)(2,1)S(1)}, u32[]{:S(2)}, u32[]{:S(2)}) collective-permute-start(bf16[128,768]{1,0:T(8,128)(2,1)S(1)} %constant_dynamic-update-slice_fusion.2.keys_ref), channel_id=1, source_target_pairs={{0,3},{1,4},{2,7},{3,0},{4,1},{5,6},{6,5},{7,2},{8,11},{9,12},{10,... | collective-permute-start | bytes 589832 | tf_op jit(solution)/shard_map/ppermute | solution.py:463
  30.0 1.5 %collective-permute-start.8 = (bf16[128,768]{1,0:T(8,128)(2,1)S(1)}, bf16[128,768]{1,0:T(8,128)(2,1)S(1)}, u32[]{:S(2)}, u32[]{:S(2)}) collective-permute-start(bf16[128,768]{1,0:T(8,128)(2,1)S(1)} %collective-permute-done.6.keys_ref), channel_id=1, source_target_pairs={{0,1},{1,0},{2,3},{3,2},{4,5},{5,4},{6,7},{7,6},{8,9},{9,8},{10,11... | collective-permute-start | bytes 589832 | tf_op jit(solution)/shard_map/ppermute | solution.py:463
  31.6 6.3 %copy-start.2 = (f32[3,384]{1,0:T(4,128)S(1)}, f32[3,384]{1,0:T(4,128)}, u32[]{:S(2)}) copy-start(f32[3,384]{1,0:T(4,128)} %pos_ref.1) | copy-start | bytes 13828
  31.6 6.3 %copy-start.3 = (f32[3,384]{1,0:T(4,128)S(1)}, f32[3,384]{1,0:T(4,128)}, u32[]{:S(2)}) copy-start(f32[3,384]{1,0:T(4,128)} %noise_ref.1) | copy-start | bytes 13828
  31.6 6.3 %copy-start.4 = (bf16[3,128]{1,0:T(4,128)(2,1)S(1)}, bf16[3,128]{1,0:T(4,128)(2,1)}, u32[]{:S(2)}) copy-start(bf16[3,128]{1,0:T(4,128)(2,1)} %wpos_ref.1) | copy-start | bytes 2308
  33.7 1.2 %collective-permute-start.9 = (bf16[16,128]{1,0:T(8,128)(2,1)S(1)}, bf16[16,128]{1,0:T(8,128)(2,1)S(1)}, u32[]{:S(2)}, u32[]{:S(2)}) collective-permute-start(bf16[16,128]{1,0:T(8,128)(2,1)S(1)} %get-tuple-element.81), channel_id=1, source_target_pairs={{0,1},{1,0},{2,3},{3,2},{4,5},{5,4},{6,7},{7,6},{8,9},{9,8},{10,11... | collective-permute-start | bytes 12296 | tf_op jit(solution)/shard_map/ppermute | solution.py:441
  34.0 3.9 %collective-permute-start.10 = (bf16[16,128]{1,0:T(8,128)(2,1)S(1)}, bf16[16,128]{1,0:T(8,128)(2,1)S(1)}, u32[]{:S(2)}, u32[]{:S(2)}) collective-permute-start(bf16[16,128]{1,0:T(8,128)(2,1)S(1)} %get-tuple-element.82), channel_id=1, source_target_pairs={{1,2},{3,4},{5,6},{7,8},{9,10},{11,12},{13,14},{2,1},{4,3},{6,5},{... | collective-permute-start | bytes 12296 | tf_op jit(solution)/shard_map/ppermute | solution.py:441

commit v7 on v6

--- a/solution.py
+++ b/solution.py
@@ -48,7 +48,7 @@
 HBM = pl.BlockSpec(memory_space=pltpu.HBM)
 
 
-def call(body, outs, name, specs, scratch=(), flops=10**7, limit=8, out_specs=None):
+def call(body, outs, specs, scratch=(), flops=10**7, limit=8, out_specs=None):
     moved = sum(o.size * o.dtype.itemsize for o in outs)
     held = [spec is HBM for spec in specs]
     run = pl.pallas_call(
@@ -57,7 +57,6 @@
         in_specs=specs,
         out_specs=tuple(out_specs or [VMEM] * len(outs)),
         scratch_shapes=list(scratch),
-        name=name,
         cost_estimate=pl.CostEstimate(flops=flops, bytes_accessed=moved, transcendentals=0),
         compiler_params=pltpu.CompilerParams(vmem_limit_bytes=limit * 2**20),
     )
@@ -179,8 +178,7 @@
     return outs
 
 
-def local_body(offsets, q_ref, k_ref, v_ref, bias_ref, wgate_hbm, att_ref, wgate_ref, sems):
-    copies = fetch(sems, (wgate_hbm, wgate_ref))
+def local_body(offsets, q_ref, k_ref, v_ref, bias_ref, att_ref):
     rows, width = q_ref.shape
     windows = rows // QWIN
     skip = BEHIND // QWIN
@@ -198,7 +196,6 @@
     )
     for a, out in zip(at, outs):
         att_ref[a, :] = out
-    copies[0].wait()
 
 
 def atoms_body(
@@ -293,7 +290,15 @@
     norm_ref[...] = normalize(token_in).astype(BF16)
 
 
-def query_body(norm_ref, wqkv_ref, wgate_ref, query_ref, gate_ref):
+def weights_body(after, wgate_hbm, wout_hbm, wback_hbm, wgate_ref, wout_ref, wback_ref, both_ref, sems):
+    copies = fetch(sems, (wout_hbm, wout_ref), (wback_hbm, wback_ref), (wgate_hbm, wgate_ref))
+    copies[0].wait()
+    copies[1].wait()
+    both_ref[...] = dot(wout_ref[...], wback_ref[...]).astype(BF16)
+    copies[2].wait()
+
+
+def query_body(norm_ref, in_ref, wqkv_ref, wgate_ref, wback_ref, query_ref, gate_ref, back_ref):
     rows, model = norm_ref.shape
     width = model // TH
     group = TH // 2
@@ -307,6 +312,7 @@
         wk = wqkv_ref[:, model + g * span : model + (g + 1) * span]
         query_ref[g * group * rows : (g + 1) * group * rows, :] = dot_nt(stacked, wk).astype(BF16)
     gate_ref[...] = jax.nn.sigmoid(dot(norm, wgate_ref[...]))
+    back_ref[...] = dot(in_ref[...].astype(BF16), wback_ref[...])
 
 
 def stage_body(
@@ -314,22 +320,16 @@
     after,
     bias_hbm,
     mask_hbm,
-    wout_hbm,
-    wback_hbm,
     out_ref,
-    wout_ref,
-    wback_ref,
     bias_ref,
     mask_ref,
     sems,
 ):
-    copies = fetch(
-        sems, (mask_hbm, mask_ref), (bias_hbm, bias_ref), (wout_hbm, wout_ref), (wback_hbm, wback_ref)
-    )
+    copies = fetch(sems, (mask_hbm, mask_ref), (bias_hbm, bias_ref))
     copies[0].wait()
     copies[1].wait()
     allowed = mask_ref[...] == 1
-    heads, rows, keys = bias_ref.shape
+    heads, rows, _ = bias_ref.shape
     if lists is None:
         for h in range(heads):
             out_ref[0, h * rows : (h + 1) * rows, :] = jnp.where(allowed, bias_ref[h], masked_score)
@@ -350,8 +350,6 @@
                     piece = pltpu.roll(piece, ((j + per - block % per) % per) * rows, 1)
                     merged = piece if j == 0 else jnp.where(lane_block == j, piece, merged)
                 out_ref[c, :, tile * 128 : (tile + 1) * 128] = merged
-    for copy in copies[2:]:
-        copy.wait()
 
 
 def part_of(rows, query_ref, keys_ref, bias, wqkv_ref):
@@ -390,18 +388,17 @@
 def attend_body(
     half,
     chunk,
-    in_ref,
+    base_ref,
     query_ref,
     gate_ref,
     keys_ref,
     bias_ref,
     wqkv_ref,
-    wout_ref,
-    wback_ref,
+    both_ref,
     *rest,
 ):
-    parts, (out_ref, back_ref, pair_out, odd_out) = rest[:-4], rest[-4:]
-    rows, model = in_ref.shape
+    parts, (gated_ref, back_ref, pair_out, odd_out) = rest[:-4], rest[-4:]
+    rows, _ = gate_ref.shape
     even = lax.axis_index("row") % 2 == 0
     found = part_of(rows, query_ref, keys_ref, lambda at: bias_ref[chunk, at, :], wqkv_ref)
     found = [[part[n] for n in range(3)] for part in parts] + [found]
@@ -410,13 +407,16 @@
     total = sum(f[1] * w for f, w in zip(found, shares))
     mixed = sum(f[2] * w for f, w in zip(found, shares))
     gated = (gate_ref[...] * (mixed / total)).astype(BF16)
-    token_out = (in_ref[...] + dot(gated, wout_ref[...])).astype(BF16)
-    out_ref[...] = token_out
-    back = dot(token_out, wback_ref[...])
+    gated_ref[...] = gated
+    back = base_ref[...] + dot(gated, both_ref[...])
     back_ref[...] = back.astype(BF16)
     lower, upper = back[:half], back[rows - half :]
     pair_out[...] = jnp.where(even, upper, lower).astype(BF16)
     odd_out[...] = jnp.where(even, lower, upper).astype(BF16)
+
+
+def out_body(in_ref, gated_ref, wout_ref, out_ref):
+    out_ref[...] = (in_ref[...] + dot(gated_ref[...], wout_ref[...])).astype(BF16)
 
 
 def final_body(living_ref, hot_ref, mid_ref, back_ref, pair_ref, odd_ref, wpos_ref, pos_ref, noise_ref, out_ref):
@@ -438,7 +438,9 @@
     far = [(g * count + a, g * count + b) for g in range(groups) for a, b in odds + [(b, a) for a, b in odds]]
     if groups % 2 == 0 and count % 2 == 0:
         far += [(g * count + i, (g ^ 1) * count + i) for g in range(groups) for i in (0, count - 1)]
-    return lax.ppermute(pair, "row", near), lax.ppermute(odd, ("grp", "row"), far)
+    odd = lax.ppermute(odd, ("grp", "row"), far)
+    pair = lax.ppermute(pair, "row", near)
+    return pair, odd
 
 
 def kind_of(i):
@@ -506,7 +508,6 @@
             shape(w_atom_out.shape, BF16),
             shape(w_agg.shape, BF16),
         ],
-        "embed",
         [HBM] * 11,
         [
             pltpu.SMEM((1, 1), jnp.int32),
@@ -532,14 +533,9 @@
         w_agg,
     )
     pair, odd = exchange(pair, odd, groups, count)
-    att, wgate = call(
-        local_body,
-        [shape((rows, width), BF16), shape(w_tok_gate.shape, BF16)],
-        "local",
-        [SMEM] + [VMEM] * 4 + [HBM],
-        [pltpu.SemaphoreType.DMA((1,))],
-        flops=10**9,
-    )(offsets, q, keys, values, bias, w_tok_gate)
+    (att,) = call(
+        local_body, [shape((rows, width), BF16)], [SMEM] + [VMEM] * 4, flops=10**9
+    )(offsets, q, keys, values, bias)
     packed = model + 128
     mid, own, pair, odd, hot, living = call(
         functools.partial(atoms_body, half),
@@ -551,16 +547,25 @@
             shape((rows, block_rows + 2 * half), BF16),
             shape((1, rows), F32),
         ],
-        "atoms",
         [SMEM, SMEM] + [VMEM] * 11,
         [pltpu.VMEM((BEHIND + rows + AHEAD, width), F32)] * 2 + [pltpu.VMEM((rows, width), BF16)],
     )(info, offsets, tokens, start, q, keys, values, pair, odd, att, bias, wout, wagg)
     pair, odd = exchange(pair, odd, groups, count)
+    wgate, wout, wback, both = call(
+        weights_body,
+        [
+            shape(w_tok_gate.shape, BF16),
+            shape(w_tok_out.shape, BF16),
+            shape(w_back.shape, BF16),
+            shape(w_back.shape, BF16),
+        ],
+        [VMEM] + [HBM] * 3,
+        [pltpu.SemaphoreType.DMA((3,))],
+        flops=10**9,
+    )(own, w_tok_gate, w_tok_out, w_back)
+    odd, wgate, wout, wback, both = lax.optimization_barrier((odd, wgate, wout, wback, both))
     token_in, norm = call(
-        token_body,
-        [shape((block_rows, model), F32), shape((block_rows, model), BF16)],
-        "token",
-        [VMEM] * 4,
+        token_body, [shape((block_rows, model), F32), shape((block_rows, model), BF16)], [VMEM] * 4
     )(own, pair, odd, token_single)
 
     doubling = count & (count - 1) == 0 and count >= 16 and 128 % block_rows == 0
@@ -571,35 +576,32 @@
     def query(seen):
         return call(
             query_body,
-            [shape((TH * block_rows, model), BF16), shape((block_rows, model), F32)],
-            "query",
-            [VMEM, VMEM, VMEM],
+            [
+                shape((TH * block_rows, model), BF16),
+                shape((block_rows, model), F32),
+                shape((block_rows, width), F32),
+            ],
+            [VMEM] * 5,
             flops=10**9,
-        )(seen, w_tok_qkv, wgate)
+        )(seen, token_in, w_tok_qkv, wgate, wback)
 
     def stage(seen):
         return call(
             functools.partial(stage_body, lists),
-            [
-                shape((chunks, TH * block_rows, span), F32),
-                shape(w_tok_out.shape, BF16),
-                shape(w_back.shape, BF16),
-            ],
-            "stage",
-            [VMEM] + [HBM] * 4,
+            [shape((chunks, TH * block_rows, span), F32)],
+            [VMEM] + [HBM] * 2,
             [
                 pltpu.VMEM(token_bias.shape, F32),
                 pltpu.VMEM(pair_mask.shape, jnp.int32),
-                pltpu.SemaphoreType.DMA((4,)),
+                pltpu.SemaphoreType.DMA((2,)),
             ],
             flops=10**9,
-        )(seen, token_bias, pair_mask, w_tok_out, w_back)
+        )(seen, token_bias, pair_mask)[0]
 
     def part(chunk, seen):
         return call(
             functools.partial(part_body, chunk),
             [shape((3, block_rows, model), F32)],
-            "part",
             [VMEM] * 4,
             flops=10**9,
         )(query_rows, seen, score_bias, w_tok_qkv)[0]
@@ -609,9 +611,9 @@
         for n, step in enumerate(steps[:-1]):
             arrived = swap(held, count, step)
             if n == 0:
-                arrived, (query_rows, gate) = lax.optimization_barrier((arrived, query(norm)))
+                arrived, (query_rows, gate, base) = lax.optimization_barrier((arrived, query(norm)))
             if n == 1:
-                arrived, (score_bias, wout, wback) = lax.optimization_barrier((arrived, stage(held)))
+                arrived, score_bias = lax.optimization_barrier((arrived, stage(held)))
             held = jnp.concatenate([held, arrived], axis=0)
         last = swap(held, count, steps[-1])
         near = swap(held, count, [1, 1])
@@ -621,10 +623,10 @@
         parts = parts + [part(2, last)]
     else:
         end = lax.all_gather(norm, "row", axis=0, tiled=True)
-        query_rows, gate = query(norm)
-        score_bias, wout, wback = stage(norm)
+        query_rows, gate, base = query(norm)
+        score_bias = stage(norm)
         parts = []
-    token_out, back, pair, odd = call(
+    gated, back, pair, odd = call(
         functools.partial(attend_body, half, chunks - 1),
         [
             shape((block_rows, model), BF16),
@@ -632,15 +634,15 @@
             shape((half, width), BF16),
             shape((half, width), BF16),
         ],
-        "attend",
-        [VMEM] * (8 + len(parts)),
-    )(token_in, query_rows, gate, end, score_bias, w_tok_qkv, wout, wback, *parts)
+        [VMEM] * (7 + len(parts)),
+    )(base, query_rows, gate, end, score_bias, w_tok_qkv, both, *parts)
     pair, odd = exchange(pair, odd, groups, count)
+    (token_out,) = call(
+        out_body, [shape((block_rows, model), BF16)], [VMEM] * 3, flops=10**9
+    )(token_in, gated, wout)
+    odd, token_out = lax.optimization_barrier((odd, token_out))
     (denoised,) = call(
-        final_body,
-        [shape(positions.shape, F32)],
-        "final",
-        [VMEM] * 9,
+        final_body, [shape(positions.shape, F32)], [VMEM] * 9
     )(living, hot, mid, back, pair, odd, w_pos, positions, noise)
     return (denoised, token_out)
 

time: 39.4 us -> 38.6 us (0.980)
  waiting for transfers between devices: 16.6 us -> 14.6 us
  Pallas kernels: 16.6 us -> 17.8 us
    ppermute x6, waiting for transfers between devices: 7.74 us -> 5.73 us  [the longest x3 5.72 us: exchange(): odd = lax.ppermute(odd, ('grp', 'row'), far)]
    pallas_call x11 -> x13, Pallas kernels: 16.6 us -> 17.8 us  [call(): run(*[pltpu.with_memory_space_constraint(x, pltpu.HBM) if h and x.size >...]
  transfers between devices with their start and end apart: 11 -> 11, of which waited for: 7 -> 6; matrix products, arithmetic and copies ran while one was open for 0% -> 0% of each run, Pallas kernels for 23% -> 29%
where the time goes in v7:
time: 38.6 us; the launch traced here: 38.3 us
  Pallas kernels  17.8 us (46%)
  waiting for transfers between devices  14.6 us (38%)
  starting transfers between devices  4.39 us (11%)
  between operations  1.44 us (4%)
    pallas_call x13, Pallas kernels, call(): run(*[pltpu.with_memory_space_constraint(x, pltpu.HBM) if h and x.size >...  17.8 us
    ppermute x5, waiting for transfers between devices, swap(): lax.ppermute(value, 'row', [(i, i ^ step[kind_of(i)]) for i in range(coun...  8.87 us
    ppermute x3, waiting for transfers between devices, exchange(): odd = lax.ppermute(odd, ('grp', 'row'), far)  5.72 us
    ppermute x3, starting transfers between devices, exchange(): odd = lax.ppermute(odd, ('grp', 'row'), far)  2.91 us
    ppermute x5, starting transfers between devices, swap(): lax.ppermute(value, 'row', [(i, i ^ step[kind_of(i)]) for i in range(coun...  0.99 us
  transfers between devices with their start and end apart: 11, of which 6 were waited for; matrix products, arithmetic and copies ran while one was open for 0% of the time, Pallas kernels for 29%

profile of v7, /device:TPU:24, one launch (start us, length us, event | category | flops | bytes accessed | tf_op | source)
XLA Modules:
  0.0 38.3 jit_solution(6955281039426980150)
XLA Ops:
  1.3 2.3 %shard_map.194 = (s32[8]{0:T(128)S(1)}, f32[384,128]{1,0:T(8,128)S(1)}, bf16[384,128]{1,0:T(8,128)(2,1)S(1)}, f32[480,128]{1,0:T(8,128)S(1)}, f32[480,128]{1,0:T...) custom-call(s32[1,1]{1,0:T(1,128)} %bitcast.2.counts_hbm, ...), custom_call_target="tpu_custom_call" | custom-call | flops 10000000 | bytes 1902160 | tf_op jit(solution)/shard_map/pallas_call | solution.py:63
  3.7 1.5 %collective-permute-start.1 = (bf16[96,256]{1,0:T(8,128)(2,1)S(1)}, bf16[96,256]{1,0:T(8,128)(2,1)S(1)}, u32[]{:S(2)}, u32[]{:S(2)}) collective-permute-start(bf16[96,256]{1,0:T(8,128)(2,1)S(1)} %get-tuple-element.57), channel_id=1, source_target_pairs={{1,2},{3,4},{5,6},{7,8},{9,10},{11,12},{13,14},{2,1},{4,3},{6,5},{... | collective-permute-start | bytes 147464 | tf_op jit(solution)/shard_map/ppermute | solution.py:441
  5.2 1.2 %shard_map.195.att_ref = bf16[384,128]{1,0:T(8,128)(2,1)S(1)} custom-call(s32[1,12]{1,0:T(1,128)S(1)} %get-tuple-element.50.offsets, bf16[384,128]{1,0:T(8,128)(2,1)S(1)} %get-tuple-element.53.q_ref, f32[480,128]{1,0:T(8,128)S(1)} %get-tuple-element.54.k_ref, f32[480,128]{1,0:T(8,128)S(1)} %get-tuple-element.55.v_ref, ...), custom_call_target="tpu_custom_call" | custom-call | flops 1000000000 | bytes 98304 | tf_op jit(solution)/shard_map/pallas_call | solution.py:63
  6.4 1.8 %collective-permute-done.1.odd_ref = bf16[96,256]{1,0:T(8,128)(2,1)S(1)} collective-permute-done((bf16[96,256]{1,0:T(8,128)(2,1)S(1)}, bf16[96,256]{1,0:T(8,128)(2,1)S(1)}, u32[]{:S(2)}, u32[]{:S(2)}) %collective-permute-start.1) | collective-permute-done | bytes 49184 | tf_op jit(solution)/shard_map/ppermute | solution.py:441
  8.3 1.7 %shard_map.196 = (f32[384,128]{1,0:T(8,128)S(1)}, f32[32,896]{1,0:T(8,128)S(1)}, bf16[16,896]{1,0:T(8,128)(2,1)S(1)}, bf16[16,896]{1,0:T(8,128)(2,1)S(1)}, bf16[...) custom-call(s32[8]{0:T(128)S(1)} %get-tuple-element.49.info, s32[1,12]{1,0:T(1,128)S(1)} %get-tuple-element.50.offsets, ...), custom_call_target="tpu_custom_call" | custom-call | flops 10000000 | bytes 419328 | tf_op jit(solution)/shard_map/pallas_call | solution.py:63
  10.1 1.4 %collective-permute-start.3 = (bf16[16,896]{1,0:T(8,128)(2,1)S(1)}, bf16[16,896]{1,0:T(8,128)(2,1)S(1)}, u32[]{:S(2)}, u32[]{:S(2)}) collective-permute-start(bf16[16,896]{1,0:T(8,128)(2,1)S(1)} %get-tuple-element.66), channel_id=1, source_target_pairs={{1,2},{3,4},{5,6},{7,8},{9,10},{11,12},{13,14},{2,1},{4,3},{6,5},{... | collective-permute-start | bytes 86024 | tf_op jit(solution)/shard_map/ppermute | solution.py:441
  11.5 1.9 %shard_map.197 = (bf16[768,768]{1,0:T(8,128)(2,1)S(1)}, bf16[768,768]{1,0:T(8,128)(2,1)S(1)}, bf16[768,128]{1,0:T(8,128)(2,1)S(1)}, bf16[768,128]{1,0:T(8,128)(2,1)S(1)}) custom-call(f32[32,896]{1,0:T(8,128)S(1)} %get-tuple-element.64.after.own_ref, bf16[768,768]{1,0:T(8,128)(2,1)} %wgate_hbm.1, bf16[768,768]{1,0:T(8,128)(2,1)} %wout_hbm.3, ...), custom_call_target="tpu_custom_call" | custom-call | flops 1000000000 | bytes 2752512 | tf_op jit(solution)/shard_map/pallas_call | solution.py:63
  13.4 0.9 %collective-permute-done.3.odd_ref = bf16[16,896]{1,0:T(8,128)(2,1)S(1)} collective-permute-done((bf16[16,896]{1,0:T(8,128)(2,1)S(1)}, bf16[16,896]{1,0:T(8,128)(2,1)S(1)}, u32[]{:S(2)}, u32[]{:S(2)}) %collective-permute-start.3) | collective-permute-done | bytes 28704 | tf_op jit(solution)/shard_map/ppermute | solution.py:441
  14.4 0.3 shard_map.198
  14.8 1.0 %shard_map.199 = (bf16[512,768]{1,0:T(8,128)(2,1)S(1)}, f32[32,768]{1,0:T(8,128)S(1)}, f32[32,128]{1,0:T(8,128)S(1)}) custom-call(bf16[32,768]{1,0:T(8,128)(2,1)S(1)} %get-tuple-element.72.norm_ref, f32[32,768]{1,0:T(8,128)S(1)} %get-tuple-element.73.in_ref, bf16[768,2304]{1,0:T(8,128)(2,1)S(1)} %copy-done, ...), custom_call_target="tpu_custom_call" | custom-call | flops 1000000000 | bytes 901120 | tf_op jit(solution)/shard_map/pallas_call | solution.py:63
  15.8 4.9 %collective-permute-done.4 = bf16[32,768]{1,0:T(8,128)(2,1)S(1)} collective-permute-done((bf16[32,768]{1,0:T(8,128)(2,1)S(1)}, bf16[32,768]{1,0:T(8,128)(2,1)S(1)}, u32[]{:S(2)}, u32[]{:S(2)}) %collective-permute-start.4) | collective-permute-done | bytes 49184 | tf_op jit(solution)/shard_map/ppermute | solution.py:465
  20.7 2.6 %shard_map.200.bias_ref = f32[4,512,128]{2,1,0:T(8,128)S(1)} custom-call(bf16[64,768]{1,0:T(8,128)(2,1)S(1)} %get-tuple-element.96.after, f32[16,32,512]{2,1,0:T(8,128)} %bias_hbm.3, s32[32,512]{1,0:T(8,128)} %mask_hbm.1), custom_call_target="tpu_custom_call" | custom-call | flops 1000000000 | bytes 1048576 | tf_op jit(solution)/shard_map/pallas_call | solution.py:63
  23.3 1.5 %collective-permute-done.5 = bf16[64,768]{1,0:T(8,128)(2,1)S(1)} collective-permute-done((bf16[64,768]{1,0:T(8,128)(2,1)S(1)}, bf16[64,768]{1,0:T(8,128)(2,1)S(1)}, u32[]{:S(2)}, u32[]{:S(2)}) %collective-permute-start.5) | collective-permute-done | bytes 98336 | tf_op jit(solution)/shard_map/ppermute | solution.py:465
  25.0 0.3 collective-permute-start.6
  25.2 1.1 %shard_map.201.rest_0_ = f32[3,32,768]{2,1,0:T(8,128)S(1)} custom-call(bf16[512,768]{1,0:T(8,128)(2,1)S(1)} %get-tuple-element.80.query_ref, bf16[128,768]{1,0:T(8,128)(2,1)S(1)} %constant_dynamic-update-slice_fusion.2.keys_ref, f32[4,512,128]{2,1,0:T(8,128)S(1)} %shard_map.200.bias_ref, bf16[768,2304]{1,0:T(8,128)(2,1)S(1)} %copy-done), custom_call_target="tpu_custom_call" | custom-call | flops 1000000000 | bytes 294912 | tf_op jit(solution)/shard_map/pallas_call | solution.py:63
  26.4 1.1 %shard_map.202.rest_1_ = f32[3,32,768]{2,1,0:T(8,128)S(1)} custom-call(bf16[512,768]{1,0:T(8,128)(2,1)S(1)} %get-tuple-element.80.query_ref, bf16[128,768]{1,0:T(8,128)(2,1)S(1)} %collective-permute-done.7.keys_ref, f32[4,512,128]{2,1,0:T(8,128)S(1)} %shard_map.200.bias_ref, bf16[768,2304]{1,0:T(8,128)(2,1)S(1)} %copy-done), custom_call_target="tpu_custom_call" | custom-call | flops 1000000000 | bytes 294912 | tf_op jit(solution)/shard_map/pallas_call | solution.py:63
  27.5 2.5 %collective-permute-done.6.keys_ref = bf16[128,768]{1,0:T(8,128)(2,1)S(1)} collective-permute-done((bf16[128,768]{1,0:T(8,128)(2,1)S(1)}, bf16[128,768]{1,0:T(8,128)(2,1)S(1)}, u32[]{:S(2)}, u32[]{:S(2)}) %collective-permute-start.6) | collective-permute-done | bytes 196640 | tf_op jit(solution)/shard_map/ppermute | solution.py:465
  30.1 0.4 %collective-permute-start.8 = (bf16[128,768]{1,0:T(8,128)(2,1)S(1)}, bf16[128,768]{1,0:T(8,128)(2,1)S(1)}, u32[]{:S(2)}, u32[]{:S(2)}) collective-permute-start(bf16[128,768]{1,0:T(8,128)(2,1)S(1)} %collective-permute-done.6.keys_ref), channel_id=1, source_target_pairs={{0,1},{1,0},{2,3},{3,2},{4,5},{5,4},{6,7},{7,6},{8,9},{9,8},{10,11... | collective-permute-start | bytes 589832 | tf_op jit(solution)/shard_map/ppermute | solution.py:465
  30.4 1.1 %shard_map.203.rest_2_ = f32[3,32,768]{2,1,0:T(8,128)S(1)} custom-call(bf16[512,768]{1,0:T(8,128)(2,1)S(1)} %get-tuple-element.80.query_ref, bf16[128,768]{1,0:T(8,128)(2,1)S(1)} %collective-permute-done.6.keys_ref, f32[4,512,128]{2,1,0:T(8,128)S(1)} %shard_map.200.bias_ref, bf16[768,2304]{1,0:T(8,128)(2,1)S(1)} %copy-done), custom_call_target="tpu_custom_call" | custom-call | flops 1000000000 | bytes 294912 | tf_op jit(solution)/shard_map/pallas_call | solution.py:63
  31.6 1.3 %shard_map.204 = (bf16[32,768]{1,0:T(8,128)(2,1)S(1)}, bf16[32,128]{1,0:T(8,128)(2,1)S(1)}, bf16[16,128]{1,0:T(8,128)(2,1)S(1)}, bf16[16,128]{1,0:T(8,128)(2,1)S(1)}) custom-call(f32[32,128]{1,0:T(8,128)S(1)} %get-tuple-element.79.base_ref, bf16[512,768]{1,0:T(8,128)(2,1)S(1)} %get-tuple-element.80.query_ref, f32[32,768]{1,0:T(8,128)S(1)} %get-tuple-element.81.gate_ref, ...), custom_call_target="tpu_custom_call" | custom-call | flops 10000000 | bytes 65536 | tf_op jit(solution)/shard_map/pallas_call | solution.py:63
  32.9 0.3 collective-permute-start.9
  33.3 1.0 %shard_map.205 = bf16[32,768]{1,0:T(8,128)(2,1)} custom-call(f32[32,768]{1,0:T(8,128)S(1)} %get-tuple-element.73.in_ref, bf16[32,768]{1,0:T(8,128)(2,1)S(1)} %get-tuple-element.92.gated_ref, bf16[768,768]{1,0:T(8,128)(2,1)S(1)} %get-tuple-element.93.wout_ref), custom_call_target="tpu_custom_call" | custom-call | flops 1000000000 | bytes 49152 | tf_op jit(solution)/shard_map/pallas_call | solution.py:63
  34.2 3.0 %collective-permute-done.10.odd_ref = bf16[16,128]{1,0:T(8,128)(2,1)S(1)} collective-permute-done((bf16[16,128]{1,0:T(8,128)(2,1)S(1)}, bf16[16,128]{1,0:T(8,128)(2,1)S(1)}, u32[]{:S(2)}, u32[]{:S(2)}) %collective-permute-start.10) | collective-permute-done | bytes 4128 | tf_op jit(solution)/shard_map/ppermute | solution.py:441
  37.2 1.1 %shard_map.206 = f32[3,384]{1,0:T(4,128)} custom-call(f32[1,384]{1,0:T(1,128)S(1)} %get-tuple-element.61.living_ref, bf16[384,64]{1,0:T(8,128)(2,1)S(1)} %get-tuple-element.62.hot_ref, f32[384,128]{1,0:T(8,128)S(1)} %get-tuple-element.63.mid_ref, bf16[32,128]{1,0:T(8,128)(2,1)S(1)} %get-tuple-element.89.back_ref, ...), custom_call_target="tpu_custom_call" | custom-call | flops 10000000 | bytes 4608 | tf_op jit(solution)/shard_map/pallas_call | solution.py:63
  (24 shorter events, 0.5 us)
Async XLA Ops:
  3.6 2.8 %collective-permute-start = (bf16[96,256]{1,0:T(8,128)(2,1)S(1)}, bf16[96,256]{1,0:T(8,128)(2,1)S(1)}, u32[]{:S(2)}, u32[]{:S(2)}) collective-permute-start(bf16[96,256]{1,0:T(8,128)(2,1)S(1)} %get-tuple-element.56), channel_id=1, source_target_pairs={{0,1},{1,0},{2,3},{3,2},{4,5},{5,4},{6,7},{7,6},{8,9},{9,8},{10,11... | collective-permute-start | bytes 147464 | tf_op jit(solution)/shard_map/ppermute | solution.py:442
  3.7 4.6 %collective-permute-start.1 = (bf16[96,256]{1,0:T(8,128)(2,1)S(1)}, bf16[96,256]{1,0:T(8,128)(2,1)S(1)}, u32[]{:S(2)}, u32[]{:S(2)}) collective-permute-start(bf16[96,256]{1,0:T(8,128)(2,1)S(1)} %get-tuple-element.57), channel_id=1, source_target_pairs={{1,2},{3,4},{5,6},{7,8},{9,10},{11,12},{13,14},{2,1},{4,3},{6,5},{... | collective-permute-start | bytes 147464 | tf_op jit(solution)/shard_map/ppermute | solution.py:441
  10.0 4.4 %collective-permute-start.2 = (bf16[16,896]{1,0:T(8,128)(2,1)S(1)}, bf16[16,896]{1,0:T(8,128)(2,1)S(1)}, u32[]{:S(2)}, u32[]{:S(2)}) collective-permute-start(bf16[16,896]{1,0:T(8,128)(2,1)S(1)} %get-tuple-element.65), channel_id=1, source_target_pairs={{0,1},{1,0},{2,3},{3,2},{4,5},{5,4},{6,7},{7,6},{8,9},{9,8},{10,11... | collective-permute-start | bytes 86024 | tf_op jit(solution)/shard_map/ppermute | solution.py:442
  10.1 4.3 %collective-permute-start.3 = (bf16[16,896]{1,0:T(8,128)(2,1)S(1)}, bf16[16,896]{1,0:T(8,128)(2,1)S(1)}, u32[]{:S(2)}, u32[]{:S(2)}) collective-permute-start(bf16[16,896]{1,0:T(8,128)(2,1)S(1)} %get-tuple-element.66), channel_id=1, source_target_pairs={{1,2},{3,4},{5,6},{7,8},{9,10},{11,12},{13,14},{2,1},{4,3},{6,5},{... | collective-permute-start | bytes 86024 | tf_op jit(solution)/shard_map/ppermute | solution.py:441
  11.5 2.9 %copy-start.1 = (bf16[32,768]{1,0:T(8,128)(2,1)S(1)}, bf16[32,768]{1,0:T(8,128)(2,1)}, u32[]{:S(2)}) copy-start(bf16[32,768]{1,0:T(8,128)(2,1)} %single_ref.1) | copy-start | bytes 147460
  11.5 3.3 %copy-start = (bf16[768,2304]{1,0:T(8,128)(2,1)S(1)}, bf16[768,2304]{1,0:T(8,128)(2,1)}, u32[]{:S(2)}) copy-start(bf16[768,2304]{1,0:T(8,128)(2,1)} %wqkv_ref.9) | copy-start | bytes 10616836
  14.7 5.9 %collective-permute-start.4 = (bf16[32,768]{1,0:T(8,128)(2,1)S(1)}, bf16[32,768]{1,0:T(8,128)(2,1)S(1)}, u32[]{:S(2)}, u32[]{:S(2)}) collective-permute-start(bf16[32,768]{1,0:T(8,128)(2,1)S(1)} %get-tuple-element.72.norm_ref), channel_id=1, source_target_pairs={{0,9},{1,8},{2,11},{3,10},{4,13},{5,12},{6,15},{7,14},{8,1},{9,0},... | collective-permute-start | bytes 147464 | tf_op jit(solution)/shard_map/ppermute | solution.py:465
  20.7 4.1 %collective-permute-start.5 = (bf16[64,768]{1,0:T(8,128)(2,1)S(1)}, bf16[64,768]{1,0:T(8,128)(2,1)S(1)}, u32[]{:S(2)}, u32[]{:S(2)}) collective-permute-start(bf16[64,768]{1,0:T(8,128)(2,1)S(1)} %get-tuple-element.96.after), channel_id=1, source_target_pairs={{0,5},{1,2},{2,1},{3,6},{4,7},{5,0},{6,3},{7,4},{8,13},{9,10},{10,... | collective-permute-start | bytes 294920 | tf_op jit(solution)/shard_map/ppermute | solution.py:465
  24.8 1.6 %collective-permute-start.7 = (bf16[128,768]{1,0:T(8,128)(2,1)S(1)}, bf16[128,768]{1,0:T(8,128)(2,1)S(1)}, u32[]{:S(2)}, u32[]{:S(2)}) collective-permute-start(bf16[128,768]{1,0:T(8,128)(2,1)S(1)} %constant_dynamic-update-slice_fusion.2.keys_ref), channel_id=1, source_target_pairs={{0,1},{1,0},{2,3},{3,2},{4,5},{5,4},{6,7},{7,6},{8,9},{9,8},{10,11... | collective-permute-start | bytes 589832 | tf_op jit(solution)/shard_map/ppermute | solution.py:465
  25.0 5.1 %collective-permute-start.6 = (bf16[128,768]{1,0:T(8,128)(2,1)S(1)}, bf16[128,768]{1,0:T(8,128)(2,1)S(1)}, u32[]{:S(2)}, u32[]{:S(2)}) collective-permute-start(bf16[128,768]{1,0:T(8,128)(2,1)S(1)} %constant_dynamic-update-slice_fusion.2.keys_ref), channel_id=1, source_target_pairs={{0,3},{1,4},{2,7},{3,0},{4,1},{5,6},{6,5},{7,2},{8,11},{9,12},{10,... | collective-permute-start | bytes 589832 | tf_op jit(solution)/shard_map/ppermute | solution.py:465
  30.1 1.5 %collective-permute-start.8 = (bf16[128,768]{1,0:T(8,128)(2,1)S(1)}, bf16[128,768]{1,0:T(8,128)(2,1)S(1)}, u32[]{:S(2)}, u32[]{:S(2)}) collective-permute-start(bf16[128,768]{1,0:T(8,128)(2,1)S(1)} %collective-permute-done.6.keys_ref), channel_id=1, source_target_pairs={{0,1},{1,0},{2,3},{3,2},{4,5},{5,4},{6,7},{7,6},{8,9},{9,8},{10,11... | collective-permute-start | bytes 589832 | tf_op jit(solution)/shard_map/ppermute | solution.py:465
  32.9 4.3 %collective-permute-start.9 = (bf16[16,128]{1,0:T(8,128)(2,1)S(1)}, bf16[16,128]{1,0:T(8,128)(2,1)S(1)}, u32[]{:S(2)}, u32[]{:S(2)}) collective-permute-start(bf16[16,128]{1,0:T(8,128)(2,1)S(1)} %get-tuple-element.90), channel_id=1, source_target_pairs={{0,1},{1,0},{2,3},{3,2},{4,5},{5,4},{6,7},{7,6},{8,9},{9,8},{10,11... | collective-permute-start | bytes 12296 | tf_op jit(solution)/shard_map/ppermute | solution.py:442
  33.2 3.9 %collective-permute-start.10 = (bf16[16,128]{1,0:T(8,128)(2,1)S(1)}, bf16[16,128]{1,0:T(8,128)(2,1)S(1)}, u32[]{:S(2)}, u32[]{:S(2)}) collective-permute-start(bf16[16,128]{1,0:T(8,128)(2,1)S(1)} %get-tuple-element.91), channel_id=1, source_target_pairs={{1,2},{3,4},{5,6},{7,8},{9,10},{11,12},{13,14},{2,1},{4,3},{6,5},{... | collective-permute-start | bytes 12296 | tf_op jit(solution)/shard_map/ppermute | solution.py:441
  33.2 3.9 %copy-start.2 = (f32[3,384]{1,0:T(4,128)S(1)}, f32[3,384]{1,0:T(4,128)}, u32[]{:S(2)}) copy-start(f32[3,384]{1,0:T(4,128)} %pos_ref.1) | copy-start | bytes 13828
  33.2 3.9 %copy-start.3 = (f32[3,384]{1,0:T(4,128)S(1)}, f32[3,384]{1,0:T(4,128)}, u32[]{:S(2)}) copy-start(f32[3,384]{1,0:T(4,128)} %noise_ref.1) | copy-start | bytes 13828
  33.2 3.9 %copy-start.4 = (bf16[3,128]{1,0:T(4,128)(2,1)S(1)}, bf16[3,128]{1,0:T(4,128)(2,1)}, u32[]{:S(2)}) copy-start(bf16[3,128]{1,0:T(4,128)(2,1)} %wpos_ref.1) | copy-start | bytes 2308

commit v8 on v7

--- a/solution.py
+++ b/solution.py
@@ -72,6 +72,11 @@
     for copy in copies:
         copy.start()
     return copies
+
+
+def quarters(src, dst):
+    step = src.shape[0] // 4
+    return [(src.at[pl.ds(n * step, step)], dst.at[pl.ds(n * step, step)]) for n in range(4)]
 
 
 def embed_body(
@@ -88,9 +93,7 @@
     wagg_hbm,
     info_ref,
     start_ref,
-    q_ref,
-    k_ref,
-    v_ref,
+    normed_ref,
     pair_ref,
     odd_ref,
     offsets_ref,
@@ -98,12 +101,13 @@
     bias_ref,
     wout_ref,
     wagg_ref,
+    wqkv_ref,
     counts_ref,
     pos_ref,
     noise_ref,
     single_ref,
     wc_ref,
-    wqkv_ref,
+    wide_ref,
     sems,
 ):
     copies = fetch(
@@ -112,17 +116,16 @@
         (noise_hbm, noise_ref),
         (wc_hbm, wc_ref),
         (single_hbm, single_ref),
+        (counts_hbm, counts_ref),
         (wqkv_hbm, wqkv_ref),
-        (counts_hbm, counts_ref),
         (offsets_hbm, offsets_ref),
         (token_hbm, token_ref.at[0]),
-        (bias_hbm, bias_ref),
+        *quarters(bias_hbm, bias_ref),
         (wout_hbm, wout_ref),
         (wagg_hbm, wagg_ref),
     )
     rows, width = single_ref.shape
-    for ref in (k_ref, v_ref):
-        ref[rows:, :] = jnp.zeros((AHEAD, width), F32)
+    wide_ref[rows:, :] = jnp.zeros((AHEAD, width), F32)
     for copy in copies[:3]:
         copy.wait()
     scaled = input_scale * (pos_ref[...] + noise_level * noise_ref[...])
@@ -133,11 +136,10 @@
     for c in range(3):
         start = start + across[:, c : c + 1] * wc_ref[c : c + 1, :]
     start_ref[...] = start
-    normed = normalize(start).astype(BF16)
+    normed = normalize(start)
+    normed_ref[...] = normed.astype(BF16)
+    wide_ref[:rows, :] = normed
     copies[4].wait()
-    qkv = dot(normed, wqkv_ref[...]).astype(BF16)
-    q_ref[...] = qkv[:, :width]
-    copies[5].wait()
     live = counts_ref[0, 0]
     me = lax.axis_index("row")
     info_ref[0] = live
@@ -145,12 +147,9 @@
     info_ref[2] = lax.axis_size("row") - 1
     tail = live - BEHIND
     even = me % 2 == 0
-    for n, ref in enumerate((k_ref, v_ref)):
-        at = slice(n * width, (n + 1) * width)
-        ref[:rows, :] = qkv[:, (n + 1) * width : (n + 2) * width].astype(F32)
-        pair_ref[:, at] = ref[pl.ds(jnp.where(even, tail, 0), AHEAD), :].astype(BF16)
-        odd_ref[:, at] = ref[pl.ds(jnp.where(even, 0, tail), AHEAD), :].astype(BF16)
-    for copy in copies[6:]:
+    pair_ref[...] = wide_ref[pl.ds(jnp.where(even, tail, 0), AHEAD), :].astype(BF16)
+    odd_ref[...] = wide_ref[pl.ds(jnp.where(even, 0, tail), AHEAD), :].astype(BF16)
+    for copy in copies[5:]:
         copy.wait()
 
 
@@ -178,8 +177,13 @@
     return outs
 
 
-def local_body(offsets, q_ref, k_ref, v_ref, bias_ref, att_ref):
-    rows, width = q_ref.shape
+def local_body(offsets, normed_ref, wqkv_ref, bias_ref, q_ref, k_ref, v_ref, att_ref):
+    rows, width = normed_ref.shape
+    qkv = dot(normed_ref[...], wqkv_ref[...]).astype(BF16)
+    q_ref[...] = qkv[:, :width]
+    for n, ref in enumerate((k_ref, v_ref)):
+        ref[:rows, :] = qkv[:, (n + 1) * width : (n + 2) * width].astype(F32)
+        ref[rows:, :] = jnp.zeros((AHEAD, width), F32)
     windows = rows // QWIN
     skip = BEHIND // QWIN
     stop = windows - (AHEAD - QWIN) // QWIN
@@ -213,6 +217,7 @@
     bias_ref,
     wout_ref,
     wagg_ref,
+    wqkv_ref,
     mid_ref,
     own_ref,
     pair_out,
@@ -226,8 +231,8 @@
     rows, width = start_ref.shape
     live, me, last = info[0], info[1], info[2]
     even = me % 2 == 0
-    pair = pair_ref[...].astype(F32)
-    odd = odd_ref[...].astype(F32)
+    pair = dot(pair_ref[...], wqkv_ref[:, width:]).astype(BF16).astype(F32)
+    odd = dot(odd_ref[...], wqkv_ref[:, width:]).astype(BF16).astype(F32)
     for n, (ref, ext) in enumerate(((k_ref, k_ext), (v_ref, v_ext))):
         at = slice(n * width, (n + 1) * width)
         ext[:BEHIND, :] = jnp.where(even, odd[:BEHIND, at], pair[:BEHIND, at])
@@ -291,14 +296,30 @@
 
 
 def weights_body(after, wgate_hbm, wout_hbm, wback_hbm, wgate_ref, wout_ref, wback_ref, both_ref, sems):
-    copies = fetch(sems, (wout_hbm, wout_ref), (wback_hbm, wback_ref), (wgate_hbm, wgate_ref))
-    copies[0].wait()
-    copies[1].wait()
+    copies = fetch(sems, (wback_hbm, wback_ref), *quarters(wout_hbm, wout_ref), *quarters(wgate_hbm, wgate_ref))
+    for copy in copies[:5]:
+        copy.wait()
     both_ref[...] = dot(wout_ref[...], wback_ref[...]).astype(BF16)
-    copies[2].wait()
-
-
-def query_body(norm_ref, in_ref, wqkv_ref, wgate_ref, wback_ref, query_ref, gate_ref, back_ref):
+    for copy in copies[5:]:
+        copy.wait()
+
+
+def query_body(
+    norm_ref,
+    in_ref,
+    wqkv_ref,
+    wgate_ref,
+    wback_ref,
+    bias_hbm,
+    mask_hbm,
+    query_ref,
+    gate_ref,
+    back_ref,
+    bias_ref,
+    mask_ref,
+    sems,
+):
+    copies = fetch(sems, (mask_hbm, mask_ref), *quarters(bias_hbm, bias_ref))
     rows, model = norm_ref.shape
     width = model // TH
     group = TH // 2
@@ -313,43 +334,32 @@
         query_ref[g * group * rows : (g + 1) * group * rows, :] = dot_nt(stacked, wk).astype(BF16)
     gate_ref[...] = jax.nn.sigmoid(dot(norm, wgate_ref[...]))
     back_ref[...] = dot(in_ref[...].astype(BF16), wback_ref[...])
-
-
-def stage_body(
-    lists,
-    after,
-    bias_hbm,
-    mask_hbm,
-    out_ref,
-    bias_ref,
-    mask_ref,
-    sems,
-):
-    copies = fetch(sems, (mask_hbm, mask_ref), (bias_hbm, bias_ref))
-    copies[0].wait()
-    copies[1].wait()
+    for copy in copies:
+        copy.wait()
+
+
+def stage_body(lists, after, bias_ref, mask_ref, out_ref):
     allowed = mask_ref[...] == 1
     heads, rows, _ = bias_ref.shape
     if lists is None:
         for h in range(heads):
             out_ref[0, h * rows : (h + 1) * rows, :] = jnp.where(allowed, bias_ref[h], masked_score)
-    else:
-        for h in range(heads):
-            bias_ref[h] = jnp.where(allowed, bias_ref[h], masked_score)
-        me = lax.axis_index("row")
-        kind = kind_of(me)
-        per = 128 // rows
-        lane_block = iota((heads * rows, 128), 1) // rows
-        for c in range(len(lists[0])):
-            for tile in range(len(lists[0][c]) // per):
-                for j in range(per):
-                    n = tile * per + j
-                    block = me ^ jnp.where(kind == 0, lists[0][c][n], lists[1][c][n])
-                    source = pl.ds(pl.multiple_of((block // per) * 128, 128), 128)
-                    piece = bias_ref[:, :, source].reshape(heads * rows, 128)
-                    piece = pltpu.roll(piece, ((j + per - block % per) % per) * rows, 1)
-                    merged = piece if j == 0 else jnp.where(lane_block == j, piece, merged)
-                out_ref[c, :, tile * 128 : (tile + 1) * 128] = merged
+        return
+    me = lax.axis_index("row")
+    kind = kind_of(me)
+    per = 128 // rows
+    lane_block = iota((heads * rows, 128), 1) // rows
+    for c in range(len(lists[0])):
+        for tile in range(len(lists[0][c]) // per):
+            for j in range(per):
+                n = tile * per + j
+                block = me ^ jnp.where(kind == 0, lists[0][c][n], lists[1][c][n])
+                source = pl.ds(pl.multiple_of((block // per) * 128, 128), 128)
+                piece = jnp.where((mask_ref[:, source] == 1)[None], bias_ref[:, :, source], masked_score)
+                piece = piece.reshape(heads * rows, 128)
+                piece = pltpu.roll(piece, ((j + per - block % per) % per) * rows, 1)
+                merged = piece if j == 0 else jnp.where(lane_block == j, piece, merged)
+            out_ref[c, :, tile * 128 : (tile + 1) * 128] = merged
 
 
 def part_of(rows, query_ref, keys_ref, bias, wqkv_ref):
@@ -492,21 +502,20 @@
     block_rows, model = token_single.shape
     half = block_rows // 2
     info_shape = shape((8,), jnp.int32)
-    info, start, q, keys, values, pair, odd, offsets, tokens, bias, wout, wagg = call(
+    info, start, normed, pair, odd, offsets, tokens, bias, wout, wagg, wqkv = call(
         embed_body,
         [
             info_shape,
             shape((rows, width), F32),
             shape((rows, width), BF16),
-            shape((rows + AHEAD, width), F32),
-            shape((rows + AHEAD, width), F32),
-            shape((AHEAD, 2 * width), BF16),
-            shape((AHEAD, 2 * width), BF16),
+            shape((AHEAD, width), BF16),
+            shape((AHEAD, width), BF16),
             shape((1, rows // QWIN), jnp.int32),
             shape((1, rows), jnp.int32),
             shape(atom_bias.shape, F32),
             shape(w_atom_out.shape, BF16),
             shape(w_agg.shape, BF16),
+            shape(w_atom_qkv.shape, BF16),
         ],
         [HBM] * 11,
         [
@@ -515,10 +524,10 @@
             pltpu.VMEM(noise.shape, F32),
             pltpu.VMEM(atom_single.shape, BF16),
             pltpu.VMEM(w_coord.shape, F32),
-            pltpu.VMEM(w_atom_qkv.shape, BF16),
-            pltpu.SemaphoreType.DMA((11,)),
+            pltpu.VMEM((rows + AHEAD, width), F32),
+            pltpu.SemaphoreType.DMA((14,)),
         ],
-        out_specs=[SMEM] + [VMEM] * 6 + [SMEM] + [VMEM] * 4,
+        out_specs=[SMEM] + [VMEM] * 4 + [SMEM] + [VMEM] * 5,
     )(
         atom_counts[None],
         positions,
@@ -533,9 +542,17 @@
         w_agg,
     )
     pair, odd = exchange(pair, odd, groups, count)
-    (att,) = call(
-        local_body, [shape((rows, width), BF16)], [SMEM] + [VMEM] * 4, flops=10**9
-    )(offsets, q, keys, values, bias)
+    q, keys, values, att = call(
+        local_body,
+        [
+            shape((rows, width), BF16),
+            shape((rows + AHEAD, width), F32),
+            shape((rows + AHEAD, width), F32),
+            shape((rows, width), BF16),
+        ],
+        [SMEM] + [VMEM] * 3,
+        flops=10**9,
+    )(offsets, normed, wqkv, bias)
     packed = model + 128
     mid, own, pair, odd, hot, living = call(
         functools.partial(atoms_body, half),
@@ -547,9 +564,9 @@
             shape((rows, block_rows + 2 * half), BF16),
             shape((1, rows), F32),
         ],
-        [SMEM, SMEM] + [VMEM] * 11,
+        [SMEM, SMEM] + [VMEM] * 12,
         [pltpu.VMEM((BEHIND + rows + AHEAD, width), F32)] * 2 + [pltpu.VMEM((rows, width), BF16)],
-    )(info, offsets, tokens, start, q, keys, values, pair, odd, att, bias, wout, wagg)
+    )(info, offsets, tokens, start, q, keys, values, pair, odd, att, bias, wout, wagg, wqkv)
     pair, odd = exchange(pair, odd, groups, count)
     wgate, wout, wback, both = call(
         weights_body,
@@ -560,7 +577,7 @@
             shape(w_back.shape, BF16),
         ],
         [VMEM] + [HBM] * 3,
-        [pltpu.SemaphoreType.DMA((3,))],
+        [pltpu.SemaphoreType.DMA((9,))],
         flops=10**9,
     )(own, w_tok_gate, w_tok_out, w_back)
     odd, wgate, wout, wback, both = lax.optimization_barrier((odd, wgate, wout, wback, both))
@@ -580,23 +597,21 @@
                 shape((TH * block_rows, model), BF16),
                 shape((block_rows, model), F32),
                 shape((block_rows, width), F32),
+                shape(token_bias.shape, F32),
+                shape(pair_mask.shape, jnp.int32),
             ],
-            [VMEM] * 5,
+            [VMEM] * 5 + [HBM] * 2,
+            [pltpu.SemaphoreType.DMA((5,))],
             flops=10**9,
-        )(seen, token_in, w_tok_qkv, wgate, wback)
-
-    def stage(seen):
+        )(seen, token_in, w_tok_qkv, wgate, wback, token_bias, pair_mask)
+
+    def stage(seen, bias, mask):
         return call(
             functools.partial(stage_body, lists),
             [shape((chunks, TH * block_rows, span), F32)],
-            [VMEM] + [HBM] * 2,
-            [
-                pltpu.VMEM(token_bias.shape, F32),
-                pltpu.VMEM(pair_mask.shape, jnp.int32),
-                pltpu.SemaphoreType.DMA((2,)),
-            ],
+            [VMEM] * 3,
             flops=10**9,
-        )(seen, token_bias, pair_mask)[0]
+        )(seen, bias, mask)[0]
 
     def part(chunk, seen):
         return call(
@@ -611,9 +626,9 @@
         for n, step in enumerate(steps[:-1]):
             arrived = swap(held, count, step)
             if n == 0:
-                arrived, (query_rows, gate, base) = lax.optimization_barrier((arrived, query(norm)))
+                arrived, (query_rows, gate, base, raw, mask) = lax.optimization_barrier((arrived, query(norm)))
             if n == 1:
-                arrived, score_bias = lax.optimization_barrier((arrived, stage(held)))
+                arrived, score_bias = lax.optimization_barrier((arrived, stage(held, raw, mask)))
             held = jnp.concatenate([held, arrived], axis=0)
         last = swap(held, count, steps[-1])
         near = swap(held, count, [1, 1])
@@ -623,8 +638,8 @@
         parts = parts + [part(2, last)]
     else:
         end = lax.all_gather(norm, "row", axis=0, tiled=True)
-        query_rows, gate, base = query(norm)
-        score_bias = stage(norm)
+        query_rows, gate, base, raw, mask = query(norm)
+        score_bias = stage(norm, raw, mask)
         parts = []
     gated, back, pair, odd = call(
         functools.partial(attend_body, half, chunks - 1),

time: 38.6 us -> 37.7 us (0.977)
  waiting for transfers between devices: 14.6 us -> 14 us
    ppermute x3, waiting for transfers between devices: 5.72 us -> 4.5 us  [exchange(): odd = lax.ppermute(odd, ('grp', 'row'), far)]
    ppermute x5, waiting for transfers between devices: 8.87 us -> 9.44 us  [swap(): lax.ppermute(value, 'row', [(i, i ^ step[kind_of(i)]) for i in range(coun...]
  transfers between devices with their start and end apart: 11 -> 11, of which waited for: 6 -> 7; matrix products, arithmetic and copies ran while one was open for 0% -> 0% of each run, Pallas kernels for 29% -> 30%
where the time goes in v8:
time: 37.7 us; the launch traced here: 37.5 us
  Pallas kernels  17.8 us (47%)
  waiting for transfers between devices  14 us (37%)
  starting transfers between devices  4.23 us (11%)
  between operations  1.44 us (4%)
    pallas_call x13, Pallas kernels, call(): run(*[pltpu.with_memory_space_constraint(x, pltpu.HBM) if h and x.size >...  17.8 us
    ppermute x5, waiting for transfers between devices, swap(): lax.ppermute(value, 'row', [(i, i ^ step[kind_of(i)]) for i in range(coun...  9.44 us
    ppermute x3, waiting for transfers between devices, exchange(): odd = lax.ppermute(odd, ('grp', 'row'), far)  4.5 us
    ppermute x3, starting transfers between devices, exchange(): odd = lax.ppermute(odd, ('grp', 'row'), far)  3.07 us
  transfers between devices with their start and end apart: 11, of which 7 were waited for; matrix products, arithmetic and copies ran while one was open for 0% of the time, Pallas kernels for 30%

profile of v8, /device:TPU:24, one launch (start us, length us, event | category | flops | bytes accessed | tf_op | source)
XLA Modules:
  0.0 37.5 jit_solution(1422102896718285158)
XLA Ops:
  1.3 2.1 %shard_map.194 = (s32[8]{0:T(128)S(1)}, f32[384,128]{1,0:T(8,128)S(1)}, bf16[384,128]{1,0:T(8,128)(2,1)S(1)}, bf16[96,128]{1,0:T(8,128)(2,1)S(1)}, bf16[96,128]{...) custom-call(s32[1,1]{1,0:T(1,128)} %bitcast.2.counts_hbm, ...), custom_call_target="tpu_custom_call" | custom-call | flops 10000000 | bytes 1459792 | tf_op jit(solution)/shard_map/pallas_call | solution.py:63
  3.5 1.5 %collective-permute-start.1 = (bf16[96,128]{1,0:T(8,128)(2,1)S(1)}, bf16[96,128]{1,0:T(8,128)(2,1)S(1)}, u32[]{:S(2)}, u32[]{:S(2)}) collective-permute-start(bf16[96,128]{1,0:T(8,128)(2,1)S(1)} %get-tuple-element.67), channel_id=1, source_target_pairs={{1,2},{3,4},{5,6},{7,8},{9,10},{11,12},{13,14},{2,1},{4,3},{6,5},{... | collective-permute-start | bytes 73736 | tf_op jit(solution)/shard_map/ppermute | solution.py:451
  5.0 1.5 %shard_map.195 = (bf16[384,128]{1,0:T(8,128)(2,1)S(1)}, f32[480,128]{1,0:T(8,128)S(1)}, f32[480,128]{1,0:T(8,128)S(1)}, bf16[384,128]{1,0:T(8,128)(2,1)S(1)}) custom-call(s32[1,12]{1,0:T(1,128)S(1)} %get-tuple-element.57.offsets, bf16[384,128]{1,0:T(8,128)(2,1)S(1)} %get-tuple-element.60.normed_ref, bf16[128,384]{1,0:T(8,128)(2,1)S(1)} %get-tuple-element.61.wqkv_ref, ...), custom_call_target="tpu_custom_call" | custom-call | flops 1000000000 | bytes 688128 | tf_op jit(solution)/shard_map/pallas_call | solution.py:63
  6.5 1.2 %collective-permute-done.1.odd_ref = bf16[96,128]{1,0:T(8,128)(2,1)S(1)} collective-permute-done((bf16[96,128]{1,0:T(8,128)(2,1)S(1)}, bf16[96,128]{1,0:T(8,128)(2,1)S(1)}, u32[]{:S(2)}, u32[]{:S(2)}) %collective-permute-start.1) | collective-permute-done | bytes 24608 | tf_op jit(solution)/shard_map/ppermute | solution.py:451
  7.7 1.9 %shard_map.196 = (f32[384,128]{1,0:T(8,128)S(1)}, f32[32,896]{1,0:T(8,128)S(1)}, bf16[16,896]{1,0:T(8,128)(2,1)S(1)}, bf16[16,896]{1,0:T(8,128)(2,1)S(1)}, bf16[...) custom-call(s32[8]{0:T(128)S(1)} %get-tuple-element.56.info, s32[1,12]{1,0:T(1,128)S(1)} %get-tuple-element.57.offsets, ...), custom_call_target="tpu_custom_call" | custom-call | flops 10000000 | bytes 419328 | tf_op jit(solution)/shard_map/pallas_call | solution.py:63
  9.6 1.5 %collective-permute-start.3 = (bf16[16,896]{1,0:T(8,128)(2,1)S(1)}, bf16[16,896]{1,0:T(8,128)(2,1)S(1)}, u32[]{:S(2)}, u32[]{:S(2)}) collective-permute-start(bf16[16,896]{1,0:T(8,128)(2,1)S(1)} %get-tuple-element.76), channel_id=1, source_target_pairs={{1,2},{3,4},{5,6},{7,8},{9,10},{11,12},{13,14},{2,1},{4,3},{6,5},{... | collective-permute-start | bytes 86024 | tf_op jit(solution)/shard_map/ppermute | solution.py:451
  11.1 2.0 %shard_map.197 = (bf16[768,768]{1,0:T(8,128)(2,1)S(1)}, bf16[768,768]{1,0:T(8,128)(2,1)S(1)}, bf16[768,128]{1,0:T(8,128)(2,1)S(1)}, bf16[768,128]{1,0:T(8,128)(2,1)S(1)}) custom-call(f32[32,896]{1,0:T(8,128)S(1)} %get-tuple-element.74.after.own_ref, bf16[768,768]{1,0:T(8,128)(2,1)} %wgate_hbm.1, bf16[768,768]{1,0:T(8,128)(2,1)} %wout_hbm.3, ...), custom_call_target="tpu_custom_call" | custom-call | flops 1000000000 | bytes 2752512 | tf_op jit(solution)/shard_map/pallas_call | solution.py:63
  13.1 0.7 %collective-permute-done.3.odd_ref = bf16[16,896]{1,0:T(8,128)(2,1)S(1)} collective-permute-done((bf16[16,896]{1,0:T(8,128)(2,1)S(1)}, bf16[16,896]{1,0:T(8,128)(2,1)S(1)}, u32[]{:S(2)}, u32[]{:S(2)}) %collective-permute-start.3) | collective-permute-done | bytes 28704 | tf_op jit(solution)/shard_map/ppermute | solution.py:451
  13.8 0.3 shard_map.198
  14.3 2.0 %shard_map.199 = (bf16[512,768]{1,0:T(8,128)(2,1)S(1)}, f32[32,768]{1,0:T(8,128)S(1)}, f32[32,128]{1,0:T(8,128)S(1)}, f32[16,32,512]{2,1,0:T(8,128)S(1)}, s32[32,512]{1,0:T(8,128)S(1)}) custom-call(bf16[32,768]{1,0:T(8,128)(2,1)S(1)} %get-tuple-element.82.norm_ref, f32[32,768]{1,0:T(8,128)S(1)} %get-tuple-element.83.in_ref, bf16[768,2304]{1,0:T(8,128)(2,1)S(1)} %copy-done, ...), custom_call_target="tpu_custom_call" | custom-call | flops 1000000000 | bytes 2015232 | tf_op jit(solution)/shard_map/pallas_call | solution.py:63
  16.3 3.8 %collective-permute-done.4 = bf16[32,768]{1,0:T(8,128)(2,1)S(1)} collective-permute-done((bf16[32,768]{1,0:T(8,128)(2,1)S(1)}, bf16[32,768]{1,0:T(8,128)(2,1)S(1)}, u32[]{:S(2)}, u32[]{:S(2)}) %collective-permute-start.4) | collective-permute-done | bytes 49184 | tf_op jit(solution)/shard_map/ppermute | solution.py:475
  20.2 1.2 %shard_map.200.bias_ref = f32[4,512,128]{2,1,0:T(8,128)S(1)} custom-call(bf16[64,768]{1,0:T(8,128)(2,1)S(1)} %get-tuple-element.110.after, f32[16,32,512]{2,1,0:T(8,128)S(1)} %get-tuple-element.95.bias_ref, s32[32,512]{1,0:T(8,128)S(1)} %get-tuple-element.96.mask_ref), custom_call_target="tpu_custom_call" | custom-call | flops 1000000000 | bytes 1048576 | tf_op jit(solution)/shard_map/pallas_call | solution.py:63
  21.4 2.8 %collective-permute-done.5 = bf16[64,768]{1,0:T(8,128)(2,1)S(1)} collective-permute-done((bf16[64,768]{1,0:T(8,128)(2,1)S(1)}, bf16[64,768]{1,0:T(8,128)(2,1)S(1)}, u32[]{:S(2)}, u32[]{:S(2)}) %collective-permute-start.5) | collective-permute-done | bytes 98336 | tf_op jit(solution)/shard_map/ppermute | solution.py:475
  24.4 1.1 %shard_map.201.rest_0_ = f32[3,32,768]{2,1,0:T(8,128)S(1)} custom-call(bf16[512,768]{1,0:T(8,128)(2,1)S(1)} %get-tuple-element.92.query_ref, bf16[128,768]{1,0:T(8,128)(2,1)S(1)} %constant_dynamic-update-slice_fusion.2.keys_ref, f32[4,512,128]{2,1,0:T(8,128)S(1)} %shard_map.200.bias_ref, bf16[768,2304]{1,0:T(8,128)(2,1)S(1)} %copy-done), custom_call_target="tpu_custom_call" | custom-call | flops 1000000000 | bytes 294912 | tf_op jit(solution)/shard_map/pallas_call | solution.py:63
  25.6 0.2 collective-permute-done.7.keys_ref
  25.8 1.1 %shard_map.202.rest_1_ = f32[3,32,768]{2,1,0:T(8,128)S(1)} custom-call(bf16[512,768]{1,0:T(8,128)(2,1)S(1)} %get-tuple-element.92.query_ref, bf16[128,768]{1,0:T(8,128)(2,1)S(1)} %collective-permute-done.7.keys_ref, f32[4,512,128]{2,1,0:T(8,128)S(1)} %shard_map.200.bias_ref, bf16[768,2304]{1,0:T(8,128)(2,1)S(1)} %copy-done), custom_call_target="tpu_custom_call" | custom-call | flops 1000000000 | bytes 294912 | tf_op jit(solution)/shard_map/pallas_call | solution.py:63
  26.9 2.6 %collective-permute-done.6.keys_ref = bf16[128,768]{1,0:T(8,128)(2,1)S(1)} collective-permute-done((bf16[128,768]{1,0:T(8,128)(2,1)S(1)}, bf16[128,768]{1,0:T(8,128)(2,1)S(1)}, u32[]{:S(2)}, u32[]{:S(2)}) %collective-permute-start.6) | collective-permute-done | bytes 196640 | tf_op jit(solution)/shard_map/ppermute | solution.py:475
  29.5 0.4 %collective-permute-start.8 = (bf16[128,768]{1,0:T(8,128)(2,1)S(1)}, bf16[128,768]{1,0:T(8,128)(2,1)S(1)}, u32[]{:S(2)}, u32[]{:S(2)}) collective-permute-start(bf16[128,768]{1,0:T(8,128)(2,1)S(1)} %collective-permute-done.6.keys_ref), channel_id=1, source_target_pairs={{0,1},{1,0},{2,3},{3,2},{4,5},{5,4},{6,7},{7,6},{8,9},{9,8},{10,11... | collective-permute-start | bytes 589832 | tf_op jit(solution)/shard_map/ppermute | solution.py:475
  29.9 1.1 %shard_map.203.rest_2_ = f32[3,32,768]{2,1,0:T(8,128)S(1)} custom-call(bf16[512,768]{1,0:T(8,128)(2,1)S(1)} %get-tuple-element.92.query_ref, bf16[128,768]{1,0:T(8,128)(2,1)S(1)} %collective-permute-done.6.keys_ref, f32[4,512,128]{2,1,0:T(8,128)S(1)} %shard_map.200.bias_ref, bf16[768,2304]{1,0:T(8,128)(2,1)S(1)} %copy-done), custom_call_target="tpu_custom_call" | custom-call | flops 1000000000 | bytes 294912 | tf_op jit(solution)/shard_map/pallas_call | solution.py:63
  31.1 1.3 %shard_map.204 = (bf16[32,768]{1,0:T(8,128)(2,1)S(1)}, bf16[32,128]{1,0:T(8,128)(2,1)S(1)}, bf16[16,128]{1,0:T(8,128)(2,1)S(1)}, bf16[16,128]{1,0:T(8,128)(2,1)S(1)}) custom-call(f32[32,128]{1,0:T(8,128)S(1)} %get-tuple-element.91.base_ref, bf16[512,768]{1,0:T(8,128)(2,1)S(1)} %get-tuple-element.92.query_ref, f32[32,768]{1,0:T(8,128)S(1)} %get-tuple-element.93.gate_ref, ...), custom_call_target="tpu_custom_call" | custom-call | flops 10000000 | bytes 65536 | tf_op jit(solution)/shard_map/pallas_call | solution.py:63
  32.4 0.4 collective-permute-start.9
  32.8 1.0 %shard_map.205 = bf16[32,768]{1,0:T(8,128)(2,1)} custom-call(f32[32,768]{1,0:T(8,128)S(1)} %get-tuple-element.83.in_ref, bf16[32,768]{1,0:T(8,128)(2,1)S(1)} %get-tuple-element.106.gated_ref, bf16[768,768]{1,0:T(8,128)(2,1)S(1)} %get-tuple-element.107.wout_ref), custom_call_target="tpu_custom_call" | custom-call | flops 1000000000 | bytes 49152 | tf_op jit(solution)/shard_map/pallas_call | solution.py:63
  33.8 2.6 %collective-permute-done.10.odd_ref = bf16[16,128]{1,0:T(8,128)(2,1)S(1)} collective-permute-done((bf16[16,128]{1,0:T(8,128)(2,1)S(1)}, bf16[16,128]{1,0:T(8,128)(2,1)S(1)}, u32[]{:S(2)}, u32[]{:S(2)}) %collective-permute-start.10) | collective-permute-done | bytes 4128 | tf_op jit(solution)/shard_map/ppermute | solution.py:451
  36.4 1.1 %shard_map.206 = f32[3,384]{1,0:T(4,128)} custom-call(f32[1,384]{1,0:T(1,128)S(1)} %get-tuple-element.71.living_ref, bf16[384,64]{1,0:T(8,128)(2,1)S(1)} %get-tuple-element.72.hot_ref, f32[384,128]{1,0:T(8,128)S(1)} %get-tuple-element.73.mid_ref, bf16[32,128]{1,0:T(8,128)(2,1)S(1)} %get-tuple-element.103.back_ref, ...), custom_call_target="tpu_custom_call" | custom-call | flops 10000000 | bytes 4608 | tf_op jit(solution)/shard_map/pallas_call | solution.py:63
  (24 shorter events, 0.5 us)
Async XLA Ops:
  3.4 3.1 %collective-permute-start = (bf16[96,128]{1,0:T(8,128)(2,1)S(1)}, bf16[96,128]{1,0:T(8,128)(2,1)S(1)}, u32[]{:S(2)}, u32[]{:S(2)}) collective-permute-start(bf16[96,128]{1,0:T(8,128)(2,1)S(1)} %get-tuple-element.66), channel_id=1, source_target_pairs={{0,1},{1,0},{2,3},{3,2},{4,5},{5,4},{6,7},{7,6},{8,9},{9,8},{10,11... | collective-permute-start | bytes 73736 | tf_op jit(solution)/shard_map/ppermute | solution.py:452
  3.5 4.2 %collective-permute-start.1 = (bf16[96,128]{1,0:T(8,128)(2,1)S(1)}, bf16[96,128]{1,0:T(8,128)(2,1)S(1)}, u32[]{:S(2)}, u32[]{:S(2)}) collective-permute-start(bf16[96,128]{1,0:T(8,128)(2,1)S(1)} %get-tuple-element.67), channel_id=1, source_target_pairs={{1,2},{3,4},{5,6},{7,8},{9,10},{11,12},{13,14},{2,1},{4,3},{6,5},{... | collective-permute-start | bytes 73736 | tf_op jit(solution)/shard_map/ppermute | solution.py:451
  9.6 4.3 %collective-permute-start.3 = (bf16[16,896]{1,0:T(8,128)(2,1)S(1)}, bf16[16,896]{1,0:T(8,128)(2,1)S(1)}, u32[]{:S(2)}, u32[]{:S(2)}) collective-permute-start(bf16[16,896]{1,0:T(8,128)(2,1)S(1)} %get-tuple-element.76), channel_id=1, source_target_pairs={{1,2},{3,4},{5,6},{7,8},{9,10},{11,12},{13,14},{2,1},{4,3},{6,5},{... | collective-permute-start | bytes 86024 | tf_op jit(solution)/shard_map/ppermute | solution.py:451
  11.1 2.8 %collective-permute-start.2 = (bf16[16,896]{1,0:T(8,128)(2,1)S(1)}, bf16[16,896]{1,0:T(8,128)(2,1)S(1)}, u32[]{:S(2)}, u32[]{:S(2)}) collective-permute-start(bf16[16,896]{1,0:T(8,128)(2,1)S(1)} %get-tuple-element.75), channel_id=1, source_target_pairs={{0,1},{1,0},{2,3},{3,2},{4,5},{5,4},{6,7},{7,6},{8,9},{9,8},{10,11... | collective-permute-start | bytes 86024 | tf_op jit(solution)/shard_map/ppermute | solution.py:452
  11.1 2.8 %copy-start.1 = (bf16[32,768]{1,0:T(8,128)(2,1)S(1)}, bf16[32,768]{1,0:T(8,128)(2,1)}, u32[]{:S(2)}) copy-start(bf16[32,768]{1,0:T(8,128)(2,1)} %single_ref.1) | copy-start | bytes 147460
  11.1 3.2 %copy-start = (bf16[768,2304]{1,0:T(8,128)(2,1)S(1)}, bf16[768,2304]{1,0:T(8,128)(2,1)}, u32[]{:S(2)}) copy-start(bf16[768,2304]{1,0:T(8,128)(2,1)} %wqkv_ref.9) | copy-start | bytes 10616836
  14.2 5.9 %collective-permute-start.4 = (bf16[32,768]{1,0:T(8,128)(2,1)S(1)}, bf16[32,768]{1,0:T(8,128)(2,1)S(1)}, u32[]{:S(2)}, u32[]{:S(2)}) collective-permute-start(bf16[32,768]{1,0:T(8,128)(2,1)S(1)} %get-tuple-element.82.norm_ref), channel_id=1, source_target_pairs={{0,9},{1,8},{2,11},{3,10},{4,13},{5,12},{6,15},{7,14},{8,1},{9,0},... | collective-permute-start | bytes 147464 | tf_op jit(solution)/shard_map/ppermute | solution.py:475
  20.1 4.1 %collective-permute-start.5 = (bf16[64,768]{1,0:T(8,128)(2,1)S(1)}, bf16[64,768]{1,0:T(8,128)(2,1)S(1)}, u32[]{:S(2)}, u32[]{:S(2)}) collective-permute-start(bf16[64,768]{1,0:T(8,128)(2,1)S(1)} %get-tuple-element.110.after), channel_id=1, source_target_pairs={{0,5},{1,2},{2,1},{3,6},{4,7},{5,0},{6,3},{7,4},{8,13},{9,10},{10,... | collective-permute-start | bytes 294920 | tf_op jit(solution)/shard_map/ppermute | solution.py:475
  24.3 1.5 %collective-permute-start.7 = (bf16[128,768]{1,0:T(8,128)(2,1)S(1)}, bf16[128,768]{1,0:T(8,128)(2,1)S(1)}, u32[]{:S(2)}, u32[]{:S(2)}) collective-permute-start(bf16[128,768]{1,0:T(8,128)(2,1)S(1)} %constant_dynamic-update-slice_fusion.2.keys_ref), channel_id=1, source_target_pairs={{0,1},{1,0},{2,3},{3,2},{4,5},{5,4},{6,7},{7,6},{8,9},{9,8},{10,11... | collective-permute-start | bytes 589832 | tf_op jit(solution)/shard_map/ppermute | solution.py:475
  24.4 5.1 %collective-permute-start.6 = (bf16[128,768]{1,0:T(8,128)(2,1)S(1)}, bf16[128,768]{1,0:T(8,128)(2,1)S(1)}, u32[]{:S(2)}, u32[]{:S(2)}) collective-permute-start(bf16[128,768]{1,0:T(8,128)(2,1)S(1)} %constant_dynamic-update-slice_fusion.2.keys_ref), channel_id=1, source_target_pairs={{0,3},{1,4},{2,7},{3,0},{4,1},{5,6},{6,5},{7,2},{8,11},{9,12},{10,... | collective-permute-start | bytes 589832 | tf_op jit(solution)/shard_map/ppermute | solution.py:475
  29.5 1.5 %collective-permute-start.8 = (bf16[128,768]{1,0:T(8,128)(2,1)S(1)}, bf16[128,768]{1,0:T(8,128)(2,1)S(1)}, u32[]{:S(2)}, u32[]{:S(2)}) collective-permute-start(bf16[128,768]{1,0:T(8,128)(2,1)S(1)} %collective-permute-done.6.keys_ref), channel_id=1, source_target_pairs={{0,1},{1,0},{2,3},{3,2},{4,5},{5,4},{6,7},{7,6},{8,9},{9,8},{10,11... | collective-permute-start | bytes 589832 | tf_op jit(solution)/shard_map/ppermute | solution.py:475
  32.4 4.0 %collective-permute-start.10 = (bf16[16,128]{1,0:T(8,128)(2,1)S(1)}, bf16[16,128]{1,0:T(8,128)(2,1)S(1)}, u32[]{:S(2)}, u32[]{:S(2)}) collective-permute-start(bf16[16,128]{1,0:T(8,128)(2,1)S(1)} %get-tuple-element.105), channel_id=1, source_target_pairs={{1,2},{3,4},{5,6},{7,8},{9,10},{11,12},{13,14},{2,1},{4,3},{6,5},{... | collective-permute-start | bytes 12296 | tf_op jit(solution)/shard_map/ppermute | solution.py:451
  32.4 3.9 %collective-permute-start.9 = (bf16[16,128]{1,0:T(8,128)(2,1)S(1)}, bf16[16,128]{1,0:T(8,128)(2,1)S(1)}, u32[]{:S(2)}, u32[]{:S(2)}) collective-permute-start(bf16[16,128]{1,0:T(8,128)(2,1)S(1)} %get-tuple-element.104), channel_id=1, source_target_pairs={{0,1},{1,0},{2,3},{3,2},{4,5},{5,4},{6,7},{7,6},{8,9},{9,8},{10,11... | collective-permute-start | bytes 12296 | tf_op jit(solution)/shard_map/ppermute | solution.py:452
  32.8 3.6 %copy-start.2 = (f32[3,384]{1,0:T(4,128)S(1)}, f32[3,384]{1,0:T(4,128)}, u32[]{:S(2)}) copy-start(f32[3,384]{1,0:T(4,128)} %pos_ref.1) | copy-start | bytes 13828
  32.8 3.6 %copy-start.3 = (f32[3,384]{1,0:T(4,128)S(1)}, f32[3,384]{1,0:T(4,128)}, u32[]{:S(2)}) copy-start(f32[3,384]{1,0:T(4,128)} %noise_ref.1) | copy-start | bytes 13828
  32.8 3.6 %copy-start.4 = (bf16[3,128]{1,0:T(4,128)(2,1)S(1)}, bf16[3,128]{1,0:T(4,128)(2,1)}, u32[]{:S(2)}) copy-start(bf16[3,128]{1,0:T(4,128)(2,1)} %wpos_ref.1) | copy-start | bytes 2308

commit v9 on v8

--- a/solution.py
+++ b/solution.py
@@ -129,12 +129,15 @@
     for copy in copies[:3]:
         copy.wait()
     scaled = input_scale * (pos_ref[...] + noise_level * noise_ref[...])
-    padded = jnp.concatenate([scaled, jnp.zeros((5, rows), F32)], axis=0)
-    across = jnp.transpose(padded)
+    moved = lax.dot_general(
+        jnp.concatenate([scaled, jnp.zeros((5, rows), F32)], axis=0),
+        jnp.concatenate([wc_ref[...], jnp.zeros((5, width), F32)], axis=0),
+        (((0,), (0,)), ((), ())),
+        precision=lax.Precision.HIGHEST,
+        preferred_element_type=F32,
+    )
     copies[3].wait()
-    start = single_ref[...].astype(F32)
-    for c in range(3):
-        start = start + across[:, c : c + 1] * wc_ref[c : c + 1, :]
+    start = single_ref[...].astype(F32) + moved
     start_ref[...] = start
     normed = normalize(start)
     normed_ref[...] = normed.astype(BF16)
@@ -177,7 +180,22 @@
     return outs
 
 
-def local_body(offsets, normed_ref, wqkv_ref, bias_ref, q_ref, k_ref, v_ref, att_ref):
+def local_body(
+    offsets,
+    normed_ref,
+    wqkv_ref,
+    bias_ref,
+    token_bias_hbm,
+    mask_hbm,
+    q_ref,
+    k_ref,
+    v_ref,
+    att_ref,
+    token_bias_ref,
+    mask_ref,
+    sems,
+):
+    copies = fetch(sems, (mask_hbm, mask_ref), *quarters(token_bias_hbm, token_bias_ref))
     rows, width = normed_ref.shape
     qkv = dot(normed_ref[...], wqkv_ref[...]).astype(BF16)
     q_ref[...] = qkv[:, :width]
@@ -200,6 +218,8 @@
     )
     for a, out in zip(at, outs):
         att_ref[a, :] = out
+    for copy in copies:
+        copy.wait()
 
 
 def atoms_body(
@@ -218,16 +238,22 @@
     wout_ref,
     wagg_ref,
     wqkv_ref,
+    wgate_hbm,
+    wback_hbm,
     mid_ref,
     own_ref,
     pair_out,
     odd_out,
     hot_ref,
     living_ref,
+    wgate_ref,
+    wback_ref,
     k_ext,
     v_ext,
     att,
+    sems,
 ):
+    copies = fetch(sems, (wback_hbm, wback_ref), *quarters(wgate_hbm, wgate_ref))
     rows, width = start_ref.shape
     live, me, last = info[0], info[1], info[2]
     even = me % 2 == 0
@@ -278,6 +304,8 @@
     upper = jnp.concatenate([sums[half + block_rows :], packed[half + block_rows :]], axis=1)
     pair_out[...] = jnp.where(even, upper, lower).astype(BF16)
     odd_out[...] = jnp.where(even, lower, upper).astype(BF16)
+    for copy in copies:
+        copy.wait()
 
 
 def token_body(own_ref, pair_ref, odd_ref, single_ref, in_ref, norm_ref):
@@ -295,13 +323,10 @@
     norm_ref[...] = normalize(token_in).astype(BF16)
 
 
-def weights_body(after, wgate_hbm, wout_hbm, wback_hbm, wgate_ref, wout_ref, wback_ref, both_ref, sems):
-    copies = fetch(sems, (wback_hbm, wback_ref), *quarters(wout_hbm, wout_ref), *quarters(wgate_hbm, wgate_ref))
-    for copy in copies[:5]:
+def weights_body(after, wback_ref, wout_hbm, wout_ref, both_ref, sems):
+    for copy in fetch(sems, *quarters(wout_hbm, wout_ref)):
         copy.wait()
     both_ref[...] = dot(wout_ref[...], wback_ref[...]).astype(BF16)
-    for copy in copies[5:]:
-        copy.wait()
 
 
 def query_body(
@@ -310,16 +335,10 @@
     wqkv_ref,
     wgate_ref,
     wback_ref,
-    bias_hbm,
-    mask_hbm,
     query_ref,
     gate_ref,
     back_ref,
-    bias_ref,
-    mask_ref,
-    sems,
 ):
-    copies = fetch(sems, (mask_hbm, mask_ref), *quarters(bias_hbm, bias_ref))
     rows, model = norm_ref.shape
     width = model // TH
     group = TH // 2
@@ -334,8 +353,6 @@
         query_ref[g * group * rows : (g + 1) * group * rows, :] = dot_nt(stacked, wk).astype(BF16)
     gate_ref[...] = jax.nn.sigmoid(dot(norm, wgate_ref[...]))
     back_ref[...] = dot(in_ref[...].astype(BF16), wback_ref[...])
-    for copy in copies:
-        copy.wait()
 
 
 def stage_body(lists, after, bias_ref, mask_ref, out_ref):
@@ -542,19 +559,22 @@
         w_agg,
     )
     pair, odd = exchange(pair, odd, groups, count)
-    q, keys, values, att = call(
+    q, keys, values, att, raw, mask = call(
         local_body,
         [
             shape((rows, width), BF16),
             shape((rows + AHEAD, width), F32),
             shape((rows + AHEAD, width), F32),
             shape((rows, width), BF16),
+            shape(token_bias.shape, F32),
+            shape(pair_mask.shape, jnp.int32),
         ],
-        [SMEM] + [VMEM] * 3,
+        [SMEM] + [VMEM] * 3 + [HBM] * 2,
+        [pltpu.SemaphoreType.DMA((5,))],
         flops=10**9,
-    )(offsets, normed, wqkv, bias)
+    )(offsets, normed, wqkv, bias, token_bias, pair_mask)
     packed = model + 128
-    mid, own, pair, odd, hot, living = call(
+    mid, own, pair, odd, hot, living, wgate, wback = call(
         functools.partial(atoms_body, half),
         [
             shape((rows, width), F32),
@@ -563,24 +583,22 @@
             shape((half, packed), BF16),
             shape((rows, block_rows + 2 * half), BF16),
             shape((1, rows), F32),
-        ],
-        [SMEM, SMEM] + [VMEM] * 12,
-        [pltpu.VMEM((BEHIND + rows + AHEAD, width), F32)] * 2 + [pltpu.VMEM((rows, width), BF16)],
-    )(info, offsets, tokens, start, q, keys, values, pair, odd, att, bias, wout, wagg, wqkv)
-    pair, odd = exchange(pair, odd, groups, count)
-    wgate, wout, wback, both = call(
-        weights_body,
-        [
             shape(w_tok_gate.shape, BF16),
-            shape(w_tok_out.shape, BF16),
-            shape(w_back.shape, BF16),
             shape(w_back.shape, BF16),
         ],
-        [VMEM] + [HBM] * 3,
-        [pltpu.SemaphoreType.DMA((9,))],
+        [SMEM, SMEM] + [VMEM] * 12 + [HBM] * 2,
+        [pltpu.VMEM((BEHIND + rows + AHEAD, width), F32)] * 2
+        + [pltpu.VMEM((rows, width), BF16), pltpu.SemaphoreType.DMA((5,))],
+    )(info, offsets, tokens, start, q, keys, values, pair, odd, att, bias, wout, wagg, wqkv, w_tok_gate, w_back)
+    pair, odd = exchange(pair, odd, groups, count)
+    wout, both = call(
+        weights_body,
+        [shape(w_tok_out.shape, BF16), shape(w_back.shape, BF16)],
+        [VMEM, VMEM, HBM],
+        [pltpu.SemaphoreType.DMA((4,))],
         flops=10**9,
-    )(own, w_tok_gate, w_tok_out, w_back)
-    odd, wgate, wout, wback, both = lax.optimization_barrier((odd, wgate, wout, wback, both))
+    )(own, wback, w_tok_out)
+    odd, wout, both = lax.optimization_barrier((odd, wout, both))
     token_in, norm = call(
         token_body, [shape((block_rows, model), F32), shape((block_rows, model), BF16)], [VMEM] * 4
     )(own, pair, odd, token_single)
@@ -597,13 +615,10 @@
                 shape((TH * block_rows, model), BF16),
                 shape((block_rows, model), F32),
                 shape((block_rows, width), F32),
-                shape(token_bias.shape, F32),
-                shape(pair_mask.shape, jnp.int32),
             ],
-            [VMEM] * 5 + [HBM] * 2,
-            [pltpu.SemaphoreType.DMA((5,))],
+            [VMEM] * 5,
             flops=10**9,
-        )(seen, token_in, w_tok_qkv, wgate, wback, token_bias, pair_mask)
+        )(seen, token_in, w_tok_qkv, wgate, wback)
 
     def stage(seen, bias, mask):
         return call(
@@ -626,7 +641,7 @@
         for n, step in enumerate(steps[:-1]):
             arrived = swap(held, count, step)
             if n == 0:
-                arrived, (query_rows, gate, base, raw, mask) = lax.optimization_barrier((arrived, query(norm)))
+                arrived, (query_rows, gate, base) = lax.optimization_barrier((arrived, query(norm)))
             if n == 1:
                 arrived, score_bias = lax.optimization_barrier((arrived, stage(held, raw, mask)))
             held = jnp.concatenate([held, arrived], axis=0)
@@ -638,7 +653,7 @@
         parts = parts + [part(2, last)]
     else:
         end = lax.all_gather(norm, "row", axis=0, tiled=True)
-        query_rows, gate, base, raw, mask = query(norm)
+        query_rows, gate, base = query(norm)
         score_bias = stage(norm, raw, mask)
         parts = []
     gated, back, pair, odd = call(

time: 37.7 us -> 39.1 us (1.037)
  Pallas kernels: 17.8 us -> 18.6 us
  waiting for transfers between devices: 14 us -> 14.6 us
    ppermute x5, waiting for transfers between devices: 9.44 us -> 10.5 us  [swap(): lax.ppermute(value, 'row', [(i, i ^ step[kind_of(i)]) for i in range(coun...]
    pallas_call x13, Pallas kernels: 17.8 us -> 18.6 us  [call(): run(*[pltpu.with_memory_space_constraint(x, pltpu.HBM) if h and x.size >...]
    ppermute x3, waiting for transfers between devices: 4.5 us -> 4.06 us  [exchange(): odd = lax.ppermute(odd, ('grp', 'row'), far)]
  transfers between devices with their start and end apart: 11 -> 11, of which waited for: 7 -> 7; matrix products, arithmetic and copies ran while one was open for 0% -> 0% of each run, Pallas kernels for 30% -> 28%
where the time goes in v9:
time: 39.1 us; the launch traced here: 38.9 us
  Pallas kernels  18.6 us (48%)
  waiting for transfers between devices  14.6 us (37%)
  starting transfers between devices  4.22 us (11%)
  between operations  1.43 us (4%)
    pallas_call x13, Pallas kernels, call(): run(*[pltpu.with_memory_space_constraint(x, pltpu.HBM) if h and x.size >...  18.6 us
    ppermute x5, waiting for transfers between devices, swap(): lax.ppermute(value, 'row', [(i, i ^ step[kind_of(i)]) for i in range(coun...  10.5 us
    ppermute x3, waiting for transfers between devices, exchange(): odd = lax.ppermute(odd, ('grp', 'row'), far)  4.06 us
    ppermute x3, starting transfers between devices, exchange(): odd = lax.ppermute(odd, ('grp', 'row'), far)  3.02 us
  transfers between devices with their start and end apart: 11, of which 7 were waited for; matrix products, arithmetic and copies ran while one was open for 0% of the time, Pallas kernels for 28%

profile of v9, /device:TPU:24, one launch (start us, length us, event | category | flops | bytes accessed | tf_op | source)
XLA Modules:
  0.0 38.9 jit_solution(5693522377139681480)
XLA Ops:
  1.3 2.1 %shard_map.194 = (s32[8]{0:T(128)S(1)}, f32[384,128]{1,0:T(8,128)S(1)}, bf16[384,128]{1,0:T(8,128)(2,1)S(1)}, bf16[96,128]{1,0:T(8,128)(2,1)S(1)}, bf16[96,128]{...) custom-call(s32[1,1]{1,0:T(1,128)} %bitcast.2.counts_hbm, ...), custom_call_target="tpu_custom_call" | custom-call | flops 10000000 | bytes 1459792 | tf_op jit(solution)/shard_map/pallas_call | solution.py:63
  3.5 1.5 %collective-permute-start.1 = (bf16[96,128]{1,0:T(8,128)(2,1)S(1)}, bf16[96,128]{1,0:T(8,128)(2,1)S(1)}, u32[]{:S(2)}, u32[]{:S(2)}) collective-permute-start(bf16[96,128]{1,0:T(8,128)(2,1)S(1)} %get-tuple-element.63), channel_id=1, source_target_pairs={{1,2},{3,4},{5,6},{7,8},{9,10},{11,12},{13,14},{2,1},{4,3},{6,5},{... | collective-permute-start | bytes 73736 | tf_op jit(solution)/shard_map/ppermute | solution.py:468
  5.0 2.5 %shard_map.195 = (bf16[384,128]{1,0:T(8,128)(2,1)S(1)}, f32[480,128]{1,0:T(8,128)S(1)}, f32[480,128]{1,0:T(8,128)S(1)}, bf16[384,128]{1,0:T(8,128)(2,1)S(1)}, f3...) custom-call(s32[1,12]{1,0:T(1,128)S(1)} %get-tuple-element.53.offsets, ...), custom_call_target="tpu_custom_call" | custom-call | flops 1000000000 | bytes 1802240 | tf_op jit(solution)/shard_map/pallas_call | solution.py:63
  7.5 0.2 collective-permute-done.1.odd_ref
  7.7 2.8 %shard_map.196 = (f32[384,128]{1,0:T(8,128)S(1)}, f32[32,896]{1,0:T(8,128)S(1)}, bf16[16,896]{1,0:T(8,128)(2,1)S(1)}, bf16[16,896]{1,0:T(8,128)(2,1)S(1)}, bf16[...) custom-call(s32[8]{0:T(128)S(1)} %get-tuple-element.52.info, ...), custom_call_target="tpu_custom_call" | custom-call | flops 10000000 | bytes 1795584 | tf_op jit(solution)/shard_map/pallas_call | solution.py:63
  10.6 1.5 %collective-permute-start.3 = (bf16[16,896]{1,0:T(8,128)(2,1)S(1)}, bf16[16,896]{1,0:T(8,128)(2,1)S(1)}, u32[]{:S(2)}, u32[]{:S(2)}) collective-permute-start(bf16[16,896]{1,0:T(8,128)(2,1)S(1)} %get-tuple-element.72), channel_id=1, source_target_pairs={{1,2},{3,4},{5,6},{7,8},{9,10},{11,12},{13,14},{2,1},{4,3},{6,5},{... | collective-permute-start | bytes 86024 | tf_op jit(solution)/shard_map/ppermute | solution.py:468
  12.1 1.9 %shard_map.197 = (bf16[768,768]{1,0:T(8,128)(2,1)S(1)}, bf16[768,128]{1,0:T(8,128)(2,1)S(1)}) custom-call(f32[32,896]{1,0:T(8,128)S(1)} %get-tuple-element.70.after.own_ref, bf16[768,128]{1,0:T(8,128)(2,1)S(1)} %get-tuple-element.73.wback_ref, bf16[768,768]{1,0:T(8,128)(2,1)} %wout_hbm.3), custom_call_target="tpu_custom_call" | custom-call | flops 1000000000 | bytes 1376256 | tf_op jit(solution)/shard_map/pallas_call | solution.py:63
  14.0 0.9 %collective-permute-done.3.odd_ref = bf16[16,896]{1,0:T(8,128)(2,1)S(1)} collective-permute-done((bf16[16,896]{1,0:T(8,128)(2,1)S(1)}, bf16[16,896]{1,0:T(8,128)(2,1)S(1)}, u32[]{:S(2)}, u32[]{:S(2)}) %collective-permute-start.3) | collective-permute-done | bytes 28704 | tf_op jit(solution)/shard_map/ppermute | solution.py:468
  14.9 0.3 shard_map.198
  15.4 1.0 %shard_map.199 = (bf16[512,768]{1,0:T(8,128)(2,1)S(1)}, f32[32,768]{1,0:T(8,128)S(1)}, f32[32,128]{1,0:T(8,128)S(1)}) custom-call(bf16[32,768]{1,0:T(8,128)(2,1)S(1)} %get-tuple-element.77.norm_ref, f32[32,768]{1,0:T(8,128)S(1)} %get-tuple-element.78.in_ref, bf16[768,2304]{1,0:T(8,128)(2,1)S(1)} %copy-done, ...), custom_call_target="tpu_custom_call" | custom-call | flops 1000000000 | bytes 901120 | tf_op jit(solution)/shard_map/pallas_call | solution.py:63
  16.4 4.9 %collective-permute-done.4 = bf16[32,768]{1,0:T(8,128)(2,1)S(1)} collective-permute-done((bf16[32,768]{1,0:T(8,128)(2,1)S(1)}, bf16[32,768]{1,0:T(8,128)(2,1)S(1)}, u32[]{:S(2)}, u32[]{:S(2)}) %collective-permute-start.4) | collective-permute-done | bytes 49184 | tf_op jit(solution)/shard_map/ppermute | solution.py:492
  21.3 1.2 %shard_map.200.bias_ref = f32[4,512,128]{2,1,0:T(8,128)S(1)} custom-call(bf16[64,768]{1,0:T(8,128)(2,1)S(1)} %get-tuple-element.102.after, f32[16,32,512]{2,1,0:T(8,128)S(1)} %get-tuple-element.87.bias_ref, s32[32,512]{1,0:T(8,128)S(1)} %get-tuple-element.88.mask_ref), custom_call_target="tpu_custom_call" | custom-call | flops 1000000000 | bytes 1048576 | tf_op jit(solution)/shard_map/pallas_call | solution.py:63
  22.5 2.8 %collective-permute-done.5 = bf16[64,768]{1,0:T(8,128)(2,1)S(1)} collective-permute-done((bf16[64,768]{1,0:T(8,128)(2,1)S(1)}, bf16[64,768]{1,0:T(8,128)(2,1)S(1)}, u32[]{:S(2)}, u32[]{:S(2)}) %collective-permute-start.5) | collective-permute-done | bytes 98336 | tf_op jit(solution)/shard_map/ppermute | solution.py:492
  25.5 1.1 %shard_map.201.rest_0_ = f32[3,32,768]{2,1,0:T(8,128)S(1)} custom-call(bf16[512,768]{1,0:T(8,128)(2,1)S(1)} %get-tuple-element.84.query_ref, bf16[128,768]{1,0:T(8,128)(2,1)S(1)} %constant_dynamic-update-slice_fusion.2.keys_ref, f32[4,512,128]{2,1,0:T(8,128)S(1)} %shard_map.200.bias_ref, bf16[768,2304]{1,0:T(8,128)(2,1)S(1)} %copy-done), custom_call_target="tpu_custom_call" | custom-call | flops 1000000000 | bytes 294912 | tf_op jit(solution)/shard_map/pallas_call | solution.py:63
  26.7 0.2 collective-permute-done.7.keys_ref
  26.8 1.1 %shard_map.202.rest_1_ = f32[3,32,768]{2,1,0:T(8,128)S(1)} custom-call(bf16[512,768]{1,0:T(8,128)(2,1)S(1)} %get-tuple-element.84.query_ref, bf16[128,768]{1,0:T(8,128)(2,1)S(1)} %collective-permute-done.7.keys_ref, f32[4,512,128]{2,1,0:T(8,128)S(1)} %shard_map.200.bias_ref, bf16[768,2304]{1,0:T(8,128)(2,1)S(1)} %copy-done), custom_call_target="tpu_custom_call" | custom-call | flops 1000000000 | bytes 294912 | tf_op jit(solution)/shard_map/pallas_call | solution.py:63
  28.0 2.6 %collective-permute-done.6.keys_ref = bf16[128,768]{1,0:T(8,128)(2,1)S(1)} collective-permute-done((bf16[128,768]{1,0:T(8,128)(2,1)S(1)}, bf16[128,768]{1,0:T(8,128)(2,1)S(1)}, u32[]{:S(2)}, u32[]{:S(2)}) %collective-permute-start.6) | collective-permute-done | bytes 196640 | tf_op jit(solution)/shard_map/ppermute | solution.py:492
  30.6 0.4 %collective-permute-start.8 = (bf16[128,768]{1,0:T(8,128)(2,1)S(1)}, bf16[128,768]{1,0:T(8,128)(2,1)S(1)}, u32[]{:S(2)}, u32[]{:S(2)}) collective-permute-start(bf16[128,768]{1,0:T(8,128)(2,1)S(1)} %collective-permute-done.6.keys_ref), channel_id=1, source_target_pairs={{0,1},{1,0},{2,3},{3,2},{4,5},{5,4},{6,7},{7,6},{8,9},{9,8},{10,11... | collective-permute-start | bytes 589832 | tf_op jit(solution)/shard_map/ppermute | solution.py:492
  31.0 1.1 %shard_map.203.rest_2_ = f32[3,32,768]{2,1,0:T(8,128)S(1)} custom-call(bf16[512,768]{1,0:T(8,128)(2,1)S(1)} %get-tuple-element.84.query_ref, bf16[128,768]{1,0:T(8,128)(2,1)S(1)} %collective-permute-done.6.keys_ref, f32[4,512,128]{2,1,0:T(8,128)S(1)} %shard_map.200.bias_ref, bf16[768,2304]{1,0:T(8,128)(2,1)S(1)} %copy-done), custom_call_target="tpu_custom_call" | custom-call | flops 1000000000 | bytes 294912 | tf_op jit(solution)/shard_map/pallas_call | solution.py:63
  32.2 1.3 %shard_map.204 = (bf16[32,768]{1,0:T(8,128)(2,1)S(1)}, bf16[32,128]{1,0:T(8,128)(2,1)S(1)}, bf16[16,128]{1,0:T(8,128)(2,1)S(1)}, bf16[16,128]{1,0:T(8,128)(2,1)S(1)}) custom-call(f32[32,128]{1,0:T(8,128)S(1)} %get-tuple-element.83.base_ref, bf16[512,768]{1,0:T(8,128)(2,1)S(1)} %get-tuple-element.84.query_ref, f32[32,768]{1,0:T(8,128)S(1)} %get-tuple-element.85.gate_ref, ...), custom_call_target="tpu_custom_call" | custom-call | flops 10000000 | bytes 65536 | tf_op jit(solution)/shard_map/pallas_call | solution.py:63
  33.5 0.3 collective-permute-start.9
  33.8 1.0 %shard_map.205 = bf16[32,768]{1,0:T(8,128)(2,1)} custom-call(f32[32,768]{1,0:T(8,128)S(1)} %get-tuple-element.78.in_ref, bf16[32,768]{1,0:T(8,128)(2,1)S(1)} %get-tuple-element.98.gated_ref, bf16[768,768]{1,0:T(8,128)(2,1)S(1)} %get-tuple-element.99.wout_ref), custom_call_target="tpu_custom_call" | custom-call | flops 1000000000 | bytes 49152 | tf_op jit(solution)/shard_map/pallas_call | solution.py:63
  34.8 3.0 %collective-permute-done.10.odd_ref = bf16[16,128]{1,0:T(8,128)(2,1)S(1)} collective-permute-done((bf16[16,128]{1,0:T(8,128)(2,1)S(1)}, bf16[16,128]{1,0:T(8,128)(2,1)S(1)}, u32[]{:S(2)}, u32[]{:S(2)}) %collective-permute-start.10) | collective-permute-done | bytes 4128 | tf_op jit(solution)/shard_map/ppermute | solution.py:468
  37.8 1.1 %shard_map.206 = f32[3,384]{1,0:T(4,128)} custom-call(f32[1,384]{1,0:T(1,128)S(1)} %get-tuple-element.67.living_ref, bf16[384,64]{1,0:T(8,128)(2,1)S(1)} %get-tuple-element.68.hot_ref, f32[384,128]{1,0:T(8,128)S(1)} %get-tuple-element.69.mid_ref, bf16[32,128]{1,0:T(8,128)(2,1)S(1)} %get-tuple-element.95.back_ref, ...), custom_call_target="tpu_custom_call" | custom-call | flops 10000000 | bytes 4608 | tf_op jit(solution)/shard_map/pallas_call | solution.py:63
  (24 shorter events, 0.5 us)
Async XLA Ops:
  3.4 4.1 %collective-permute-start = (bf16[96,128]{1,0:T(8,128)(2,1)S(1)}, bf16[96,128]{1,0:T(8,128)(2,1)S(1)}, u32[]{:S(2)}, u32[]{:S(2)}) collective-permute-start(bf16[96,128]{1,0:T(8,128)(2,1)S(1)} %get-tuple-element.62), channel_id=1, source_target_pairs={{0,1},{1,0},{2,3},{3,2},{4,5},{5,4},{6,7},{7,6},{8,9},{9,8},{10,11... | collective-permute-start | bytes 73736 | tf_op jit(solution)/shard_map/ppermute | solution.py:469
  3.5 4.2 %collective-permute-start.1 = (bf16[96,128]{1,0:T(8,128)(2,1)S(1)}, bf16[96,128]{1,0:T(8,128)(2,1)S(1)}, u32[]{:S(2)}, u32[]{:S(2)}) collective-permute-start(bf16[96,128]{1,0:T(8,128)(2,1)S(1)} %get-tuple-element.63), channel_id=1, source_target_pairs={{1,2},{3,4},{5,6},{7,8},{9,10},{11,12},{13,14},{2,1},{4,3},{6,5},{... | collective-permute-start | bytes 73736 | tf_op jit(solution)/shard_map/ppermute | solution.py:468
  10.6 4.4 %collective-permute-start.2 = (bf16[16,896]{1,0:T(8,128)(2,1)S(1)}, bf16[16,896]{1,0:T(8,128)(2,1)S(1)}, u32[]{:S(2)}, u32[]{:S(2)}) collective-permute-start(bf16[16,896]{1,0:T(8,128)(2,1)S(1)} %get-tuple-element.71), channel_id=1, source_target_pairs={{0,1},{1,0},{2,3},{3,2},{4,5},{5,4},{6,7},{7,6},{8,9},{9,8},{10,11... | collective-permute-start | bytes 86024 | tf_op jit(solution)/shard_map/ppermute | solution.py:469
  10.6 4.3 %collective-permute-start.3 = (bf16[16,896]{1,0:T(8,128)(2,1)S(1)}, bf16[16,896]{1,0:T(8,128)(2,1)S(1)}, u32[]{:S(2)}, u32[]{:S(2)}) collective-permute-start(bf16[16,896]{1,0:T(8,128)(2,1)S(1)} %get-tuple-element.72), channel_id=1, source_target_pairs={{1,2},{3,4},{5,6},{7,8},{9,10},{11,12},{13,14},{2,1},{4,3},{6,5},{... | collective-permute-start | bytes 86024 | tf_op jit(solution)/shard_map/ppermute | solution.py:468
  12.1 2.8 %copy-start.1 = (bf16[32,768]{1,0:T(8,128)(2,1)S(1)}, bf16[32,768]{1,0:T(8,128)(2,1)}, u32[]{:S(2)}) copy-start(bf16[32,768]{1,0:T(8,128)(2,1)} %single_ref.1) | copy-start | bytes 147460
  12.1 3.2 %copy-start = (bf16[768,2304]{1,0:T(8,128)(2,1)S(1)}, bf16[768,2304]{1,0:T(8,128)(2,1)}, u32[]{:S(2)}) copy-start(bf16[768,2304]{1,0:T(8,128)(2,1)} %wqkv_ref.9) | copy-start | bytes 10616836
  15.3 5.9 %collective-permute-start.4 = (bf16[32,768]{1,0:T(8,128)(2,1)S(1)}, bf16[32,768]{1,0:T(8,128)(2,1)S(1)}, u32[]{:S(2)}, u32[]{:S(2)}) collective-permute-start(bf16[32,768]{1,0:T(8,128)(2,1)S(1)} %get-tuple-element.77.norm_ref), channel_id=1, source_target_pairs={{0,9},{1,8},{2,11},{3,10},{4,13},{5,12},{6,15},{7,14},{8,1},{9,0},... | collective-permute-start | bytes 147464 | tf_op jit(solution)/shard_map/ppermute | solution.py:492
  21.2 4.1 %collective-permute-start.5 = (bf16[64,768]{1,0:T(8,128)(2,1)S(1)}, bf16[64,768]{1,0:T(8,128)(2,1)S(1)}, u32[]{:S(2)}, u32[]{:S(2)}) collective-permute-start(bf16[64,768]{1,0:T(8,128)(2,1)S(1)} %get-tuple-element.102.after), channel_id=1, source_target_pairs={{0,5},{1,2},{2,1},{3,6},{4,7},{5,0},{6,3},{7,4},{8,13},{9,10},{10,... | collective-permute-start | bytes 294920 | tf_op jit(solution)/shard_map/ppermute | solution.py:492
  25.3 1.5 %collective-permute-start.7 = (bf16[128,768]{1,0:T(8,128)(2,1)S(1)}, bf16[128,768]{1,0:T(8,128)(2,1)S(1)}, u32[]{:S(2)}, u32[]{:S(2)}) collective-permute-start(bf16[128,768]{1,0:T(8,128)(2,1)S(1)} %constant_dynamic-update-slice_fusion.2.keys_ref), channel_id=1, source_target_pairs={{0,1},{1,0},{2,3},{3,2},{4,5},{5,4},{6,7},{7,6},{8,9},{9,8},{10,11... | collective-permute-start | bytes 589832 | tf_op jit(solution)/shard_map/ppermute | solution.py:492
  25.5 5.1 %collective-permute-start.6 = (bf16[128,768]{1,0:T(8,128)(2,1)S(1)}, bf16[128,768]{1,0:T(8,128)(2,1)S(1)}, u32[]{:S(2)}, u32[]{:S(2)}) collective-permute-start(bf16[128,768]{1,0:T(8,128)(2,1)S(1)} %constant_dynamic-update-slice_fusion.2.keys_ref), channel_id=1, source_target_pairs={{0,3},{1,4},{2,7},{3,0},{4,1},{5,6},{6,5},{7,2},{8,11},{9,12},{10,... | collective-permute-start | bytes 589832 | tf_op jit(solution)/shard_map/ppermute | solution.py:492
  30.6 1.5 %collective-permute-start.8 = (bf16[128,768]{1,0:T(8,128)(2,1)S(1)}, bf16[128,768]{1,0:T(8,128)(2,1)S(1)}, u32[]{:S(2)}, u32[]{:S(2)}) collective-permute-start(bf16[128,768]{1,0:T(8,128)(2,1)S(1)} %collective-permute-done.6.keys_ref), channel_id=1, source_target_pairs={{0,1},{1,0},{2,3},{3,2},{4,5},{5,4},{6,7},{7,6},{8,9},{9,8},{10,11... | collective-permute-start | bytes 589832 | tf_op jit(solution)/shard_map/ppermute | solution.py:492
  33.5 4.3 %collective-permute-start.9 = (bf16[16,128]{1,0:T(8,128)(2,1)S(1)}, bf16[16,128]{1,0:T(8,128)(2,1)S(1)}, u32[]{:S(2)}, u32[]{:S(2)}) collective-permute-start(bf16[16,128]{1,0:T(8,128)(2,1)S(1)} %get-tuple-element.96), channel_id=1, source_target_pairs={{0,1},{1,0},{2,3},{3,2},{4,5},{5,4},{6,7},{7,6},{8,9},{9,8},{10,11... | collective-permute-start | bytes 12296 | tf_op jit(solution)/shard_map/ppermute | solution.py:469
  33.8 3.9 %collective-permute-start.10 = (bf16[16,128]{1,0:T(8,128)(2,1)S(1)}, bf16[16,128]{1,0:T(8,128)(2,1)S(1)}, u32[]{:S(2)}, u32[]{:S(2)}) collective-permute-start(bf16[16,128]{1,0:T(8,128)(2,1)S(1)} %get-tuple-element.97), channel_id=1, source_target_pairs={{1,2},{3,4},{5,6},{7,8},{9,10},{11,12},{13,14},{2,1},{4,3},{6,5},{... | collective-permute-start | bytes 12296 | tf_op jit(solution)/shard_map/ppermute | solution.py:468
  33.8 3.9 %copy-start.2 = (f32[3,384]{1,0:T(4,128)S(1)}, f32[3,384]{1,0:T(4,128)}, u32[]{:S(2)}) copy-start(f32[3,384]{1,0:T(4,128)} %pos_ref.1) | copy-start | bytes 13828
  33.8 3.9 %copy-start.3 = (f32[3,384]{1,0:T(4,128)S(1)}, f32[3,384]{1,0:T(4,128)}, u32[]{:S(2)}) copy-start(f32[3,384]{1,0:T(4,128)} %noise_ref.1) | copy-start | bytes 13828
  33.8 3.9 %copy-start.4 = (bf16[3,128]{1,0:T(4,128)(2,1)S(1)}, bf16[3,128]{1,0:T(4,128)(2,1)}, u32[]{:S(2)}) copy-start(bf16[3,128]{1,0:T(4,128)(2,1)} %wpos_ref.1) | copy-start | bytes 2308
